TPU v7x, 128 devices: a whole 4x4x4 slice. The times are simulated.
128 devices in a mesh: pb: 64 (over z, y, x), ka: 2 (over core).
Axes of the slice: x: 4, y: 4, z: 4, core: 2. Of those that a mesh axis runs over, the one named last changes fastest.
Arguments:
- query_tokens: bfloat16 [65536, 768], P(('pb', 'ka')), may hold values from -272 to 272
- source_tokens: bfloat16 [3, 16384, 768], P(None, ('pb', 'ka')), may hold values from -6 to 6
- w_query: bfloat16 [768, 768], replicated, may hold values from -0.21875 to 0.21875
- w_keyval: bfloat16 [768, 1536], replicated, may hold values from -0.21875 to 0.21875
- w_out: bfloat16 [768, 768], replicated, may hold values from -0.21875 to 0.21875
- slab_map: int32 [3, 128], replicated, may hold values from 0 to 127, as said below
- neighbours: int32 [512, 2, 6], P(('pb', 'ka')), may hold values from 0 to 383, as said below
- counts: int32 [512, 2], P(('pb', 'ka')), may hold values from 1 to 6, as said below
Outputs:
- output: bfloat16 [65536, 768], P(('pb', 'ka'))
Inputs may be any that keep to these rules, and one draw needn't show every extreme that they name: Each row slab_map[c] is a permutation of the key blocks. neighbours[q, a, j] = c * 128 + b names contrast c and key block b whose stored block s has (s) % 2 == a; a query slab is 8 query blocks in a row; over all entries (live or not) of one query slab and one slab a, the named blocks are distinct and at most 1 of them have the same s // 2, a bound reached in every draw. Only the first counts[q, a] entries of neighbours[q, a] are listed.
All inputs are finite; a program needn't handle non-finite values.
Results may differ from a plain program's by a relative error of at most 0.024.
The roundings to bfloat16 on the way count: a program that leaves them out, or rounds other values in their place, can miss the bound.
Values may be sent and summed in bfloat16 or wider, within the bound.
No kernel may reach another device: no remote copies, remote signals or barrier semaphores. Data moves between devices by JAX's collectives and lax.ppermute only.
A program may use at most 192 MiB of HBM per device.

v0:
```python
import jax
import jax.numpy as jnp
from jax import lax
from jax.experimental import pallas as pl
from jax.experimental.pallas import tpu as pltpu
from jax.sharding import PartitionSpec as P


HEADS = 12
HEAD_DIM = 64
BLK = 128
CAP = 6
WIDTH = HEADS * HEAD_DIM
PARTS = 3
CUT = WIDTH // PARTS
SIDE = 4
PAIRS = HEADS // 2
HALVES = 1
SELECT_VMEM = 8 << 20
ROWS = BLK // HALVES
GROUP = 2 * BLK // ROWS
ITEM = GROUP * ROWS
BF = jnp.bfloat16
F32 = jnp.float32
I32 = jnp.int32
STRIDE = (SIDE * SIDE, SIDE, 1)
ROUTES = ((2, 0, 1), (1, 2, 0), (0, 1, 2))
LOG2E = 1.4426950408889634


SMEM = pl.BlockSpec(memory_space=pltpu.SMEM)
VMEM = pl.BlockSpec(memory_space=pltpu.VMEM)
HBM = pl.BlockSpec(memory_space=pltpu.HBM)


def shift(value, axis, step):
    stride = STRIDE[axis]
    pairs = []
    for source in range(SIDE**3):
        at = source // stride % SIDE
        pairs.append((source, source + ((at + step) % SIDE - at) * stride))
    return lax.ppermute(value, "pb", pairs)


def swap(value):
    return lax.ppermute(value, "ka", [(0, 1), (1, 0)])


def table_kernel(blocks, near_ref, count_ref, map_ref, out_ref):
    def clear(i, _):
        for k in range(8):
            out_ref[0, i * 8 + k] = 0
            out_ref[1, i * 8 + k] = -1
        return 0

    lax.fori_loop(0, 16, clear, 0)
    key_blocks = map_ref.shape[1]
    mine = lax.axis_index("pb")
    for slab in range(2):
        for q in range(blocks):
            live = count_ref[q, slab]
            for j in range(CAP):

                @pl.when(j < live)
                def _():
                    entry = near_ref[q, slab, j]
                    one = (entry >= key_blocks).astype(I32)
                    two = (entry >= 2 * key_blocks).astype(I32)
                    contrast = one + two
                    stored = map_ref[contrast, entry - contrast * key_blocks]
                    owner = lax.shift_right_logical(stored, 1)
                    out_ref[0, slab * 64 + owner] = 1 + contrast
                    away = (mine & 48) + 64 - (owner & 48) & 48
                    away = away | ((mine & 12) + 16 - (owner & 12) & 12)
                    away = away | ((mine & 3) + 4 - (owner & 3) & 3)
                    out_ref[1, (slab * blocks + q) * CAP + j] = away


def walk_slots(part, me_ref, table_ref, gathered, outs):
    across, first, second = ROUTES[part]
    for d2 in range(SIDE):
        for d1 in range(SIDE):
            at = [None, None, None]
            at[across] = me_ref[across]
            at[first] = me_ref[first] + 4 - d1 & 3
            at[second] = me_ref[second] + 4 - d2 & 3
            place = me_ref[3] * 64 + at[0] * 16 + at[1] * 4 + at[2]
            line, row = gathered[d2 * 2 + d1 // 2], d1 % 2
            for d, out in outs:
                which = table_ref[0 if d == 0 else 3 * part + d, place]
                begin = pl.multiple_of(jnp.maximum(which - 1, 0) * BLK, BLK)
                out[d2 * 4 + d1] = line[row, pl.ds(begin, BLK), :]


def select_kernel(part, me_ref, table_ref, *refs):
    walk_slots(part, me_ref, table_ref, refs[:8], list(enumerate(refs[8:], 1)))


def own_kernel(me_ref, table_ref, *refs):
    for part in range(PARTS):
        walk_slots(part, me_ref, table_ref, refs[8 * part : 8 * part + 8], [(0, refs[24 + part])])


def spread_kernel(xq_ref, wq_ref, spread):
    low = lax.broadcasted_iota(I32, (BLK, BLK), 1) < HEAD_DIM
    zero = jnp.zeros((BLK, BLK), BF)
    for q in range(xq_ref.shape[0] // BLK):
        queries = jnp.dot(
            xq_ref[q * BLK : (q + 1) * BLK, :], wq_ref[...], preferred_element_type=F32
        ).astype(BF)
        for p in range(PAIRS):
            two = queries[:, p * BLK : (p + 1) * BLK]
            spread[q, p, :BLK, :] = jnp.where(low, two, zero)
            spread[q, p, BLK:, :] = jnp.where(low, zero, two)


def fetch_parts(code, arrived, target, sem_of):
    away = (lax.shift_right_logical(code, 4), lax.shift_right_logical(code, 2) & 3, code & 3)
    for part, (across, first, second) in enumerate(ROUTES):
        for d in range(SIDE):

            @pl.when(away[across] == d)
            def _():
                pltpu.make_async_copy(
                    arrived[part][d].at[away[second] * 4 + away[first]],
                    target(part),
                    sem_of(part),
                ).start()


def hand_kernel(part, me_ref, code_ref, *refs):
    arrived = refs[:SIDE]
    out, sem = refs[SIDE:]
    count = out.shape[0]
    across, first, second = ROUTES[part]
    shifts = (4, 2, 0)

    def start(i, _):
        code = jnp.maximum(code_ref[1, me_ref[3] * count + i], 0)
        away = [lax.shift_right_logical(code, shifts[axis]) & 3 for axis in range(3)]
        for d in range(SIDE):

            @pl.when(away[across] == d)
            def _():
                pltpu.make_async_copy(
                    arrived[d].at[away[second] * 4 + away[first]], out.at[i], sem
                ).start()

        return 0

    lax.fori_loop(0, count, start, 0)
    pltpu.make_async_copy(out, out, sem).wait()


def attend_kernel(first, last, *refs):
    refs = list(refs)
    me_ref, code_ref, count_ref, spread, wk_ref, wvt_ref, wo_ref = refs[:7]
    arrived = [refs[7 + 4 * part : 11 + 4 * part] for part in range(PARTS)]
    handed = refs[19:22]
    refs = refs[22:]
    if not first:
        before = refs[:3]
        refs = refs[3:]
    if last:
        out_ref = refs.pop(0)
        peak, total, sums = refs[-3:]
    else:
        peak, total, sums = refs[:3]
        refs = refs[3:]
    item_q, item_n, item_code, tokens, keys, values, sems = refs[:7]
    blocks = spread.shape[0]
    mine = me_ref[3]
    span = blocks * CAP

    def plan_block(q, begun):
        own = count_ref[q, mine]
        live = own + count_ref[q, 1 - mine]

        def plan_item(k, _):
            t = begun + k
            item_q[t] = q
            item_n[t] = live - GROUP * k
            for g in range(GROUP):
                i = jnp.where(GROUP * k + g < live, GROUP * k + g, GROUP * k)
                near = code_ref[1, mine * span + q * CAP + jnp.minimum(i, own - 1)]
                item_code[t * GROUP + g] = jnp.where(i < own, near, 64 + q * CAP + i - own)
            return 0

        items = lax.div(live + GROUP - 1, GROUP)
        lax.fori_loop(0, items, plan_item, 0)
        return begun + items

    steps = lax.fori_loop(0, blocks, plan_block, 0)

    def fetch(t):
        slot = t & 1
        for g in range(GROUP):
            code = item_code[t * GROUP + g]
            rows = pl.ds(g * ROWS, ROWS)

            @pl.when(code < 64)
            def _():
                fetch_parts(
                    code,
                    arrived,
                    lambda part: tokens.at[slot, rows, pl.ds(part * CUT, CUT)],
                    lambda part: sems.at[slot],
                )

            @pl.when(code >= 64)
            def _():
                for part in range(PARTS):
                    pltpu.make_async_copy(
                        handed[part].at[jnp.maximum(code - 64, 0)],
                        tokens.at[slot, rows, pl.ds(part * CUT, CUT)],
                        sems.at[slot],
                    ).start()

    def landed(slot):
        pltpu.make_async_copy(tokens.at[slot], tokens.at[slot], sems.at[slot]).wait()

    def project(slot, chunk):
        part = pl.ds(chunk % 3 * CUT, CUT)
        if chunk < 3:
            keys[slot, :, part] = jnp.dot(
                tokens[slot], wk_ref[:, part], preferred_element_type=F32
            ).astype(BF)
        else:
            values[slot, part, :] = lax.dot_general(
                wvt_ref[part, :],
                tokens[slot],
                (((1,), (1,)), ((), ())),
                preferred_element_type=F32,
            ).astype(BF)

    fetch(0)
    fetch(1)
    if first:
        peak[...] = jnp.full_like(peak, -jnp.inf)
        total[...] = jnp.zeros_like(total)
        sums[...] = jnp.zeros_like(sums)
    else:
        for mine_ref, old_ref in zip((peak, total, sums), before):
            mine_ref[...] = old_ref[...]
    landed(0)
    for chunk in range(6):
        project(0, chunk)

    def step(t, _):
        slot = t & 1
        q = item_q[t]
        live = item_n[t]

        @pl.when(t + 2 < steps)
        def _():
            fetch(t + 2)

        for g in range(1, GROUP):

            @pl.when(live <= g)
            def _():
                values[slot, :, pl.ds(g * ROWS, ROWS)] = jnp.zeros((WIDTH, ROWS), BF)

        @pl.when(t + 1 < steps)
        def _():
            landed(1 - slot)

        scale = HEAD_DIM**-0.5 * LOG2E

        def score(p):
            return lax.dot_general(
                keys[slot, :, p * BLK : (p + 1) * BLK],
                spread[q, p],
                (((1,), (1,)), ((), ())),
                preferred_element_type=F32,
            )

        ahead = score(0)
        waiting = None
        for p in range(PAIRS + 1):
            scores = ahead
            if p + 1 < PAIRS:
                ahead = score(p + 1)
            if p % 2 == 0 and p < PAIRS:
                project(1 - slot, p // 2)
                project(1 - slot, 3 + p // 2)
            if waiting is not None:
                weights, factor = waiting
                top = (p - 1) * BLK
                mid = top + HEAD_DIM
                end = top + BLK
                mixed = jnp.dot(values[slot, top:end, :], weights, preferred_element_type=F32)
                sums[q, top:mid, :] = (
                    sums[q, top:mid, :] * factor[:, :BLK] + mixed[:HEAD_DIM, :BLK]
                )
                sums[q, mid:end, :] = (
                    sums[q, mid:end, :] * factor[:, BLK:] + mixed[HEAD_DIM:, BLK:]
                )
            if p < PAIRS:
                old = peak[q, p : p + 1, :]
                new = jnp.maximum(old, jnp.max(scores, axis=0, keepdims=True))
                expo = jnp.exp2((scores - new) * scale)
                factor = jnp.exp2((old - new) * scale)
                peak[q, p : p + 1, :] = new
                add = total[q, p : p + 1, :] * factor
                for g in range(GROUP):
                    some = jnp.sum(expo[g * ROWS : (g + 1) * ROWS], axis=0, keepdims=True)
                    add = add + (some if g == 0 else jnp.where(g < live, some, 0.0))
                total[q, p : p + 1, :] = add
                waiting = (expo.astype(BF), factor)
        return 0

    lax.fori_loop(0, steps, step, 0)
    if last:
        for q in range(blocks):
            done = []
            for p in range(PAIRS):
                for h in range(2):
                    top = p * BLK + h * HEAD_DIM
                    done.append(
                        sums[q, top : top + HEAD_DIM, :]
                        / total[q, p : p + 1, h * BLK : (h + 1) * BLK]
                    )
            attended = jnp.transpose(jnp.concatenate(done, axis=0)).astype(BF)
            out_ref[q * BLK : (q + 1) * BLK, :] = jnp.dot(
                attended, wo_ref[...], preferred_element_type=F32
            ).astype(BF)


def on_device(query_tokens, source_tokens, w_query, w_keyval, w_out, slab_map, neighbours, counts):
    blocks = neighbours.shape[0]
    place = lax.axis_index("pb").astype(I32)
    me = jnp.stack(
        [place // 16, place // 4 % 4, place % 4, lax.axis_index("ka").astype(I32)]
    )
    table = pl.pallas_call(
        lambda *refs: table_kernel(blocks, *refs),
        out_shape=jax.ShapeDtypeStruct((2, 128), I32),
        in_specs=[SMEM] * 3,
        out_specs=SMEM,
        name="tables",
    )(neighbours, counts, slab_map)
    note = jnp.pad(table[:1].astype(BF), ((0, 15), (0, CUT - 128)))
    tall = PARTS * BLK
    heard = []
    lines = []
    for part, (_, axis, _) in enumerate(ROUTES):
        own = source_tokens[:, :, part * CUT : (part + 1) * CUT].reshape(tall, CUT)
        own = jnp.concatenate([own, note])
        right, left = shift(own, axis, 1), shift(own, axis, -1)
        told = [own, right, shift(right, axis, 1), left]
        heard.append([t[tall, :128].astype(I32) for t in told])
        lines.append((jnp.stack(told[:2]), jnp.stack(told[2:])))
    source = {first: part for part, (_, first, _) in enumerate(ROUTES)}
    rows = [table[0]]
    for across, _, _ in ROUTES:
        rows += [heard[source[across]][SIDE - d] for d in range(1, SIDE)]
    wishes = jnp.stack(rows + [table[1]])
    partner = swap(wishes)
    wishes = wishes + partner
    partner = partner[9:]

    w_keys = w_keyval[:, :WIDTH]
    w_values = jnp.transpose(w_keyval[:, WIDTH:])
    wishes, w_keys, w_values = lax.optimization_barrier((wishes, w_keys, w_values))
    slots = jax.ShapeDtypeStruct((SIDE * SIDE, BLK, CUT), BF)
    small = pltpu.CompilerParams(vmem_limit_bytes=SELECT_VMEM)
    gathered = []
    arrived = []
    for part, (across, _, axis) in enumerate(ROUTES):
        right = [shift(half, axis, 1) for half in lines[part]]
        left = [shift(half, axis, -1) for half in lines[part]]
        far = [shift(right[0], axis, 1), shift(left[1], axis, -1)]
        gathered.append([*lines[part], *right, *far, *left])
        chosen = pl.pallas_call(
            lambda *refs: select_kernel(part, *refs),
            out_shape=[slots] * (SIDE - 1),
            in_specs=[SMEM] * 2 + [VMEM] * 8,
            out_specs=[VMEM] * (SIDE - 1),
            compiler_params=small,
            name="select",
        )(me, wishes, *gathered[part])
        arrived.append([shift(chosen[d - 1], across, d) for d in range(1, SIDE)])
    own_slots = pl.pallas_call(
        own_kernel,
        out_shape=[slots] * PARTS,
        in_specs=[SMEM] * 2 + [VMEM] * 24,
        out_specs=[VMEM] * PARTS,
        compiler_params=small,
        name="own",
    )(me, wishes, *[a for part in gathered for a in part])
    spread = pl.pallas_call(
        spread_kernel,
        out_shape=jax.ShapeDtypeStruct((blocks, PAIRS, 2 * BLK, BLK), BF),
        in_specs=[VMEM] * 2,
        out_specs=VMEM,
        compiler_params=small,
        name="spread",
    )(query_tokens, w_query)
    arrived = [[own_slots[part]] + arrived[part] for part in range(PARTS)]
    items = blocks * -(-2 * CAP // GROUP)
    handed = []
    for part in range(PARTS):
        given = pl.pallas_call(
            lambda *refs: hand_kernel(part, *refs),
            out_shape=jax.ShapeDtypeStruct((blocks * CAP, BLK, CUT), BF),
            in_specs=[SMEM] * 2 + [HBM] * SIDE,
            out_specs=VMEM,
            scratch_shapes=[pltpu.SemaphoreType.DMA],
            name="hand",
        )(me, partner, *arrived[part])
        handed.append(swap(given))
    return pl.pallas_call(
        lambda *refs: attend_kernel(True, True, *refs),
        out_shape=jax.ShapeDtypeStruct(query_tokens.shape, BF),
        in_specs=[SMEM] * 3 + [VMEM] * 4 + [HBM] * 15,
        out_specs=VMEM,
        scratch_shapes=[
            pltpu.SMEM((items,), I32),
            pltpu.SMEM((items,), I32),
            pltpu.SMEM((items * GROUP,), I32),
            pltpu.VMEM((2, ITEM, WIDTH), BF),
            pltpu.VMEM((2, ITEM, WIDTH), BF),
            pltpu.VMEM((2, WIDTH, ITEM), BF),
            pltpu.SemaphoreType.DMA((2,)),
            pltpu.VMEM((blocks, 8, 2 * BLK), F32),
            pltpu.VMEM((blocks, 8, 2 * BLK), F32),
            pltpu.VMEM((blocks, WIDTH, BLK), F32),
        ],
        name="attend",
    )(
        me,
        table,
        counts,
        spread,
        w_keys,
        w_values,
        w_out,
        *[a for part in arrived for a in part],
        *handed,
    )


def solution(mesh):
    placed = (
        P(("pb", "ka"), None),
        P(None, ("pb", "ka"), None),
        P(),
        P(),
        P(),
        P(),
        P(("pb", "ka"), None, None),
        P(("pb", "ka"), None),
    )

    return jax.shard_map(
        on_device, mesh=mesh, in_specs=placed, out_specs=P(("pb", "ka"), None), check_vma=False
    )
```

profile of v0, /device:TPU:1, one launch (start us, length us, event | category | flops | bytes accessed | tf_op | source)
XLA Modules:
  0.0 229.4 jit_solution(14117168930234465615)
XLA Ops:
  1.3 2.3 tables.1.refs_1_
  16.9 2.2 collective-permute-start.27
  20.8 2.2 collective-permute-start.21
  23.1 11.8 %collective-permute-done.8 = bf16[400,256]{1,0:T(8,128)(2,1)S(1)} collective-permute-done((bf16[400,256]{1,0:T(8,128)(2,1)S(1)}, bf16[400,256]{1,0:T(8,128)(2,1)S(1)}, u32[]{:S(2)}, u32[]{:S(2)}) %collective-permute-start.8) | collective-permute-done | bytes 204832 | tf_op jit(solution)/shard_map/ppermute | solution.py:42
  35.0 5.8 %collective-permute-done.5 = bf16[400,256]{1,0:T(8,128)(2,1)S(1)} collective-permute-done((bf16[400,256]{1,0:T(8,128)(2,1)S(1)}, bf16[400,256]{1,0:T(8,128)(2,1)S(1)}, u32[]{:S(2)}, u32[]{:S(2)}) %collective-permute-start.5) | collective-permute-done | bytes 204832 | tf_op jit(solution)/shard_map/ppermute | solution.py:42
  40.8 5.8 %collective-permute-done.2 = bf16[400,256]{1,0:T(8,128)(2,1)S(1)} collective-permute-done((bf16[400,256]{1,0:T(8,128)(2,1)S(1)}, bf16[400,256]{1,0:T(8,128)(2,1)S(1)}, u32[]{:S(2)}, u32[]{:S(2)}) %collective-permute-start.2) | collective-permute-done | bytes 204832 | tf_op jit(solution)/shard_map/ppermute | solution.py:42
  47.3 5.1 %collective-permute-start.9 = (s32[11,128]{1,0:T(8,128)S(1)}, s32[11,128]{1,0:T(8,128)S(1)}, u32[]{:S(2)}, u32[]{:S(2)}) collective-permute-start(s32[11,128]{1,0:T(8,128)S(1)} %stack.86), channel_id=1, source_target_pairs={{0,1},{1,0},{2,3},{3,2},{4,5},{5,4},{6,7},{7,6},{8,9},{9,8},{10,11... | collective-permute-start | bytes 16904 | tf_op jit(solution)/shard_map/ppermute | solution.py:46
  58.7 6.2 %collective-permute-done.25.refs_23_.refs_9_ = bf16[2,400,256]{2,1,0:T(8,128)(2,1)S(1)} collective-permute-done((bf16[2,400,256]{2,1,0:T(8,128)(2,1)S(1)}, bf16[2,400,256]{2,1,0:T(8,128)(2,1)S(1)}, u32[]{:S(2)}, u32[]{:S(2)}) %collective-permute-start.25) | collective-permute-done | bytes 409632 | tf_op jit(solution)/shard_map/ppermute | solution.py:42
  71.3 3.6 %collective-permute-done.24.refs_20_.refs_6_ = bf16[2,400,256]{2,1,0:T(8,128)(2,1)S(1)} collective-permute-done((bf16[2,400,256]{2,1,0:T(8,128)(2,1)S(1)}, bf16[2,400,256]{2,1,0:T(8,128)(2,1)S(1)}, u32[]{:S(2)}, u32[]{:S(2)}) %collective-permute-start.24) | collective-permute-done | bytes 409632 | tf_op jit(solution)/shard_map/ppermute | solution.py:42
  75.8 2.3 collective-permute-done.18.refs_12_.refs_6_
  81.8 2.4 %copy.12 = bf16[768,768]{0,1:T(8,128)(2,1)} copy(bf16[768,768]{1,0:T(8,128)(2,1)} %get-tuple-element.35) | data formatting | bytes 2359296
  90.4 2.8 %select.31 = (bf16[16,128,256]{2,1,0:T(8,128)(2,1)S(1)}, bf16[16,128,256]{2,1,0:T(8,128)(2,1)}, bf16[16,128,256]{2,1,0:T(8,128)(2,1)}) custom-call(s32[4]{0:T(128)S(1)} %pad_add_fusion.me_ref.refs_0_, s32[11,128]{1,0:T(8,128)S(1)} %add.16.table_ref.refs_1_, bf16[2,400,256]{2,1,0:T(8,128)(2,1)S(1)} %pad_maximum_fusion.2.refs_8_.refs_2_, ...), custom_call_target="tpu_custom_call" | custom-call | tf_op jit(solution)/shard_map/select/pallas_call | solution.py:375
  93.2 2.2 collective-permute-start.35
  96.7 31.1 %collective-permute-done.12.refs_4_.refs_6_ = bf16[2,400,256]{2,1,0:T(8,128)(2,1)S(1)} collective-permute-done((bf16[2,400,256]{2,1,0:T(8,128)(2,1)}, bf16[2,400,256]{2,1,0:T(8,128)(2,1)S(1)}, u32[]{:S(2)}, u32[]{:S(2)}) %collective-permute-start.12) | collective-permute-done | bytes 409632 | tf_op jit(solution)/shard_map/ppermute | solution.py:42
  129.1 6.4 %collective-permute-done.14.refs_5_.refs_7_ = bf16[2,400,256]{2,1,0:T(8,128)(2,1)S(1)} collective-permute-done((bf16[2,400,256]{2,1,0:T(8,128)(2,1)}, bf16[2,400,256]{2,1,0:T(8,128)(2,1)S(1)}, u32[]{:S(2)}, u32[]{:S(2)}) %collective-permute-start.14) | collective-permute-done | bytes 409632 | tf_op jit(solution)/shard_map/ppermute | solution.py:42
  136.8 3.3 %select.30 = (bf16[16,128,256]{2,1,0:T(8,128)(2,1)}, bf16[16,128,256]{2,1,0:T(8,128)(2,1)}, bf16[16,128,256]{2,1,0:T(8,128)(2,1)}) custom-call(s32[4]{0:T(128)S(1)} %pad_add_fusion.me_ref.refs_0_, s32[11,128]{1,0:T(8,128)S(1)} %add.16.table_ref.refs_1_, bf16[2,400,256]{2,1,0:T(8,128)(2,1)S(1)} %pad_maximum_fusion.refs_0_.refs_2_, ...), custom_call_target="tpu_custom_call" | custom-call | tf_op jit(solution)/shard_map/select/pallas_call | solution.py:375
  142.4 2.5 %collective-permute-start.29 = (bf16[16,128,256]{2,1,0:T(8,128)(2,1)}, bf16[16,128,256]{2,1,0:T(8,128)(2,1)}, u32[]{:S(2)}, u32[]{:S(2)}) collective-permute-start(bf16[16,128,256]{2,1,0:T(8,128)(2,1)} %get-tuple-element.25), channel_id=1, source_target_pairs={{0,4},{2,6},{4,0},{6,2},{8,12},{10,14},{12,8},{14,10},{16,20},{18,... | collective-permute-start | bytes 3145736 | tf_op jit(solution)/shard_map/ppermute | solution.py:42
  150.6 3.9 %hand.5 = bf16[24,128,256]{2,1,0:T(8,128)(2,1)} custom-call(s32[4]{0:T(128)} %copy-done.24, s32[2,128]{1,0:T(2,128)} %slice.78.refs_1_, bf16[16,128,256]{2,1,0:T(8,128)(2,1)} %copy-done.3, bf16[16,128,256]{2,1,0:T(8,128)(2,1)} %copy-done.25, bf16[16,128,256]{2,1,0:T(8,128)(2,1)} %copy-done.26, bf16[16,128,256]{2,1,0:T(8,128)(2,1)} %copy-done.27), custom_call_target="tpu_custom_call" | custom-call | tf_op jit(solution)/shard_map/hand/pallas_call | solution.py:404
  154.5 3.3 %collective-permute-done.32.refs_4_.refs_13_ = bf16[16,128,256]{2,1,0:T(8,128)(2,1)} collective-permute-done((bf16[16,128,256]{2,1,0:T(8,128)(2,1)}, bf16[16,128,256]{2,1,0:T(8,128)(2,1)}, u32[]{:S(2)}, u32[]{:S(2)}) %collective-permute-start.32) | collective-permute-done | bytes 1048608 | tf_op jit(solution)/shard_map/ppermute | solution.py:42
  157.9 5.2 %collective-permute-start.39 = (bf16[24,128,256]{2,1,0:T(8,128)(2,1)}, bf16[24,128,256]{2,1,0:T(8,128)(2,1)S(1)}, u32[]{:S(2)}, u32[]{:S(2)}) collective-permute-start(bf16[24,128,256]{2,1,0:T(8,128)(2,1)} %hand.5), channel_id=1, source_target_pairs={{0,1},{1,0},{2,3},{3,2},{4,5},{5,4},{6,7},{7,6},{8,9},{9,8},{10,11... | collective-permute-start | bytes 4718600 | tf_op jit(solution)/shard_map/ppermute | solution.py:46
  163.0 21.0 %collective-permute-done.33.refs_5_.refs_14_ = bf16[16,128,256]{2,1,0:T(8,128)(2,1)} collective-permute-done((bf16[16,128,256]{2,1,0:T(8,128)(2,1)}, bf16[16,128,256]{2,1,0:T(8,128)(2,1)}, u32[]{:S(2)}, u32[]{:S(2)}) %collective-permute-start.33) | collective-permute-done | bytes 1048608 | tf_op jit(solution)/shard_map/ppermute | solution.py:42
  184.0 3.9 %hand.4 = bf16[24,128,256]{2,1,0:T(8,128)(2,1)} custom-call(s32[4]{0:T(128)} %copy-done.24, s32[2,128]{1,0:T(2,128)} %slice.78.refs_1_, bf16[16,128,256]{2,1,0:T(8,128)(2,1)} %copy-done.2, bf16[16,128,256]{2,1,0:T(8,128)(2,1)} %copy-done.28, bf16[16,128,256]{2,1,0:T(8,128)(2,1)} %collective-permute-done.32.refs_4_.refs_13_, ...), custom_call_target="tpu_custom_call" | custom-call | tf_op jit(solution)/shard_map/hand/pallas_call | solution.py:404
  190.2 4.0 %hand.3 = bf16[24,128,256]{2,1,0:T(8,128)(2,1)} custom-call(s32[4]{0:T(128)} %copy-done.24, s32[2,128]{1,0:T(2,128)} %slice.78.refs_1_, bf16[16,128,256]{2,1,0:T(8,128)(2,1)} %copy-done.1, bf16[16,128,256]{2,1,0:T(8,128)(2,1)} %collective-permute-done.28.refs_3_.refs_8_, bf16[16,128,256]{2,1,0:T(8,128)(2,1)} %collective-permute-done.29.refs_4_.refs_9_, ...), custom_call_target="tpu_custom_call" | custom-call | tf_op jit(solution)/shard_map/hand/pallas_call | solution.py:404
  198.7 30.5 %attend.1 = bf16[512,768]{1,0:T(8,128)(2,1)} custom-call(s32[4]{0:T(128)} %copy-done.24, s32[2,128]{1,0:T(2,128)} %tables.1.refs_1_, s32[4,2]{1,0:T(4,128)} %copy.9.refs_1_.refs_2_, bf16[4,6,256,128]{3,2,1,0:T(8,128)(2,1)} %copy-done, bf16[768,768]{1,0:T(8,128)(2,1)} %get-tuple-element.20.refs_4_, bf16[768,768]{1,0:T(8,128)(2,1)} %bitcast.23, ...), custom_call_target="tpu_custom_call" | custom-call | tf_op jit(solution)/shard_map/attend/pallas_call | solution.py:413
  (163 shorter events, 58.9 us)
Async XLA Ops:
  16.3 37.5 %collective-permute-start.22 = (bf16[2,400,256]{2,1,0:T(8,128)(2,1)S(1)}, bf16[2,400,256]{2,1,0:T(8,128)(2,1)S(1)}, u32[]{:S(2)}, u32[]{:S(2)}) collective-permute-start(bf16[2,400,256]{2,1,0:T(8,128)(2,1)S(1)} %pad_maximum_fusion.4.refs_16_.refs_2_), channel_id=1, source_target_pairs={{0,2},{2,4},{4,6},{6,0},{8,10},{10,12},{12,14},{14,8},{16,18},{18,... | collective-permute-start | bytes 1228808 | tf_op jit(solution)/shard_map/ppermute | solution.py:42
  16.9 39.4 %collective-permute-start.27 = (bf16[2,400,256]{2,1,0:T(8,128)(2,1)S(1)}, bf16[2,400,256]{2,1,0:T(8,128)(2,1)S(1)}, u32[]{:S(2)}, u32[]{:S(2)}) collective-permute-start(bf16[2,400,256]{2,1,0:T(8,128)(2,1)S(1)} %pad_maximum_fusion.4.refs_16_.refs_2_), channel_id=1, source_target_pairs={{0,6},{2,0},{4,2},{6,4},{8,14},{10,8},{12,10},{14,12},{16,22},{18,... | collective-permute-start | bytes 1228808 | tf_op jit(solution)/shard_map/ppermute | solution.py:42
  19.2 38.7 %collective-permute-start.16 = (bf16[2,400,256]{2,1,0:T(8,128)(2,1)S(1)}, bf16[2,400,256]{2,1,0:T(8,128)(2,1)}, u32[]{:S(2)}, u32[]{:S(2)}) collective-permute-start(bf16[2,400,256]{2,1,0:T(8,128)(2,1)S(1)} %pad_maximum_fusion.2.refs_8_.refs_2_), channel_id=1, source_target_pairs={{0,32},{2,34},{4,36},{6,38},{8,40},{10,42},{12,44},{14,46},{16,48}... | collective-permute-start | bytes 1228808 | tf_op jit(solution)/shard_map/ppermute | solution.py:42
  20.8 37.1 %collective-permute-start.21 = (bf16[2,400,256]{2,1,0:T(8,128)(2,1)S(1)}, bf16[2,400,256]{2,1,0:T(8,128)(2,1)S(1)}, u32[]{:S(2)}, u32[]{:S(2)}) collective-permute-start(bf16[2,400,256]{2,1,0:T(8,128)(2,1)S(1)} %pad_maximum_fusion.2.refs_8_.refs_2_), channel_id=1, source_target_pairs={{0,96},{2,98},{4,100},{6,102},{8,104},{10,106},{12,108},{14,110},{... | collective-permute-start | bytes 1228808 | tf_op jit(solution)/shard_map/ppermute | solution.py:42
  23.0 11.9 %collective-permute-start.8 = (bf16[400,256]{1,0:T(8,128)(2,1)S(1)}, bf16[400,256]{1,0:T(8,128)(2,1)S(1)}, u32[]{:S(2)}, u32[]{:S(2)}) collective-permute-start(bf16[400,256]{1,0:T(8,128)(2,1)S(1)} %collective-permute-done.7), channel_id=1, source_target_pairs={{0,32},{2,34},{4,36},{6,38},{8,40},{10,42},{12,44},{14,46},{16,48}... | collective-permute-start | bytes 614408 | tf_op jit(solution)/shard_map/ppermute | solution.py:42
  53.8 12.3 %collective-permute-start.23 = (bf16[2,400,256]{2,1,0:T(8,128)(2,1)S(1)}, bf16[2,400,256]{2,1,0:T(8,128)(2,1)S(1)}, u32[]{:S(2)}, u32[]{:S(2)}) collective-permute-start(bf16[2,400,256]{2,1,0:T(8,128)(2,1)S(1)} %pad_maximum_fusion.5.refs_17_.refs_3_), channel_id=1, source_target_pairs={{0,2},{2,4},{4,6},{6,0},{8,10},{10,12},{12,14},{14,8},{16,18},{18,... | collective-permute-start | bytes 1228808 | tf_op jit(solution)/shard_map/ppermute | solution.py:42
  58.7 16.3 %collective-permute-start.24 = (bf16[2,400,256]{2,1,0:T(8,128)(2,1)S(1)}, bf16[2,400,256]{2,1,0:T(8,128)(2,1)S(1)}, u32[]{:S(2)}, u32[]{:S(2)}) collective-permute-start(bf16[2,400,256]{2,1,0:T(8,128)(2,1)S(1)} %collective-permute-done.22.refs_18_.refs_4_), channel_id=1, source_target_pairs={{0,2},{2,4},{4,6},{6,0},{8,10},{10,12},{12,14},{14,8},{16,18},{18,... | collective-permute-start | bytes 1228808 | tf_op jit(solution)/shard_map/ppermute | solution.py:42
  64.9 13.2 %collective-permute-start.18 = (bf16[2,400,256]{2,1,0:T(8,128)(2,1)}, bf16[2,400,256]{2,1,0:T(8,128)(2,1)S(1)}, u32[]{:S(2)}, u32[]{:S(2)}) collective-permute-start(bf16[2,400,256]{2,1,0:T(8,128)(2,1)} %collective-permute-done.16.refs_10_.refs_4_), channel_id=1, source_target_pairs={{0,32},{2,34},{4,36},{6,38},{8,40},{10,42},{12,44},{14,46},{16,48}... | collective-permute-start | bytes 1228808 | tf_op jit(solution)/shard_map/ppermute | solution.py:42
  66.1 12.8 %collective-permute-start.26 = (bf16[2,400,256]{2,1,0:T(8,128)(2,1)S(1)}, bf16[2,400,256]{2,1,0:T(8,128)(2,1)S(1)}, u32[]{:S(2)}, u32[]{:S(2)}) collective-permute-start(bf16[2,400,256]{2,1,0:T(8,128)(2,1)S(1)} %collective-permute-done.25.refs_23_.refs_9_), channel_id=1, source_target_pairs={{0,6},{2,0},{4,2},{6,4},{8,14},{10,8},{12,10},{14,12},{16,22},{18,... | collective-permute-start | bytes 1228808 | tf_op jit(solution)/shard_map/ppermute | solution.py:42
  67.8 25.3 %collective-permute-start.10 = (bf16[2,400,256]{2,1,0:T(8,128)(2,1)S(1)}, bf16[2,400,256]{2,1,0:T(8,128)(2,1)}, u32[]{:S(2)}, u32[]{:S(2)}) collective-permute-start(bf16[2,400,256]{2,1,0:T(8,128)(2,1)S(1)} %pad_maximum_fusion.refs_0_.refs_2_), channel_id=1, source_target_pairs={{0,8},{2,10},{4,12},{6,14},{8,16},{10,18},{12,20},{14,22},{16,24},... | collective-permute-start | bytes 1228808 | tf_op jit(solution)/shard_map/ppermute | solution.py:42
  70.0 25.5 %collective-permute-start.15 = (bf16[2,400,256]{2,1,0:T(8,128)(2,1)S(1)}, bf16[2,400,256]{2,1,0:T(8,128)(2,1)}, u32[]{:S(2)}, u32[]{:S(2)}) collective-permute-start(bf16[2,400,256]{2,1,0:T(8,128)(2,1)S(1)} %pad_maximum_fusion.refs_0_.refs_2_), channel_id=1, source_target_pairs={{0,24},{2,26},{4,28},{6,30},{8,0},{10,2},{12,4},{14,6},{16,8},{18,... | collective-permute-start | bytes 1228808 | tf_op jit(solution)/shard_map/ppermute | solution.py:42
  75.7 19.9 %collective-permute-start.13 = (bf16[2,400,256]{2,1,0:T(8,128)(2,1)S(1)}, bf16[2,400,256]{2,1,0:T(8,128)(2,1)}, u32[]{:S(2)}, u32[]{:S(2)}) collective-permute-start(bf16[2,400,256]{2,1,0:T(8,128)(2,1)S(1)} %pad_maximum_fusion.1.refs_1_.refs_3_), channel_id=1, source_target_pairs={{0,24},{2,26},{4,28},{6,30},{8,0},{10,2},{12,4},{14,6},{16,8},{18,... | collective-permute-start | bytes 1228808 | tf_op jit(solution)/shard_map/ppermute | solution.py:42
  78.9 16.9 %collective-permute-start.11 = (bf16[2,400,256]{2,1,0:T(8,128)(2,1)S(1)}, bf16[2,400,256]{2,1,0:T(8,128)(2,1)}, u32[]{:S(2)}, u32[]{:S(2)}) collective-permute-start(bf16[2,400,256]{2,1,0:T(8,128)(2,1)S(1)} %pad_maximum_fusion.1.refs_1_.refs_3_), channel_id=1, source_target_pairs={{0,8},{2,10},{4,12},{6,14},{8,16},{10,18},{12,20},{14,22},{16,24},... | collective-permute-start | bytes 1228808 | tf_op jit(solution)/shard_map/ppermute | solution.py:42
  89.4 50.8 %collective-permute-start.34 = (bf16[16,128,256]{2,1,0:T(8,128)(2,1)S(1)}, bf16[16,128,256]{2,1,0:T(8,128)(2,1)S(1)}, u32[]{:S(2)}, u32[]{:S(2)}) collective-permute-start(bf16[16,128,256]{2,1,0:T(8,128)(2,1)S(1)} %get-tuple-element.32), channel_id=1, source_target_pairs={{0,32},{2,34},{4,36},{6,38},{8,40},{10,42},{12,44},{14,46},{16,48}... | collective-permute-start | bytes 3145736 | tf_op jit(solution)/shard_map/ppermute | solution.py:42
  93.2 48.4 %collective-permute-start.35 = (bf16[16,128,256]{2,1,0:T(8,128)(2,1)S(1)}, bf16[16,128,256]{2,1,0:T(8,128)(2,1)S(1)}, u32[]{:S(2)}, u32[]{:S(2)}) collective-permute-start(bf16[16,128,256]{2,1,0:T(8,128)(2,1)S(1)} %get-tuple-element.33), channel_id=1, source_target_pairs={{0,64},{2,66},{4,68},{6,70},{8,72},{10,74},{12,76},{14,78},{16,80}... | collective-permute-start | bytes 3145736 | tf_op jit(solution)/shard_map/ppermute | solution.py:42
  95.4 47.0 %collective-permute-start.36 = (bf16[16,128,256]{2,1,0:T(8,128)(2,1)S(1)}, bf16[16,128,256]{2,1,0:T(8,128)(2,1)S(1)}, u32[]{:S(2)}, u32[]{:S(2)}) collective-permute-start(bf16[16,128,256]{2,1,0:T(8,128)(2,1)S(1)} %get-tuple-element.34), channel_id=1, source_target_pairs={{0,96},{2,98},{4,100},{6,102},{8,104},{10,106},{12,108},{14,110},{... | collective-permute-start | bytes 3145736 | tf_op jit(solution)/shard_map/ppermute | solution.py:42
  95.7 49.2 %collective-permute-start.31 = (bf16[16,128,256]{2,1,0:T(8,128)(2,1)S(1)}, bf16[16,128,256]{2,1,0:T(8,128)(2,1)S(1)}, u32[]{:S(2)}, u32[]{:S(2)}) collective-permute-start(bf16[16,128,256]{2,1,0:T(8,128)(2,1)S(1)} %get-tuple-element.28), channel_id=1, source_target_pairs={{0,8},{2,10},{4,12},{6,14},{8,16},{10,18},{12,20},{14,22},{16,24},... | collective-permute-start | bytes 3145736 | tf_op jit(solution)/shard_map/ppermute | solution.py:42
  95.8 32.0 %collective-permute-start.12 = (bf16[2,400,256]{2,1,0:T(8,128)(2,1)}, bf16[2,400,256]{2,1,0:T(8,128)(2,1)S(1)}, u32[]{:S(2)}, u32[]{:S(2)}) collective-permute-start(bf16[2,400,256]{2,1,0:T(8,128)(2,1)} %collective-permute-done.10.refs_2_.refs_4_), channel_id=1, source_target_pairs={{0,8},{2,10},{4,12},{6,14},{8,16},{10,18},{12,20},{14,22},{16,24},... | collective-permute-start | bytes 1228808 | tf_op jit(solution)/shard_map/ppermute | solution.py:42
  135.6 22.3 %collective-permute-start.32 = (bf16[16,128,256]{2,1,0:T(8,128)(2,1)}, bf16[16,128,256]{2,1,0:T(8,128)(2,1)}, u32[]{:S(2)}, u32[]{:S(2)}) collective-permute-start(bf16[16,128,256]{2,1,0:T(8,128)(2,1)} %get-tuple-element.29), channel_id=1, source_target_pairs={{0,16},{2,18},{4,20},{6,22},{8,24},{10,26},{12,28},{14,30},{16,0},... | collective-permute-start | bytes 3145736 | tf_op jit(solution)/shard_map/ppermute | solution.py:42
  140.2 43.8 %collective-permute-start.33 = (bf16[16,128,256]{2,1,0:T(8,128)(2,1)}, bf16[16,128,256]{2,1,0:T(8,128)(2,1)}, u32[]{:S(2)}, u32[]{:S(2)}) collective-permute-start(bf16[16,128,256]{2,1,0:T(8,128)(2,1)} %get-tuple-element.30), channel_id=1, source_target_pairs={{0,24},{2,26},{4,28},{6,30},{8,0},{10,2},{12,4},{14,6},{16,8},{18,... | collective-permute-start | bytes 3145736 | tf_op jit(solution)/shard_map/ppermute | solution.py:42
  141.6 47.5 %collective-permute-start.28 = (bf16[16,128,256]{2,1,0:T(8,128)(2,1)}, bf16[16,128,256]{2,1,0:T(8,128)(2,1)}, u32[]{:S(2)}, u32[]{:S(2)}) collective-permute-start(bf16[16,128,256]{2,1,0:T(8,128)(2,1)} %get-tuple-element.24), channel_id=1, source_target_pairs={{0,2},{2,4},{4,6},{6,0},{8,10},{10,12},{12,14},{14,8},{16,18},{18,... | collective-permute-start | bytes 3145736 | tf_op jit(solution)/shard_map/ppermute | solution.py:42
  142.4 46.6 %collective-permute-start.29 = (bf16[16,128,256]{2,1,0:T(8,128)(2,1)}, bf16[16,128,256]{2,1,0:T(8,128)(2,1)}, u32[]{:S(2)}, u32[]{:S(2)}) collective-permute-start(bf16[16,128,256]{2,1,0:T(8,128)(2,1)} %get-tuple-element.25), channel_id=1, source_target_pairs={{0,4},{2,6},{4,0},{6,2},{8,12},{10,14},{12,8},{14,10},{16,20},{18,... | collective-permute-start | bytes 3145736 | tf_op jit(solution)/shard_map/ppermute | solution.py:42
  144.9 45.3 %collective-permute-start.30 = (bf16[16,128,256]{2,1,0:T(8,128)(2,1)}, bf16[16,128,256]{2,1,0:T(8,128)(2,1)}, u32[]{:S(2)}, u32[]{:S(2)}) collective-permute-start(bf16[16,128,256]{2,1,0:T(8,128)(2,1)} %get-tuple-element.26), channel_id=1, source_target_pairs={{0,6},{2,0},{4,2},{6,4},{8,14},{10,8},{12,10},{14,12},{16,22},{18,... | collective-permute-start | bytes 3145736 | tf_op jit(solution)/shard_map/ppermute | solution.py:42
  157.9 39.5 %collective-permute-start.39 = (bf16[24,128,256]{2,1,0:T(8,128)(2,1)}, bf16[24,128,256]{2,1,0:T(8,128)(2,1)S(1)}, u32[]{:S(2)}, u32[]{:S(2)}) collective-permute-start(bf16[24,128,256]{2,1,0:T(8,128)(2,1)} %hand.5), channel_id=1, source_target_pairs={{0,1},{1,0},{2,3},{3,2},{4,5},{5,4},{6,7},{7,6},{8,9},{9,8},{10,11... | collective-permute-start | bytes 4718600 | tf_op jit(solution)/shard_map/ppermute | solution.py:46
  (52 other events, 417.5 us)
where the time goes:
time: 232 us; the launch traced here: 229 us
  waiting for transfers between devices  103 us (44%)
  Pallas kernels  54.4 us (23%)
  starting transfers between devices  46.7 us (20%)
  local copies, waits for them, and re-layouts  20.3 us (9%)
  other arithmetic  4.29 us (2%)
    ppermute x36, waiting for transfers between devices, shift(): return lax.ppermute(value, 'pb', pairs)  102 us
    ppermute x36, starting transfers between devices, shift(): return lax.ppermute(value, 'pb', pairs)  34.2 us
    pallas_call x1, Pallas kernels, on_device(): pl.pallas_call(lambda *refs: attend_kernel(True, True, *refs), out_shape=...  30.5 us
    unnamed x74, local copies, waits for them, and re-layouts  16.9 us
    ppermute x4, starting transfers between devices, swap(): return lax.ppermute(value, 'ka', [(0, 1), (1, 0)])  12.5 us
    pallas_call x3, Pallas kernels, on_device(): pl.pallas_call(lambda *refs: hand_kernel(part, *refs), out_shape=jax.Shap...  11.8 us
    pallas_call x3, Pallas kernels, on_device(): pl.pallas_call(lambda *refs: select_kernel(part, *refs), out_shape=[slots...  7.04 us
  transfers between devices with their start and end apart: 40, of which 16 were waited for; matrix products, arithmetic and copies ran while one was open for 4% of the time, Pallas kernels for 9%

commit v1 on v0

--- a/solution.py
+++ b/solution.py
@@ -78,18 +78,24 @@
 
 def walk_slots(part, me_ref, table_ref, gathered, outs):
     across, first, second = ROUTES[part]
-    for d2 in range(SIDE):
-        for d1 in range(SIDE):
-            at = [None, None, None]
-            at[across] = me_ref[across]
-            at[first] = me_ref[first] + 4 - d1 & 3
-            at[second] = me_ref[second] + 4 - d2 & 3
-            place = me_ref[3] * 64 + at[0] * 16 + at[1] * 4 + at[2]
-            line, row = gathered[d2 * 2 + d1 // 2], d1 % 2
-            for d, out in outs:
-                which = table_ref[0 if d == 0 else 3 * part + d, place]
-                begin = pl.multiple_of(jnp.maximum(which - 1, 0) * BLK, BLK)
-                out[d2 * 4 + d1] = line[row, pl.ds(begin, BLK), :]
+
+    def body(low, _):
+        for d2 in range(SIDE):
+            for high in range(2):
+                d1 = high * 2 + low
+                at = [None, None, None]
+                at[across] = me_ref[across]
+                at[first] = me_ref[first] + 4 - d1 & 3
+                at[second] = me_ref[second] + 4 - d2 & 3
+                place = me_ref[3] * 64 + at[0] * 16 + at[1] * 4 + at[2]
+                line = gathered[d2 * 2 + high]
+                for d, out in outs:
+                    which = table_ref[0 if d == 0 else 3 * part + d, place]
+                    begin = pl.multiple_of(jnp.maximum(which - 1, 0) * BLK, BLK)
+                    out[d2 * 4 + d1] = line[low, pl.ds(begin, BLK), :]
+        return 0
+
+    lax.fori_loop(0, 2, body, 0)
 
 
 def select_kernel(part, me_ref, table_ref, *refs):
@@ -349,22 +355,21 @@
         own = jnp.concatenate([own, note])
         right, left = shift(own, axis, 1), shift(own, axis, -1)
         told = [own, right, shift(right, axis, 1), left]
-        heard.append([t[tall, :128].astype(I32) for t in told])
+        heard.append(told)
         lines.append((jnp.stack(told[:2]), jnp.stack(told[2:])))
     source = {first: part for part, (_, first, _) in enumerate(ROUTES)}
-    rows = [table[0]]
-    for across, _, _ in ROUTES:
-        rows += [heard[source[across]][SIDE - d] for d in range(1, SIDE)]
-    wishes = jnp.stack(rows + [table[1]])
+    told = [heard[source[across]][SIDE - d] for across, _, _ in ROUTES for d in range(1, SIDE)]
+    small = pltpu.CompilerParams(vmem_limit_bytes=SELECT_VMEM)
+    notes = jnp.concatenate([t[tall : tall + 1, :128] for t in told]).astype(I32)
+    wishes = jnp.concatenate([table[:1], notes, table[1:]])
     partner = swap(wishes)
     wishes = wishes + partner
-    partner = partner[9:]
+    partner = partner[9:11]
 
     w_keys = w_keyval[:, :WIDTH]
     w_values = jnp.transpose(w_keyval[:, WIDTH:])
     wishes, w_keys, w_values = lax.optimization_barrier((wishes, w_keys, w_values))
     slots = jax.ShapeDtypeStruct((SIDE * SIDE, BLK, CUT), BF)
-    small = pltpu.CompilerParams(vmem_limit_bytes=SELECT_VMEM)
     gathered = []
     arrived = []
     for part, (across, _, axis) in enumerate(ROUTES):

time: 232 us -> 213 us (0.918)
  waiting for transfers between devices: 103 us -> 84.1 us
  local copies, waits for them, and re-layouts: 20.3 us -> 17.2 us
    ppermute x36, waiting for transfers between devices: 102 us -> 82.7 us  [shift(): return lax.ppermute(value, 'pb', pairs)]
    unnamed x74 -> x60, local copies, waits for them, and re-layouts: 16.9 us -> 13.7 us
  transfers between devices with their start and end apart: 40 -> 40, of which waited for: 16 -> 13; matrix products, arithmetic and copies ran while one was open for 4% -> 4% of each run, Pallas kernels for 9% -> 11%
where the time goes in v1:
time: 213 us; the launch traced here: 210 us
  waiting for transfers between devices  84.1 us (39%)
  Pallas kernels  55.6 us (26%)
  starting transfers between devices  48.8 us (23%)
  local copies, waits for them, and re-layouts  17.2 us (8%)
  other arithmetic  4.31 us (2%)
    ppermute x36, waiting for transfers between devices, shift(): return lax.ppermute(value, 'pb', pairs)  82.7 us
    ppermute x36, starting transfers between devices, shift(): return lax.ppermute(value, 'pb', pairs)  35.5 us
    pallas_call x1, Pallas kernels, on_device(): pl.pallas_call(lambda *refs: attend_kernel(True, True, *refs), out_shape=...  30.4 us
    unnamed x60, local copies, waits for them, and re-layouts  13.7 us
    ppermute x4, starting transfers between devices, swap(): return lax.ppermute(value, 'ka', [(0, 1), (1, 0)])  13.3 us
    pallas_call x3, Pallas kernels, on_device(): pl.pallas_call(lambda *refs: hand_kernel(part, *refs), out_shape=jax.Shap...  12.3 us
    pallas_call x3, Pallas kernels, on_device(): pl.pallas_call(lambda *refs: select_kernel(part, *refs), out_shape=[slots...  7.52 us
  transfers between devices with their start and end apart: 40, of which 13 were waited for; matrix products, arithmetic and copies ran while one was open for 4% of the time, Pallas kernels for 11%

profile of v1, /device:TPU:1, one launch (start us, length us, event | category | flops | bytes accessed | tf_op | source)
XLA Modules:
  0.0 210.5 jit_solution(4801364220076440784)
XLA Ops:
  1.3 2.3 %tables.1.refs_1_ = s32[2,128]{1,0:T(2,128)} custom-call(s32[4,2,6]{2,1,0:T(2,128)} %refs_0_.1, s32[4,2]{1,0:T(4,128)} %copy.9.refs_1_.refs_2_, s32[3,128]{1,0:T(4,128)} %refs_2_.2), custom_call_target="tpu_custom_call" | custom-call | tf_op jit(solution)/shard_map/tables/pallas_call | solution.py:342
  5.6 2.1 collective-permute-start.1
  13.5 3.9 %collective-permute-start.6 = (bf16[400,256]{1,0:T(8,128)(2,1)S(1)}, bf16[400,256]{1,0:T(8,128)(2,1)S(1)}, u32[]{:S(2)}, u32[]{:S(2)}) collective-permute-start(bf16[400,256]{1,0:T(8,128)(2,1)S(1)} %get-tuple-element.51), channel_id=1, source_target_pairs={{0,96},{2,98},{4,100},{6,102},{8,104},{10,106},{12,108},{14,110},{... | collective-permute-start | bytes 614408 | tf_op jit(solution)/shard_map/ppermute | solution.py:42
  23.7 2.2 %collective-permute-start.21 = (bf16[2,400,256]{2,1,0:T(8,128)(2,1)S(1)}, bf16[2,400,256]{2,1,0:T(8,128)(2,1)S(1)}, u32[]{:S(2)}, u32[]{:S(2)}) collective-permute-start(bf16[2,400,256]{2,1,0:T(8,128)(2,1)S(1)} %pad_maximum_fusion.2.refs_8_.refs_2_), channel_id=1, source_target_pairs={{0,96},{2,98},{4,100},{6,102},{8,104},{10,106},{12,108},{14,110},{... | collective-permute-start | bytes 1228808 | tf_op jit(solution)/shard_map/ppermute | solution.py:42
  26.0 5.8 %collective-permute-start.9 = (s32[11,128]{1,0:T(8,128)S(1)}, s32[11,128]{1,0:T(8,128)S(1)}, u32[]{:S(2)}, u32[]{:S(2)}) collective-permute-start(s32[11,128]{1,0:T(8,128)S(1)} %pad_add_fusion), channel_id=1, source_target_pairs={{0,1},{1,0},{2,3},{3,2},{4,5},{5,4},{6,7},{7,6},{8,9},{9,8},{10,11... | collective-permute-start | bytes 16904 | tf_op jit(solution)/shard_map/ppermute | solution.py:46
  38.1 6.1 %collective-permute-done.25.refs_23_.refs_9_ = bf16[2,400,256]{2,1,0:T(8,128)(2,1)} collective-permute-done((bf16[2,400,256]{2,1,0:T(8,128)(2,1)S(1)}, bf16[2,400,256]{2,1,0:T(8,128)(2,1)}, u32[]{:S(2)}, u32[]{:S(2)}) %collective-permute-start.25) | collective-permute-done | bytes 409632 | tf_op jit(solution)/shard_map/ppermute | solution.py:42
  45.2 2.2 %collective-permute-done.23.refs_19_.refs_5_ = bf16[2,400,256]{2,1,0:T(8,128)(2,1)S(1)} collective-permute-done((bf16[2,400,256]{2,1,0:T(8,128)(2,1)S(1)}, bf16[2,400,256]{2,1,0:T(8,128)(2,1)S(1)}, u32[]{:S(2)}, u32[]{:S(2)}) %collective-permute-start.23) | collective-permute-done | bytes 409632 | tf_op jit(solution)/shard_map/ppermute | solution.py:42
  51.9 4.5 %collective-permute-done.24.refs_20_.refs_6_ = bf16[2,400,256]{2,1,0:T(8,128)(2,1)S(1)} collective-permute-done((bf16[2,400,256]{2,1,0:T(8,128)(2,1)S(1)}, bf16[2,400,256]{2,1,0:T(8,128)(2,1)S(1)}, u32[]{:S(2)}, u32[]{:S(2)}) %collective-permute-start.24) | collective-permute-done | bytes 409632 | tf_op jit(solution)/shard_map/ppermute | solution.py:42
  59.5 2.4 %copy.12 = bf16[768,768]{0,1:T(8,128)(2,1)} copy(bf16[768,768]{1,0:T(8,128)(2,1)} %get-tuple-element.35) | data formatting | bytes 2359296
  62.0 5.4 %collective-permute-done.26.refs_21_.refs_7_ = bf16[2,400,256]{2,1,0:T(8,128)(2,1)} collective-permute-done((bf16[2,400,256]{2,1,0:T(8,128)(2,1)}, bf16[2,400,256]{2,1,0:T(8,128)(2,1)}, u32[]{:S(2)}, u32[]{:S(2)}) %collective-permute-start.26) | collective-permute-done | bytes 409632 | tf_op jit(solution)/shard_map/ppermute | solution.py:42
  72.3 2.8 %select.31 = (bf16[16,128,256]{2,1,0:T(8,128)(2,1)S(1)}, bf16[16,128,256]{2,1,0:T(8,128)(2,1)}, bf16[16,128,256]{2,1,0:T(8,128)(2,1)}) custom-call(s32[4]{0:T(128)S(1)} %pad_add_fusion.1.me_ref.refs_0_, s32[11,128]{1,0:T(8,128)S(1)} %fusion.10.table_ref.refs_1_, bf16[2,400,256]{2,1,0:T(8,128)(2,1)S(1)} %pad_maximum_fusion.2.refs_8_.refs_2_, ...), custom_call_target="tpu_custom_call" | custom-call | tf_op jit(solution)/shard_map/select/pallas_call | solution.py:380
  75.6 2.3 %collective-permute-start.36 = (bf16[16,128,256]{2,1,0:T(8,128)(2,1)S(1)}, bf16[16,128,256]{2,1,0:T(8,128)(2,1)S(1)}, u32[]{:S(2)}, u32[]{:S(2)}) collective-permute-start(bf16[16,128,256]{2,1,0:T(8,128)(2,1)S(1)} %get-tuple-element.34), channel_id=1, source_target_pairs={{0,96},{2,98},{4,100},{6,102},{8,104},{10,106},{12,108},{14,110},{... | collective-permute-start | bytes 3145736 | tf_op jit(solution)/shard_map/ppermute | solution.py:42
  79.0 30.8 %collective-permute-done.12.refs_4_.refs_6_ = bf16[2,400,256]{2,1,0:T(8,128)(2,1)S(1)} collective-permute-done((bf16[2,400,256]{2,1,0:T(8,128)(2,1)}, bf16[2,400,256]{2,1,0:T(8,128)(2,1)S(1)}, u32[]{:S(2)}, u32[]{:S(2)}) %collective-permute-start.12) | collective-permute-done | bytes 409632 | tf_op jit(solution)/shard_map/ppermute | solution.py:42
  110.2 7.0 %collective-permute-done.14.refs_5_.refs_7_ = bf16[2,400,256]{2,1,0:T(8,128)(2,1)S(1)} collective-permute-done((bf16[2,400,256]{2,1,0:T(8,128)(2,1)}, bf16[2,400,256]{2,1,0:T(8,128)(2,1)S(1)}, u32[]{:S(2)}, u32[]{:S(2)}) %collective-permute-start.14) | collective-permute-done | bytes 409632 | tf_op jit(solution)/shard_map/ppermute | solution.py:42
  117.5 3.2 %select.30 = (bf16[16,128,256]{2,1,0:T(8,128)(2,1)}, bf16[16,128,256]{2,1,0:T(8,128)(2,1)}, bf16[16,128,256]{2,1,0:T(8,128)(2,1)}) custom-call(s32[4]{0:T(128)S(1)} %pad_add_fusion.1.me_ref.refs_0_, s32[11,128]{1,0:T(8,128)S(1)} %fusion.10.table_ref.refs_1_, bf16[2,400,256]{2,1,0:T(8,128)(2,1)S(1)} %pad_maximum_fusion.refs_0_.refs_2_, ...), custom_call_target="tpu_custom_call" | custom-call | tf_op jit(solution)/shard_map/select/pallas_call | solution.py:380
  123.0 2.9 %collective-permute-start.29 = (bf16[16,128,256]{2,1,0:T(8,128)(2,1)}, bf16[16,128,256]{2,1,0:T(8,128)(2,1)}, u32[]{:S(2)}, u32[]{:S(2)}) collective-permute-start(bf16[16,128,256]{2,1,0:T(8,128)(2,1)} %get-tuple-element.25), channel_id=1, source_target_pairs={{0,4},{2,6},{4,0},{6,2},{8,12},{10,14},{12,8},{14,10},{16,20},{18,... | collective-permute-start | bytes 3145736 | tf_op jit(solution)/shard_map/ppermute | solution.py:42
  126.6 2.2 %own.1 = (bf16[16,128,256]{2,1,0:T(8,128)(2,1)S(1)}, bf16[16,128,256]{2,1,0:T(8,128)(2,1)S(1)}, bf16[16,128,256]{2,1,0:T(8,128)(2,1)S(1)}) custom-call(s32[4]{0:T(128)S(1)} %pad_add_fusion.1.me_ref.refs_0_, s32[11,128]{1,0:T(8,128)S(1)} %fusion.10.table_ref.refs_1_, bf16[2,400,256]{2,1,0:T(8,128)(2,1)S(1)} %pad_maximum_fusion.refs_0_.refs_2_, ...), custom_call_target="tpu_custom_call" | custom-call | tf_op jit(solution)/shard_map/own/pallas_call | solution.py:389
  131.8 4.0 %hand.5 = bf16[24,128,256]{2,1,0:T(8,128)(2,1)} custom-call(s32[4]{0:T(128)} %copy-done.18, s32[2,128]{1,0:T(2,128)} %slice.78.refs_1_, bf16[16,128,256]{2,1,0:T(8,128)(2,1)} %copy-done.3, bf16[16,128,256]{2,1,0:T(8,128)(2,1)} %copy-done.19, bf16[16,128,256]{2,1,0:T(8,128)(2,1)} %copy-done.20, bf16[16,128,256]{2,1,0:T(8,128)(2,1)} %copy-done.21), custom_call_target="tpu_custom_call" | custom-call | tf_op jit(solution)/shard_map/hand/pallas_call | solution.py:409
  135.8 3.1 %collective-permute-done.32.refs_4_.refs_13_ = bf16[16,128,256]{2,1,0:T(8,128)(2,1)} collective-permute-done((bf16[16,128,256]{2,1,0:T(8,128)(2,1)}, bf16[16,128,256]{2,1,0:T(8,128)(2,1)}, u32[]{:S(2)}, u32[]{:S(2)}) %collective-permute-start.32) | collective-permute-done | bytes 1048608 | tf_op jit(solution)/shard_map/ppermute | solution.py:42
  138.9 5.8 %collective-permute-start.39 = (bf16[24,128,256]{2,1,0:T(8,128)(2,1)}, bf16[24,128,256]{2,1,0:T(8,128)(2,1)}, u32[]{:S(2)}, u32[]{:S(2)}) collective-permute-start(bf16[24,128,256]{2,1,0:T(8,128)(2,1)} %hand.5), channel_id=1, source_target_pairs={{0,1},{1,0},{2,3},{3,2},{4,5},{5,4},{6,7},{7,6},{8,9},{9,8},{10,11... | collective-permute-start | bytes 4718600 | tf_op jit(solution)/shard_map/ppermute | solution.py:46
  144.7 20.7 %collective-permute-done.33.refs_5_.refs_14_ = bf16[16,128,256]{2,1,0:T(8,128)(2,1)} collective-permute-done((bf16[16,128,256]{2,1,0:T(8,128)(2,1)}, bf16[16,128,256]{2,1,0:T(8,128)(2,1)}, u32[]{:S(2)}, u32[]{:S(2)}) %collective-permute-start.33) | collective-permute-done | bytes 1048608 | tf_op jit(solution)/shard_map/ppermute | solution.py:42
  165.4 4.3 %hand.4 = bf16[24,128,256]{2,1,0:T(8,128)(2,1)} custom-call(s32[4]{0:T(128)} %copy-done.18, s32[2,128]{1,0:T(2,128)} %slice.78.refs_1_, bf16[16,128,256]{2,1,0:T(8,128)(2,1)} %copy-done.2, bf16[16,128,256]{2,1,0:T(8,128)(2,1)} %copy-done.22, bf16[16,128,256]{2,1,0:T(8,128)(2,1)} %collective-permute-done.32.refs_4_.refs_13_, ...), custom_call_target="tpu_custom_call" | custom-call | tf_op jit(solution)/shard_map/hand/pallas_call | solution.py:409
  171.4 4.1 %hand.3 = bf16[24,128,256]{2,1,0:T(8,128)(2,1)} custom-call(s32[4]{0:T(128)} %copy-done.18, s32[2,128]{1,0:T(2,128)} %slice.78.refs_1_, bf16[16,128,256]{2,1,0:T(8,128)(2,1)} %copy-done.1, bf16[16,128,256]{2,1,0:T(8,128)(2,1)} %collective-permute-done.28.refs_3_.refs_8_, bf16[16,128,256]{2,1,0:T(8,128)(2,1)} %collective-permute-done.29.refs_4_.refs_9_, ...), custom_call_target="tpu_custom_call" | custom-call | tf_op jit(solution)/shard_map/hand/pallas_call | solution.py:409
  179.9 30.4 %attend.1 = bf16[512,768]{1,0:T(8,128)(2,1)} custom-call(s32[4]{0:T(128)} %copy-done.18, s32[2,128]{1,0:T(2,128)} %tables.1.refs_1_, s32[4,2]{1,0:T(4,128)} %copy.9.refs_1_.refs_2_, bf16[4,6,256,128]{3,2,1,0:T(8,128)(2,1)} %copy-done, bf16[768,768]{1,0:T(8,128)(2,1)} %get-tuple-element.20.refs_4_, bf16[768,768]{1,0:T(8,128)(2,1)} %bitcast.23, ...), custom_call_target="tpu_custom_call" | custom-call | tf_op jit(solution)/shard_map/attend/pallas_call | solution.py:418
  (151 shorter events, 49.4 us)
Async XLA Ops:
  18.9 16.6 %collective-permute-start.22 = (bf16[2,400,256]{2,1,0:T(8,128)(2,1)S(1)}, bf16[2,400,256]{2,1,0:T(8,128)(2,1)S(1)}, u32[]{:S(2)}, u32[]{:S(2)}) collective-permute-start(bf16[2,400,256]{2,1,0:T(8,128)(2,1)S(1)} %pad_maximum_fusion.4.refs_16_.refs_2_), channel_id=1, source_target_pairs={{0,2},{2,4},{4,6},{6,0},{8,10},{10,12},{12,14},{14,8},{16,18},{18,... | collective-permute-start | bytes 1228808 | tf_op jit(solution)/shard_map/ppermute | solution.py:42
  20.1 15.6 %collective-permute-start.27 = (bf16[2,400,256]{2,1,0:T(8,128)(2,1)S(1)}, bf16[2,400,256]{2,1,0:T(8,128)(2,1)S(1)}, u32[]{:S(2)}, u32[]{:S(2)}) collective-permute-start(bf16[2,400,256]{2,1,0:T(8,128)(2,1)S(1)} %pad_maximum_fusion.4.refs_16_.refs_2_), channel_id=1, source_target_pairs={{0,6},{2,0},{4,2},{6,4},{8,14},{10,8},{12,10},{14,12},{16,22},{18,... | collective-permute-start | bytes 1228808 | tf_op jit(solution)/shard_map/ppermute | solution.py:42
  23.2 12.9 %collective-permute-start.16 = (bf16[2,400,256]{2,1,0:T(8,128)(2,1)S(1)}, bf16[2,400,256]{2,1,0:T(8,128)(2,1)}, u32[]{:S(2)}, u32[]{:S(2)}) collective-permute-start(bf16[2,400,256]{2,1,0:T(8,128)(2,1)S(1)} %pad_maximum_fusion.2.refs_8_.refs_2_), channel_id=1, source_target_pairs={{0,32},{2,34},{4,36},{6,38},{8,40},{10,42},{12,44},{14,46},{16,48}... | collective-permute-start | bytes 1228808 | tf_op jit(solution)/shard_map/ppermute | solution.py:42
  23.7 13.5 %collective-permute-start.21 = (bf16[2,400,256]{2,1,0:T(8,128)(2,1)S(1)}, bf16[2,400,256]{2,1,0:T(8,128)(2,1)S(1)}, u32[]{:S(2)}, u32[]{:S(2)}) collective-permute-start(bf16[2,400,256]{2,1,0:T(8,128)(2,1)S(1)} %pad_maximum_fusion.2.refs_8_.refs_2_), channel_id=1, source_target_pairs={{0,96},{2,98},{4,100},{6,102},{8,104},{10,106},{12,108},{14,110},{... | collective-permute-start | bytes 1228808 | tf_op jit(solution)/shard_map/ppermute | solution.py:42
  35.5 12.0 %collective-permute-start.23 = (bf16[2,400,256]{2,1,0:T(8,128)(2,1)S(1)}, bf16[2,400,256]{2,1,0:T(8,128)(2,1)S(1)}, u32[]{:S(2)}, u32[]{:S(2)}) collective-permute-start(bf16[2,400,256]{2,1,0:T(8,128)(2,1)S(1)} %pad_maximum_fusion.5.refs_17_.refs_3_), channel_id=1, source_target_pairs={{0,2},{2,4},{4,6},{6,0},{8,10},{10,12},{12,14},{14,8},{16,18},{18,... | collective-permute-start | bytes 1228808 | tf_op jit(solution)/shard_map/ppermute | solution.py:42
  35.7 13.8 %collective-permute-start.19 = (bf16[2,400,256]{2,1,0:T(8,128)(2,1)S(1)}, bf16[2,400,256]{2,1,0:T(8,128)(2,1)}, u32[]{:S(2)}, u32[]{:S(2)}) collective-permute-start(bf16[2,400,256]{2,1,0:T(8,128)(2,1)S(1)} %pad_maximum_fusion.3.refs_9_.refs_3_), channel_id=1, source_target_pairs={{0,96},{2,98},{4,100},{6,102},{8,104},{10,106},{12,108},{14,110},{... | collective-permute-start | bytes 1228808 | tf_op jit(solution)/shard_map/ppermute | solution.py:42
  36.1 14.8 %collective-permute-start.17 = (bf16[2,400,256]{2,1,0:T(8,128)(2,1)S(1)}, bf16[2,400,256]{2,1,0:T(8,128)(2,1)S(1)}, u32[]{:S(2)}, u32[]{:S(2)}) collective-permute-start(bf16[2,400,256]{2,1,0:T(8,128)(2,1)S(1)} %pad_maximum_fusion.3.refs_9_.refs_3_), channel_id=1, source_target_pairs={{0,32},{2,34},{4,36},{6,38},{8,40},{10,42},{12,44},{14,46},{16,48}... | collective-permute-start | bytes 1228808 | tf_op jit(solution)/shard_map/ppermute | solution.py:42
  38.0 18.4 %collective-permute-start.24 = (bf16[2,400,256]{2,1,0:T(8,128)(2,1)S(1)}, bf16[2,400,256]{2,1,0:T(8,128)(2,1)S(1)}, u32[]{:S(2)}, u32[]{:S(2)}) collective-permute-start(bf16[2,400,256]{2,1,0:T(8,128)(2,1)S(1)} %collective-permute-done.22.refs_18_.refs_4_), channel_id=1, source_target_pairs={{0,2},{2,4},{4,6},{6,0},{8,10},{10,12},{12,14},{14,8},{16,18},{18,... | collective-permute-start | bytes 1228808 | tf_op jit(solution)/shard_map/ppermute | solution.py:42
  44.2 12.9 %collective-permute-start.18 = (bf16[2,400,256]{2,1,0:T(8,128)(2,1)}, bf16[2,400,256]{2,1,0:T(8,128)(2,1)S(1)}, u32[]{:S(2)}, u32[]{:S(2)}) collective-permute-start(bf16[2,400,256]{2,1,0:T(8,128)(2,1)} %collective-permute-done.16.refs_10_.refs_4_), channel_id=1, source_target_pairs={{0,32},{2,34},{4,36},{6,38},{8,40},{10,42},{12,44},{14,46},{16,48}... | collective-permute-start | bytes 1228808 | tf_op jit(solution)/shard_map/ppermute | solution.py:42
  48.2 26.9 %collective-permute-start.10 = (bf16[2,400,256]{2,1,0:T(8,128)(2,1)S(1)}, bf16[2,400,256]{2,1,0:T(8,128)(2,1)}, u32[]{:S(2)}, u32[]{:S(2)}) collective-permute-start(bf16[2,400,256]{2,1,0:T(8,128)(2,1)S(1)} %pad_maximum_fusion.refs_0_.refs_2_), channel_id=1, source_target_pairs={{0,8},{2,10},{4,12},{6,14},{8,16},{10,18},{12,20},{14,22},{16,24},... | collective-permute-start | bytes 1228808 | tf_op jit(solution)/shard_map/ppermute | solution.py:42
  49.5 26.1 %collective-permute-start.15 = (bf16[2,400,256]{2,1,0:T(8,128)(2,1)S(1)}, bf16[2,400,256]{2,1,0:T(8,128)(2,1)}, u32[]{:S(2)}, u32[]{:S(2)}) collective-permute-start(bf16[2,400,256]{2,1,0:T(8,128)(2,1)S(1)} %pad_maximum_fusion.refs_0_.refs_2_), channel_id=1, source_target_pairs={{0,24},{2,26},{4,28},{6,30},{8,0},{10,2},{12,4},{14,6},{16,8},{18,... | collective-permute-start | bytes 1228808 | tf_op jit(solution)/shard_map/ppermute | solution.py:42
  51.7 26.2 %collective-permute-start.13 = (bf16[2,400,256]{2,1,0:T(8,128)(2,1)S(1)}, bf16[2,400,256]{2,1,0:T(8,128)(2,1)}, u32[]{:S(2)}, u32[]{:S(2)}) collective-permute-start(bf16[2,400,256]{2,1,0:T(8,128)(2,1)S(1)} %pad_maximum_fusion.1.refs_1_.refs_3_), channel_id=1, source_target_pairs={{0,24},{2,26},{4,28},{6,30},{8,0},{10,2},{12,4},{14,6},{16,8},{18,... | collective-permute-start | bytes 1228808 | tf_op jit(solution)/shard_map/ppermute | solution.py:42
  57.9 14.1 %collective-permute-start.20 = (bf16[2,400,256]{2,1,0:T(8,128)(2,1)}, bf16[2,400,256]{2,1,0:T(8,128)(2,1)}, u32[]{:S(2)}, u32[]{:S(2)}) collective-permute-start(bf16[2,400,256]{2,1,0:T(8,128)(2,1)} %collective-permute-done.19.refs_15_.refs_9_), channel_id=1, source_target_pairs={{0,96},{2,98},{4,100},{6,102},{8,104},{10,106},{12,108},{14,110},{... | collective-permute-start | bytes 1228808 | tf_op jit(solution)/shard_map/ppermute | solution.py:42
  72.0 48.7 %collective-permute-start.34 = (bf16[16,128,256]{2,1,0:T(8,128)(2,1)S(1)}, bf16[16,128,256]{2,1,0:T(8,128)(2,1)S(1)}, u32[]{:S(2)}, u32[]{:S(2)}) collective-permute-start(bf16[16,128,256]{2,1,0:T(8,128)(2,1)S(1)} %get-tuple-element.32), channel_id=1, source_target_pairs={{0,32},{2,34},{4,36},{6,38},{8,40},{10,42},{12,44},{14,46},{16,48}... | collective-permute-start | bytes 3145736 | tf_op jit(solution)/shard_map/ppermute | solution.py:42
  75.2 47.5 %collective-permute-start.35 = (bf16[16,128,256]{2,1,0:T(8,128)(2,1)S(1)}, bf16[16,128,256]{2,1,0:T(8,128)(2,1)S(1)}, u32[]{:S(2)}, u32[]{:S(2)}) collective-permute-start(bf16[16,128,256]{2,1,0:T(8,128)(2,1)S(1)} %get-tuple-element.33), channel_id=1, source_target_pairs={{0,64},{2,66},{4,68},{6,70},{8,72},{10,74},{12,76},{14,78},{16,80}... | collective-permute-start | bytes 3145736 | tf_op jit(solution)/shard_map/ppermute | solution.py:42
  75.6 47.4 %collective-permute-start.36 = (bf16[16,128,256]{2,1,0:T(8,128)(2,1)S(1)}, bf16[16,128,256]{2,1,0:T(8,128)(2,1)S(1)}, u32[]{:S(2)}, u32[]{:S(2)}) collective-permute-start(bf16[16,128,256]{2,1,0:T(8,128)(2,1)S(1)} %get-tuple-element.34), channel_id=1, source_target_pairs={{0,96},{2,98},{4,100},{6,102},{8,104},{10,106},{12,108},{14,110},{... | collective-permute-start | bytes 3145736 | tf_op jit(solution)/shard_map/ppermute | solution.py:42
  77.9 48.1 %collective-permute-start.31 = (bf16[16,128,256]{2,1,0:T(8,128)(2,1)S(1)}, bf16[16,128,256]{2,1,0:T(8,128)(2,1)S(1)}, u32[]{:S(2)}, u32[]{:S(2)}) collective-permute-start(bf16[16,128,256]{2,1,0:T(8,128)(2,1)S(1)} %get-tuple-element.28), channel_id=1, source_target_pairs={{0,8},{2,10},{4,12},{6,14},{8,16},{10,18},{12,20},{14,22},{16,24},... | collective-permute-start | bytes 3145736 | tf_op jit(solution)/shard_map/ppermute | solution.py:42
  78.9 30.8 %collective-permute-start.12 = (bf16[2,400,256]{2,1,0:T(8,128)(2,1)}, bf16[2,400,256]{2,1,0:T(8,128)(2,1)S(1)}, u32[]{:S(2)}, u32[]{:S(2)}) collective-permute-start(bf16[2,400,256]{2,1,0:T(8,128)(2,1)} %collective-permute-done.10.refs_2_.refs_4_), channel_id=1, source_target_pairs={{0,8},{2,10},{4,12},{6,14},{8,16},{10,18},{12,20},{14,22},{16,24},... | collective-permute-start | bytes 1228808 | tf_op jit(solution)/shard_map/ppermute | solution.py:42
  117.3 21.6 %collective-permute-start.32 = (bf16[16,128,256]{2,1,0:T(8,128)(2,1)}, bf16[16,128,256]{2,1,0:T(8,128)(2,1)}, u32[]{:S(2)}, u32[]{:S(2)}) collective-permute-start(bf16[16,128,256]{2,1,0:T(8,128)(2,1)} %get-tuple-element.29), channel_id=1, source_target_pairs={{0,16},{2,18},{4,20},{6,22},{8,24},{10,26},{12,28},{14,30},{16,0},... | collective-permute-start | bytes 3145736 | tf_op jit(solution)/shard_map/ppermute | solution.py:42
  120.7 44.6 %collective-permute-start.33 = (bf16[16,128,256]{2,1,0:T(8,128)(2,1)}, bf16[16,128,256]{2,1,0:T(8,128)(2,1)}, u32[]{:S(2)}, u32[]{:S(2)}) collective-permute-start(bf16[16,128,256]{2,1,0:T(8,128)(2,1)} %get-tuple-element.30), channel_id=1, source_target_pairs={{0,24},{2,26},{4,28},{6,30},{8,0},{10,2},{12,4},{14,6},{16,8},{18,... | collective-permute-start | bytes 3145736 | tf_op jit(solution)/shard_map/ppermute | solution.py:42
  122.7 47.7 %collective-permute-start.28 = (bf16[16,128,256]{2,1,0:T(8,128)(2,1)}, bf16[16,128,256]{2,1,0:T(8,128)(2,1)}, u32[]{:S(2)}, u32[]{:S(2)}) collective-permute-start(bf16[16,128,256]{2,1,0:T(8,128)(2,1)} %get-tuple-element.24), channel_id=1, source_target_pairs={{0,2},{2,4},{4,6},{6,0},{8,10},{10,12},{12,14},{14,8},{16,18},{18,... | collective-permute-start | bytes 3145736 | tf_op jit(solution)/shard_map/ppermute | solution.py:42
  123.0 47.4 %collective-permute-start.29 = (bf16[16,128,256]{2,1,0:T(8,128)(2,1)}, bf16[16,128,256]{2,1,0:T(8,128)(2,1)}, u32[]{:S(2)}, u32[]{:S(2)}) collective-permute-start(bf16[16,128,256]{2,1,0:T(8,128)(2,1)} %get-tuple-element.25), channel_id=1, source_target_pairs={{0,4},{2,6},{4,0},{6,2},{8,12},{10,14},{12,8},{14,10},{16,20},{18,... | collective-permute-start | bytes 3145736 | tf_op jit(solution)/shard_map/ppermute | solution.py:42
  126.0 45.4 %collective-permute-start.30 = (bf16[16,128,256]{2,1,0:T(8,128)(2,1)}, bf16[16,128,256]{2,1,0:T(8,128)(2,1)}, u32[]{:S(2)}, u32[]{:S(2)}) collective-permute-start(bf16[16,128,256]{2,1,0:T(8,128)(2,1)} %get-tuple-element.26), channel_id=1, source_target_pairs={{0,6},{2,0},{4,2},{6,4},{8,14},{10,8},{12,10},{14,12},{16,22},{18,... | collective-permute-start | bytes 3145736 | tf_op jit(solution)/shard_map/ppermute | solution.py:42
  138.9 39.6 %collective-permute-start.39 = (bf16[24,128,256]{2,1,0:T(8,128)(2,1)}, bf16[24,128,256]{2,1,0:T(8,128)(2,1)}, u32[]{:S(2)}, u32[]{:S(2)}) collective-permute-start(bf16[24,128,256]{2,1,0:T(8,128)(2,1)} %hand.5), channel_id=1, source_target_pairs={{0,1},{1,0},{2,3},{3,2},{4,5},{5,4},{6,7},{7,6},{8,9},{9,8},{10,11... | collective-permute-start | bytes 4718600 | tf_op jit(solution)/shard_map/ppermute | solution.py:46
  (45 other events, 315.5 us)

commit v2 on v0

--- a/solution.py
+++ b/solution.py
@@ -90,6 +90,26 @@
                 which = table_ref[0 if d == 0 else 3 * part + d, place]
                 begin = pl.multiple_of(jnp.maximum(which - 1, 0) * BLK, BLK)
                 out[d2 * 4 + d1] = line[row, pl.ds(begin, BLK), :]
+
+
+def note_kernel(table_ref, *refs):
+    out = refs[-1]
+    tall = PARTS * BLK
+    source = {first: part for part, (_, first, _) in enumerate(ROUTES)}
+    out[...] = jnp.zeros_like(out)
+    out[0:1, :] = table_ref[0:1, :]
+    for part, (across, _, _) in enumerate(ROUTES):
+        for d in range(1, SIDE):
+            place = source[across] * SIDE + SIDE - d
+            note = refs[place // 2][place % 2, tall : tall + 16, :128]
+            row = part * 3 + d
+            out[row : row + 1, :] = note.astype(F32).astype(I32)[0:1, :]
+    out[10:11, :] = table_ref[1:2, :]
+
+
+def weight_kernel(w_ref, keys_ref, values_ref):
+    keys_ref[...] = w_ref[:, :WIDTH]
+    values_ref[...] = jnp.transpose(w_ref[:, WIDTH:])
 
 
 def select_kernel(part, me_ref, table_ref, *refs):
@@ -342,29 +362,27 @@
     )(neighbours, counts, slab_map)
     note = jnp.pad(table[:1].astype(BF), ((0, 15), (0, CUT - 128)))
     tall = PARTS * BLK
-    heard = []
     lines = []
     for part, (_, axis, _) in enumerate(ROUTES):
         own = source_tokens[:, :, part * CUT : (part + 1) * CUT].reshape(tall, CUT)
         own = jnp.concatenate([own, note])
         right, left = shift(own, axis, 1), shift(own, axis, -1)
         told = [own, right, shift(right, axis, 1), left]
-        heard.append([t[tall, :128].astype(I32) for t in told])
         lines.append((jnp.stack(told[:2]), jnp.stack(told[2:])))
-    source = {first: part for part, (_, first, _) in enumerate(ROUTES)}
-    rows = [table[0]]
-    for across, _, _ in ROUTES:
-        rows += [heard[source[across]][SIDE - d] for d in range(1, SIDE)]
-    wishes = jnp.stack(rows + [table[1]])
+    small = pltpu.CompilerParams(vmem_limit_bytes=SELECT_VMEM)
+    wishes = pl.pallas_call(
+        note_kernel,
+        out_shape=jax.ShapeDtypeStruct((16, 128), I32),
+        in_specs=[VMEM] * 7,
+        out_specs=VMEM,
+        compiler_params=small,
+        name="notes",
+    )(table, *[half for line in lines for half in line])
     partner = swap(wishes)
     wishes = wishes + partner
-    partner = partner[9:]
-
-    w_keys = w_keyval[:, :WIDTH]
-    w_values = jnp.transpose(w_keyval[:, WIDTH:])
-    wishes, w_keys, w_values = lax.optimization_barrier((wishes, w_keys, w_values))
+    partner = partner[9:11]
+
     slots = jax.ShapeDtypeStruct((SIDE * SIDE, BLK, CUT), BF)
-    small = pltpu.CompilerParams(vmem_limit_bytes=SELECT_VMEM)
     gathered = []
     arrived = []
     for part, (across, _, axis) in enumerate(ROUTES):
@@ -397,6 +415,14 @@
         compiler_params=small,
         name="spread",
     )(query_tokens, w_query)
+    w_keys, w_values = pl.pallas_call(
+        weight_kernel,
+        out_shape=[jax.ShapeDtypeStruct((WIDTH, WIDTH), BF)] * 2,
+        in_specs=[VMEM],
+        out_specs=[VMEM] * 2,
+        compiler_params=small,
+        name="weights",
+    )(w_keyval)
     arrived = [[own_slots[part]] + arrived[part] for part in range(PARTS)]
     items = blocks * -(-2 * CAP // GROUP)
     handed = []

time: 232 us -> 219 us (0.944)
  waiting for transfers between devices: 103 us -> 86 us
  starting transfers between devices: 46.7 us -> 54.6 us
  other arithmetic: 4.29 us -> 1.08 us
    ppermute x36, waiting for transfers between devices: 102 us -> 86 us  [shift(): return lax.ppermute(value, 'pb', pairs)]
    ppermute x36, starting transfers between devices: 34.2 us -> 43.7 us  [shift(): return lax.ppermute(value, 'pb', pairs)]
    another operation x7, other arithmetic: 3.46 us -> 0.33 us  [on_device(): lines.append((jnp.stack(told[:2]), jnp.stack(told[2:])))]
    unnamed x74 -> x71, local copies, waits for them, and re-layouts: 16.9 us -> 18.2 us
  transfers between devices with their start and end apart: 40 -> 40, of which waited for: 16 -> 13; matrix products, arithmetic and copies ran while one was open for 4% -> 0% of each run, Pallas kernels for 9% -> 10%
where the time goes in v2:
time: 219 us; the launch traced here: 217 us
  waiting for transfers between devices  86 us (39%)
  Pallas kernels  55 us (25%)
  starting transfers between devices  54.6 us (25%)
  local copies, waits for them, and re-layouts  19.9 us (9%)
    ppermute x36, waiting for transfers between devices, shift(): return lax.ppermute(value, 'pb', pairs)  86 us
    ppermute x36, starting transfers between devices, shift(): return lax.ppermute(value, 'pb', pairs)  43.7 us
    pallas_call x1, Pallas kernels, on_device(): pl.pallas_call(lambda *refs: attend_kernel(True, True, *refs), out_shape=...  30.5 us
    unnamed x71, local copies, waits for them, and re-layouts  18.2 us
    pallas_call x3, Pallas kernels, on_device(): pl.pallas_call(lambda *refs: hand_kernel(part, *refs), out_shape=jax.Shap...  12.4 us
    ppermute x4, starting transfers between devices, swap(): return lax.ppermute(value, 'ka', [(0, 1), (1, 0)])  10.8 us
    pallas_call x3, Pallas kernels, on_device(): pl.pallas_call(lambda *refs: select_kernel(part, *refs), out_shape=[slots...  6.79 us
  transfers between devices with their start and end apart: 40, of which 13 were waited for; matrix products, arithmetic and copies ran while one was open for 0% of the time, Pallas kernels for 10%

profile of v2, /device:TPU:1, one launch (start us, length us, event | category | flops | bytes accessed | tf_op | source)
XLA Modules:
  0.0 217.1 jit_solution(9936341268636988115)
XLA Ops:
  1.3 2.3 %tables.1.table_ref.refs_1_ = s32[2,128]{1,0:T(2,128)} custom-call(s32[4,2,6]{2,1,0:T(2,128)} %refs_0_.1, s32[4,2]{1,0:T(4,128)} %copy.9.refs_1_.refs_2_, s32[3,128]{1,0:T(4,128)} %refs_2_.2), custom_call_target="tpu_custom_call" | custom-call | tf_op jit(solution)/shard_map/tables/pallas_call | solution.py:356
  14.2 2.2 collective-permute-start.8
  19.5 4.3 %collective-permute-done.1 = bf16[400,256]{1,0:T(8,128)(2,1)S(1)} collective-permute-done((bf16[400,256]{1,0:T(8,128)(2,1)S(1)}, bf16[400,256]{1,0:T(8,128)(2,1)S(1)}, u32[]{:S(2)}, u32[]{:S(2)}) %collective-permute-start.1) | collective-permute-done | bytes 204832 | tf_op jit(solution)/shard_map/ppermute | solution.py:42
  24.7 5.2 %collective-permute-done.7 = bf16[400,256]{1,0:T(8,128)(2,1)S(1)} collective-permute-done((bf16[400,256]{1,0:T(8,128)(2,1)S(1)}, bf16[400,256]{1,0:T(8,128)(2,1)S(1)}, u32[]{:S(2)}, u32[]{:S(2)}) %collective-permute-start.7) | collective-permute-done | bytes 204832 | tf_op jit(solution)/shard_map/ppermute | solution.py:42
  30.0 3.5 %collective-permute-start.9 = (s32[16,128]{1,0:T(8,128)S(1)}, s32[16,128]{1,0:T(8,128)S(1)}, u32[]{:S(2)}, u32[]{:S(2)}) collective-permute-start(s32[16,128]{1,0:T(8,128)S(1)} %notes.1), channel_id=1, source_target_pairs={{0,1},{1,0},{2,3},{3,2},{4,5},{5,4},{6,7},{7,6},{8,9},{9,8},{10,11... | collective-permute-start | bytes 24584 | tf_op jit(solution)/shard_map/ppermute | solution.py:46
  33.5 2.7 %collective-permute-start.27 = (bf16[2,400,256]{2,1,0:T(8,128)(2,1)S(1)}, bf16[2,400,256]{2,1,0:T(8,128)(2,1)S(1)}, u32[]{:S(2)}, u32[]{:S(2)}) collective-permute-start(bf16[2,400,256]{2,1,0:T(8,128)(2,1)S(1)} %pad_maximum_fusion.4.refs_4_.refs_16_.refs_2_), channel_id=1, source_target_pairs={{0,6},{2,0},{4,2},{6,4},{8,14},{10,8},{12,10},{14,12},{16,22},{18,... | collective-permute-start | bytes 1228808 | tf_op jit(solution)/shard_map/ppermute | solution.py:42
  36.1 2.7 %collective-permute-start.21 = (bf16[2,400,256]{2,1,0:T(8,128)(2,1)S(1)}, bf16[2,400,256]{2,1,0:T(8,128)(2,1)S(1)}, u32[]{:S(2)}, u32[]{:S(2)}) collective-permute-start(bf16[2,400,256]{2,1,0:T(8,128)(2,1)S(1)} %pad_maximum_fusion.2.refs_2_.refs_8_), channel_id=1, source_target_pairs={{0,96},{2,98},{4,100},{6,102},{8,104},{10,106},{12,108},{14,110},{... | collective-permute-start | bytes 1228808 | tf_op jit(solution)/shard_map/ppermute | solution.py:42
  40.3 4.6 %collective-permute-done.27.refs_22_.refs_8_ = bf16[2,400,256]{2,1,0:T(8,128)(2,1)S(1)} collective-permute-done((bf16[2,400,256]{2,1,0:T(8,128)(2,1)S(1)}, bf16[2,400,256]{2,1,0:T(8,128)(2,1)S(1)}, u32[]{:S(2)}, u32[]{:S(2)}) %collective-permute-start.27) | collective-permute-done | bytes 409632 | tf_op jit(solution)/shard_map/ppermute | solution.py:42
  48.8 4.9 %collective-permute-done.25.refs_23_.refs_9_ = bf16[2,400,256]{2,1,0:T(8,128)(2,1)S(1)} collective-permute-done((bf16[2,400,256]{2,1,0:T(8,128)(2,1)S(1)}, bf16[2,400,256]{2,1,0:T(8,128)(2,1)S(1)}, u32[]{:S(2)}, u32[]{:S(2)}) %collective-permute-start.25) | collective-permute-done | bytes 409632 | tf_op jit(solution)/shard_map/ppermute | solution.py:42
  55.2 3.4 %collective-permute-start.26 = (bf16[2,400,256]{2,1,0:T(8,128)(2,1)S(1)}, bf16[2,400,256]{2,1,0:T(8,128)(2,1)S(1)}, u32[]{:S(2)}, u32[]{:S(2)}) collective-permute-start(bf16[2,400,256]{2,1,0:T(8,128)(2,1)S(1)} %collective-permute-done.25.refs_23_.refs_9_), channel_id=1, source_target_pairs={{0,6},{2,0},{4,2},{6,4},{8,14},{10,8},{12,10},{14,12},{16,22},{18,... | collective-permute-start | bytes 1228808 | tf_op jit(solution)/shard_map/ppermute | solution.py:42
  59.4 2.7 %collective-permute-start.20 = (bf16[2,400,256]{2,1,0:T(8,128)(2,1)}, bf16[2,400,256]{2,1,0:T(8,128)(2,1)}, u32[]{:S(2)}, u32[]{:S(2)}) collective-permute-start(bf16[2,400,256]{2,1,0:T(8,128)(2,1)} %collective-permute-done.19.refs_15_.refs_9_), channel_id=1, source_target_pairs={{0,96},{2,98},{4,100},{6,102},{8,104},{10,106},{12,108},{14,110},{... | collective-permute-start | bytes 1228808 | tf_op jit(solution)/shard_map/ppermute | solution.py:42
  63.6 2.7 %collective-permute-start.15 = (bf16[2,400,256]{2,1,0:T(8,128)(2,1)S(1)}, bf16[2,400,256]{2,1,0:T(8,128)(2,1)}, u32[]{:S(2)}, u32[]{:S(2)}) collective-permute-start(bf16[2,400,256]{2,1,0:T(8,128)(2,1)S(1)} %pad_maximum_fusion.refs_0_.refs_2_), channel_id=1, source_target_pairs={{0,24},{2,26},{4,28},{6,30},{8,0},{10,2},{12,4},{14,6},{16,8},{18,... | collective-permute-start | bytes 1228808 | tf_op jit(solution)/shard_map/ppermute | solution.py:42
  76.3 2.6 %select.31 = (bf16[16,128,256]{2,1,0:T(8,128)(2,1)S(1)}, bf16[16,128,256]{2,1,0:T(8,128)(2,1)}, bf16[16,128,256]{2,1,0:T(8,128)(2,1)}) custom-call(s32[4]{0:T(128)S(1)} %pad_add_fusion.me_ref.refs_0_, s32[16,128]{1,0:T(8,128)S(1)} %add.16.table_ref.refs_1_, bf16[2,400,256]{2,1,0:T(8,128)(2,1)S(1)} %pad_maximum_fusion.2.refs_2_.refs_8_, ...), custom_call_target="tpu_custom_call" | custom-call | tf_op jit(solution)/shard_map/select/pallas_call | solution.py:393
  79.1 2.3 %collective-permute-start.36 = (bf16[16,128,256]{2,1,0:T(8,128)(2,1)S(1)}, bf16[16,128,256]{2,1,0:T(8,128)(2,1)S(1)}, u32[]{:S(2)}, u32[]{:S(2)}) collective-permute-start(bf16[16,128,256]{2,1,0:T(8,128)(2,1)S(1)} %get-tuple-element.32), channel_id=1, source_target_pairs={{0,96},{2,98},{4,100},{6,102},{8,104},{10,106},{12,108},{14,110},{... | collective-permute-start | bytes 3145736 | tf_op jit(solution)/shard_map/ppermute | solution.py:42
  83.8 30.9 %collective-permute-done.12.refs_4_.refs_6_ = bf16[2,400,256]{2,1,0:T(8,128)(2,1)S(1)} collective-permute-done((bf16[2,400,256]{2,1,0:T(8,128)(2,1)}, bf16[2,400,256]{2,1,0:T(8,128)(2,1)S(1)}, u32[]{:S(2)}, u32[]{:S(2)}) %collective-permute-start.12) | collective-permute-done | bytes 409632 | tf_op jit(solution)/shard_map/ppermute | solution.py:42
  115.9 6.6 %collective-permute-done.14.refs_5_.refs_7_ = bf16[2,400,256]{2,1,0:T(8,128)(2,1)S(1)} collective-permute-done((bf16[2,400,256]{2,1,0:T(8,128)(2,1)}, bf16[2,400,256]{2,1,0:T(8,128)(2,1)S(1)}, u32[]{:S(2)}, u32[]{:S(2)}) %collective-permute-start.14) | collective-permute-done | bytes 409632 | tf_op jit(solution)/shard_map/ppermute | solution.py:42
  123.5 3.3 %select.30 = (bf16[16,128,256]{2,1,0:T(8,128)(2,1)}, bf16[16,128,256]{2,1,0:T(8,128)(2,1)}, bf16[16,128,256]{2,1,0:T(8,128)(2,1)}) custom-call(s32[4]{0:T(128)S(1)} %pad_add_fusion.me_ref.refs_0_, s32[16,128]{1,0:T(8,128)S(1)} %add.16.table_ref.refs_1_, bf16[2,400,256]{2,1,0:T(8,128)(2,1)S(1)} %pad_maximum_fusion.refs_0_.refs_2_, ...), custom_call_target="tpu_custom_call" | custom-call | tf_op jit(solution)/shard_map/select/pallas_call | solution.py:393
  136.4 4.0 %hand.5 = bf16[24,128,256]{2,1,0:T(8,128)(2,1)} custom-call(s32[4]{0:T(128)} %copy-done.29, s32[2,128]{1,0:T(2,128)} %slice.21.refs_1_, bf16[16,128,256]{2,1,0:T(8,128)(2,1)} %copy-done.3, bf16[16,128,256]{2,1,0:T(8,128)(2,1)} %copy-done.31, bf16[16,128,256]{2,1,0:T(8,128)(2,1)} %copy-done.32, bf16[16,128,256]{2,1,0:T(8,128)(2,1)} %copy-done.33), custom_call_target="tpu_custom_call" | custom-call | tf_op jit(solution)/shard_map/hand/pallas_call | solution.py:430
  140.4 4.3 %collective-permute-done.32.refs_4_.refs_13_ = bf16[16,128,256]{2,1,0:T(8,128)(2,1)} collective-permute-done((bf16[16,128,256]{2,1,0:T(8,128)(2,1)}, bf16[16,128,256]{2,1,0:T(8,128)(2,1)}, u32[]{:S(2)}, u32[]{:S(2)}) %collective-permute-start.32) | collective-permute-done | bytes 1048608 | tf_op jit(solution)/shard_map/ppermute | solution.py:42
  144.8 5.2 %collective-permute-start.39 = (bf16[24,128,256]{2,1,0:T(8,128)(2,1)}, bf16[24,128,256]{2,1,0:T(8,128)(2,1)}, u32[]{:S(2)}, u32[]{:S(2)}) collective-permute-start(bf16[24,128,256]{2,1,0:T(8,128)(2,1)} %hand.5), channel_id=1, source_target_pairs={{0,1},{1,0},{2,3},{3,2},{4,5},{5,4},{6,7},{7,6},{8,9},{9,8},{10,11... | collective-permute-start | bytes 4718600 | tf_op jit(solution)/shard_map/ppermute | solution.py:46
  150.0 20.7 %collective-permute-done.33.refs_5_.refs_14_ = bf16[16,128,256]{2,1,0:T(8,128)(2,1)} collective-permute-done((bf16[16,128,256]{2,1,0:T(8,128)(2,1)}, bf16[16,128,256]{2,1,0:T(8,128)(2,1)}, u32[]{:S(2)}, u32[]{:S(2)}) %collective-permute-start.33) | collective-permute-done | bytes 1048608 | tf_op jit(solution)/shard_map/ppermute | solution.py:42
  170.6 4.4 %hand.4 = bf16[24,128,256]{2,1,0:T(8,128)(2,1)} custom-call(s32[4]{0:T(128)} %copy-done.29, s32[2,128]{1,0:T(2,128)} %slice.21.refs_1_, bf16[16,128,256]{2,1,0:T(8,128)(2,1)} %copy-done.2, bf16[16,128,256]{2,1,0:T(8,128)(2,1)} %copy-done.34, bf16[16,128,256]{2,1,0:T(8,128)(2,1)} %collective-permute-done.32.refs_4_.refs_13_, ...), custom_call_target="tpu_custom_call" | custom-call | tf_op jit(solution)/shard_map/hand/pallas_call | solution.py:430
  176.4 4.0 %hand.3 = bf16[24,128,256]{2,1,0:T(8,128)(2,1)} custom-call(s32[4]{0:T(128)} %copy-done.29, s32[2,128]{1,0:T(2,128)} %slice.21.refs_1_, bf16[16,128,256]{2,1,0:T(8,128)(2,1)} %copy-done.1, bf16[16,128,256]{2,1,0:T(8,128)(2,1)} %collective-permute-done.28.refs_3_.refs_8_, bf16[16,128,256]{2,1,0:T(8,128)(2,1)} %collective-permute-done.29.refs_4_.refs_9_, ...), custom_call_target="tpu_custom_call" | custom-call | tf_op jit(solution)/shard_map/hand/pallas_call | solution.py:430
  186.5 30.5 %attend.1 = bf16[512,768]{1,0:T(8,128)(2,1)} custom-call(s32[4]{0:T(128)} %copy-done.29, s32[2,128]{1,0:T(2,128)} %tables.1.table_ref.refs_1_, s32[4,2]{1,0:T(4,128)} %copy.9.refs_1_.refs_2_, bf16[4,6,256,128]{3,2,1,0:T(8,128)(2,1)} %copy-done, bf16[768,768]{1,0:T(8,128)(2,1)} %copy-done.26, bf16[768,768]{1,0:T(8,128)(2,1)} %copy-done.27, ...), custom_call_target="tpu_custom_call" | custom-call | tf_op jit(solution)/shard_map/attend/pallas_call | solution.py:439
  (151 shorter events, 56.9 us)
Async XLA Ops:
  18.3 20.6 %collective-permute-start.22 = (bf16[2,400,256]{2,1,0:T(8,128)(2,1)S(1)}, bf16[2,400,256]{2,1,0:T(8,128)(2,1)S(1)}, u32[]{:S(2)}, u32[]{:S(2)}) collective-permute-start(bf16[2,400,256]{2,1,0:T(8,128)(2,1)S(1)} %pad_maximum_fusion.4.refs_4_.refs_16_.refs_2_), channel_id=1, source_target_pairs={{0,2},{2,4},{4,6},{6,0},{8,10},{10,12},{12,14},{14,8},{16,18},{18,... | collective-permute-start | bytes 1228808 | tf_op jit(solution)/shard_map/ppermute | solution.py:42
  38.8 14.8 %collective-permute-start.25 = (bf16[2,400,256]{2,1,0:T(8,128)(2,1)S(1)}, bf16[2,400,256]{2,1,0:T(8,128)(2,1)S(1)}, u32[]{:S(2)}, u32[]{:S(2)}) collective-permute-start(bf16[2,400,256]{2,1,0:T(8,128)(2,1)S(1)} %pad_maximum_fusion.5.refs_5_.refs_17_.refs_3_), channel_id=1, source_target_pairs={{0,6},{2,0},{4,2},{6,4},{8,14},{10,8},{12,10},{14,12},{16,22},{18,... | collective-permute-start | bytes 1228808 | tf_op jit(solution)/shard_map/ppermute | solution.py:42
  38.9 15.5 %collective-permute-start.23 = (bf16[2,400,256]{2,1,0:T(8,128)(2,1)S(1)}, bf16[2,400,256]{2,1,0:T(8,128)(2,1)S(1)}, u32[]{:S(2)}, u32[]{:S(2)}) collective-permute-start(bf16[2,400,256]{2,1,0:T(8,128)(2,1)S(1)} %pad_maximum_fusion.5.refs_5_.refs_17_.refs_3_), channel_id=1, source_target_pairs={{0,2},{2,4},{4,6},{6,0},{8,10},{10,12},{12,14},{14,8},{16,18},{18,... | collective-permute-start | bytes 1228808 | tf_op jit(solution)/shard_map/ppermute | solution.py:42
  44.9 14.5 %collective-permute-start.19 = (bf16[2,400,256]{2,1,0:T(8,128)(2,1)S(1)}, bf16[2,400,256]{2,1,0:T(8,128)(2,1)}, u32[]{:S(2)}, u32[]{:S(2)}) collective-permute-start(bf16[2,400,256]{2,1,0:T(8,128)(2,1)S(1)} %pad_maximum_fusion.3.refs_3_.refs_9_), channel_id=1, source_target_pairs={{0,96},{2,98},{4,100},{6,102},{8,104},{10,106},{12,108},{14,110},{... | collective-permute-start | bytes 1228808 | tf_op jit(solution)/shard_map/ppermute | solution.py:42
  48.0 14.1 %collective-permute-start.17 = (bf16[2,400,256]{2,1,0:T(8,128)(2,1)S(1)}, bf16[2,400,256]{2,1,0:T(8,128)(2,1)S(1)}, u32[]{:S(2)}, u32[]{:S(2)}) collective-permute-start(bf16[2,400,256]{2,1,0:T(8,128)(2,1)S(1)} %pad_maximum_fusion.3.refs_3_.refs_9_), channel_id=1, source_target_pairs={{0,32},{2,34},{4,36},{6,38},{8,40},{10,42},{12,44},{14,46},{16,48}... | collective-permute-start | bytes 1228808 | tf_op jit(solution)/shard_map/ppermute | solution.py:42
  48.8 14.0 %collective-permute-start.24 = (bf16[2,400,256]{2,1,0:T(8,128)(2,1)S(1)}, bf16[2,400,256]{2,1,0:T(8,128)(2,1)S(1)}, u32[]{:S(2)}, u32[]{:S(2)}) collective-permute-start(bf16[2,400,256]{2,1,0:T(8,128)(2,1)S(1)} %collective-permute-done.22.refs_18_.refs_4_), channel_id=1, source_target_pairs={{0,2},{2,4},{4,6},{6,0},{8,10},{10,12},{12,14},{14,8},{16,18},{18,... | collective-permute-start | bytes 1228808 | tf_op jit(solution)/shard_map/ppermute | solution.py:42
  53.7 14.1 %collective-permute-start.18 = (bf16[2,400,256]{2,1,0:T(8,128)(2,1)S(1)}, bf16[2,400,256]{2,1,0:T(8,128)(2,1)S(1)}, u32[]{:S(2)}, u32[]{:S(2)}) collective-permute-start(bf16[2,400,256]{2,1,0:T(8,128)(2,1)S(1)} %collective-permute-done.16.refs_10_.refs_4_), channel_id=1, source_target_pairs={{0,32},{2,34},{4,36},{6,38},{8,40},{10,42},{12,44},{14,46},{16,48}... | collective-permute-start | bytes 1228808 | tf_op jit(solution)/shard_map/ppermute | solution.py:42
  55.2 13.4 %collective-permute-start.26 = (bf16[2,400,256]{2,1,0:T(8,128)(2,1)S(1)}, bf16[2,400,256]{2,1,0:T(8,128)(2,1)S(1)}, u32[]{:S(2)}, u32[]{:S(2)}) collective-permute-start(bf16[2,400,256]{2,1,0:T(8,128)(2,1)S(1)} %collective-permute-done.25.refs_23_.refs_9_), channel_id=1, source_target_pairs={{0,6},{2,0},{4,2},{6,4},{8,14},{10,8},{12,10},{14,12},{16,22},{18,... | collective-permute-start | bytes 1228808 | tf_op jit(solution)/shard_map/ppermute | solution.py:42
  59.4 16.4 %collective-permute-start.20 = (bf16[2,400,256]{2,1,0:T(8,128)(2,1)}, bf16[2,400,256]{2,1,0:T(8,128)(2,1)}, u32[]{:S(2)}, u32[]{:S(2)}) collective-permute-start(bf16[2,400,256]{2,1,0:T(8,128)(2,1)} %collective-permute-done.19.refs_15_.refs_9_), channel_id=1, source_target_pairs={{0,96},{2,98},{4,100},{6,102},{8,104},{10,106},{12,108},{14,110},{... | collective-permute-start | bytes 1228808 | tf_op jit(solution)/shard_map/ppermute | solution.py:42
  62.8 16.1 %collective-permute-start.10 = (bf16[2,400,256]{2,1,0:T(8,128)(2,1)S(1)}, bf16[2,400,256]{2,1,0:T(8,128)(2,1)}, u32[]{:S(2)}, u32[]{:S(2)}) collective-permute-start(bf16[2,400,256]{2,1,0:T(8,128)(2,1)S(1)} %pad_maximum_fusion.refs_0_.refs_2_), channel_id=1, source_target_pairs={{0,8},{2,10},{4,12},{6,14},{8,16},{10,18},{12,20},{14,22},{16,24},... | collective-permute-start | bytes 1228808 | tf_op jit(solution)/shard_map/ppermute | solution.py:42
  63.6 15.5 %collective-permute-start.15 = (bf16[2,400,256]{2,1,0:T(8,128)(2,1)S(1)}, bf16[2,400,256]{2,1,0:T(8,128)(2,1)}, u32[]{:S(2)}, u32[]{:S(2)}) collective-permute-start(bf16[2,400,256]{2,1,0:T(8,128)(2,1)S(1)} %pad_maximum_fusion.refs_0_.refs_2_), channel_id=1, source_target_pairs={{0,24},{2,26},{4,28},{6,30},{8,0},{10,2},{12,4},{14,6},{16,8},{18,... | collective-permute-start | bytes 1228808 | tf_op jit(solution)/shard_map/ppermute | solution.py:42
  68.6 13.2 %collective-permute-start.13 = (bf16[2,400,256]{2,1,0:T(8,128)(2,1)S(1)}, bf16[2,400,256]{2,1,0:T(8,128)(2,1)}, u32[]{:S(2)}, u32[]{:S(2)}) collective-permute-start(bf16[2,400,256]{2,1,0:T(8,128)(2,1)S(1)} %pad_maximum_fusion.1.refs_1_.refs_3_), channel_id=1, source_target_pairs={{0,24},{2,26},{4,28},{6,30},{8,0},{10,2},{12,4},{14,6},{16,8},{18,... | collective-permute-start | bytes 1228808 | tf_op jit(solution)/shard_map/ppermute | solution.py:42
  69.4 12.8 %collective-permute-start.11 = (bf16[2,400,256]{2,1,0:T(8,128)(2,1)S(1)}, bf16[2,400,256]{2,1,0:T(8,128)(2,1)}, u32[]{:S(2)}, u32[]{:S(2)}) collective-permute-start(bf16[2,400,256]{2,1,0:T(8,128)(2,1)S(1)} %pad_maximum_fusion.1.refs_1_.refs_3_), channel_id=1, source_target_pairs={{0,8},{2,10},{4,12},{6,14},{8,16},{10,18},{12,20},{14,22},{16,24},... | collective-permute-start | bytes 1228808 | tf_op jit(solution)/shard_map/ppermute | solution.py:42
  75.8 50.9 %collective-permute-start.34 = (bf16[16,128,256]{2,1,0:T(8,128)(2,1)S(1)}, bf16[16,128,256]{2,1,0:T(8,128)(2,1)S(1)}, u32[]{:S(2)}, u32[]{:S(2)}) collective-permute-start(bf16[16,128,256]{2,1,0:T(8,128)(2,1)S(1)} %get-tuple-element.30), channel_id=1, source_target_pairs={{0,32},{2,34},{4,36},{6,38},{8,40},{10,42},{12,44},{14,46},{16,48}... | collective-permute-start | bytes 3145736 | tf_op jit(solution)/shard_map/ppermute | solution.py:42
  78.9 49.2 %collective-permute-start.35 = (bf16[16,128,256]{2,1,0:T(8,128)(2,1)S(1)}, bf16[16,128,256]{2,1,0:T(8,128)(2,1)S(1)}, u32[]{:S(2)}, u32[]{:S(2)}) collective-permute-start(bf16[16,128,256]{2,1,0:T(8,128)(2,1)S(1)} %get-tuple-element.31), channel_id=1, source_target_pairs={{0,64},{2,66},{4,68},{6,70},{8,72},{10,74},{12,76},{14,78},{16,80}... | collective-permute-start | bytes 3145736 | tf_op jit(solution)/shard_map/ppermute | solution.py:42
  79.1 49.0 %collective-permute-start.36 = (bf16[16,128,256]{2,1,0:T(8,128)(2,1)S(1)}, bf16[16,128,256]{2,1,0:T(8,128)(2,1)S(1)}, u32[]{:S(2)}, u32[]{:S(2)}) collective-permute-start(bf16[16,128,256]{2,1,0:T(8,128)(2,1)S(1)} %get-tuple-element.32), channel_id=1, source_target_pairs={{0,96},{2,98},{4,100},{6,102},{8,104},{10,106},{12,108},{14,110},{... | collective-permute-start | bytes 3145736 | tf_op jit(solution)/shard_map/ppermute | solution.py:42
  81.8 48.2 %collective-permute-start.31 = (bf16[16,128,256]{2,1,0:T(8,128)(2,1)S(1)}, bf16[16,128,256]{2,1,0:T(8,128)(2,1)S(1)}, u32[]{:S(2)}, u32[]{:S(2)}) collective-permute-start(bf16[16,128,256]{2,1,0:T(8,128)(2,1)S(1)} %get-tuple-element.26), channel_id=1, source_target_pairs={{0,8},{2,10},{4,12},{6,14},{8,16},{10,18},{12,20},{14,22},{16,24},... | collective-permute-start | bytes 3145736 | tf_op jit(solution)/shard_map/ppermute | solution.py:42
  82.2 32.6 %collective-permute-start.12 = (bf16[2,400,256]{2,1,0:T(8,128)(2,1)}, bf16[2,400,256]{2,1,0:T(8,128)(2,1)S(1)}, u32[]{:S(2)}, u32[]{:S(2)}) collective-permute-start(bf16[2,400,256]{2,1,0:T(8,128)(2,1)} %collective-permute-done.10.refs_2_.refs_4_), channel_id=1, source_target_pairs={{0,8},{2,10},{4,12},{6,14},{8,16},{10,18},{12,20},{14,22},{16,24},... | collective-permute-start | bytes 1228808 | tf_op jit(solution)/shard_map/ppermute | solution.py:42
  122.5 22.3 %collective-permute-start.32 = (bf16[16,128,256]{2,1,0:T(8,128)(2,1)}, bf16[16,128,256]{2,1,0:T(8,128)(2,1)}, u32[]{:S(2)}, u32[]{:S(2)}) collective-permute-start(bf16[16,128,256]{2,1,0:T(8,128)(2,1)} %get-tuple-element.27), channel_id=1, source_target_pairs={{0,16},{2,18},{4,20},{6,22},{8,24},{10,26},{12,28},{14,30},{16,0},... | collective-permute-start | bytes 3145736 | tf_op jit(solution)/shard_map/ppermute | solution.py:42
  126.7 43.9 %collective-permute-start.33 = (bf16[16,128,256]{2,1,0:T(8,128)(2,1)}, bf16[16,128,256]{2,1,0:T(8,128)(2,1)}, u32[]{:S(2)}, u32[]{:S(2)}) collective-permute-start(bf16[16,128,256]{2,1,0:T(8,128)(2,1)} %get-tuple-element.28), channel_id=1, source_target_pairs={{0,24},{2,26},{4,28},{6,30},{8,0},{10,2},{12,4},{14,6},{16,8},{18,... | collective-permute-start | bytes 3145736 | tf_op jit(solution)/shard_map/ppermute | solution.py:42
  128.1 47.5 %collective-permute-start.28 = (bf16[16,128,256]{2,1,0:T(8,128)(2,1)}, bf16[16,128,256]{2,1,0:T(8,128)(2,1)}, u32[]{:S(2)}, u32[]{:S(2)}) collective-permute-start(bf16[16,128,256]{2,1,0:T(8,128)(2,1)} %get-tuple-element.22), channel_id=1, source_target_pairs={{0,2},{2,4},{4,6},{6,0},{8,10},{10,12},{12,14},{14,8},{16,18},{18,... | collective-permute-start | bytes 3145736 | tf_op jit(solution)/shard_map/ppermute | solution.py:42
  128.2 47.5 %collective-permute-start.29 = (bf16[16,128,256]{2,1,0:T(8,128)(2,1)}, bf16[16,128,256]{2,1,0:T(8,128)(2,1)}, u32[]{:S(2)}, u32[]{:S(2)}) collective-permute-start(bf16[16,128,256]{2,1,0:T(8,128)(2,1)} %get-tuple-element.23), channel_id=1, source_target_pairs={{0,4},{2,6},{4,0},{6,2},{8,12},{10,14},{12,8},{14,10},{16,20},{18,... | collective-permute-start | bytes 3145736 | tf_op jit(solution)/shard_map/ppermute | solution.py:42
  130.0 46.3 %collective-permute-start.30 = (bf16[16,128,256]{2,1,0:T(8,128)(2,1)}, bf16[16,128,256]{2,1,0:T(8,128)(2,1)}, u32[]{:S(2)}, u32[]{:S(2)}) collective-permute-start(bf16[16,128,256]{2,1,0:T(8,128)(2,1)} %get-tuple-element.24), channel_id=1, source_target_pairs={{0,6},{2,0},{4,2},{6,4},{8,14},{10,8},{12,10},{14,12},{16,22},{18,... | collective-permute-start | bytes 3145736 | tf_op jit(solution)/shard_map/ppermute | solution.py:42
  144.8 41.7 %collective-permute-start.39 = (bf16[24,128,256]{2,1,0:T(8,128)(2,1)}, bf16[24,128,256]{2,1,0:T(8,128)(2,1)}, u32[]{:S(2)}, u32[]{:S(2)}) collective-permute-start(bf16[24,128,256]{2,1,0:T(8,128)(2,1)} %hand.5), channel_id=1, source_target_pairs={{0,1},{1,0},{2,3},{3,2},{4,5},{5,4},{6,7},{7,6},{8,9},{9,8},{10,11... | collective-permute-start | bytes 4718600 | tf_op jit(solution)/shard_map/ppermute | solution.py:46
  (51 other events, 309.1 us)

commit v3 on v2

--- a/solution.py
+++ b/solution.py
@@ -112,8 +112,10 @@
     values_ref[...] = jnp.transpose(w_ref[:, WIDTH:])
 
 
-def select_kernel(part, me_ref, table_ref, *refs):
-    walk_slots(part, me_ref, table_ref, refs[:8], list(enumerate(refs[8:], 1)))
+def select_kernel(me_ref, table_ref, *refs):
+    for part in range(PARTS):
+        outs = list(enumerate(refs[24 + 3 * part : 27 + 3 * part], 1))
+        walk_slots(part, me_ref, table_ref, refs[8 * part : 8 * part + 8], outs)
 
 
 def own_kernel(me_ref, table_ref, *refs):
@@ -158,14 +160,16 @@
     def start(i, _):
         code = jnp.maximum(code_ref[1, me_ref[3] * count + i], 0)
         away = [lax.shift_right_logical(code, shifts[axis]) & 3 for axis in range(3)]
-        for d in range(SIDE):
-
-            @pl.when(away[across] == d)
-            def _():
-                pltpu.make_async_copy(
-                    arrived[d].at[away[second] * 4 + away[first]], out.at[i], sem
-                ).start()
-
+        place = away[second] * 4 + away[first]
+
+        def bring(d):
+            pltpu.make_async_copy(arrived[d].at[place], out.at[i], sem).start()
+            return 0
+
+        def either(d):
+            return lambda: lax.cond(away[across] == d, lambda: bring(d), lambda: bring(d + 1))
+
+        lax.cond(away[across] < 2, either(0), either(2))
         return 0
 
     lax.fori_loop(0, count, start, 0)
@@ -390,15 +394,16 @@
         left = [shift(half, axis, -1) for half in lines[part]]
         far = [shift(right[0], axis, 1), shift(left[1], axis, -1)]
         gathered.append([*lines[part], *right, *far, *left])
-        chosen = pl.pallas_call(
-            lambda *refs: select_kernel(part, *refs),
-            out_shape=[slots] * (SIDE - 1),
-            in_specs=[SMEM] * 2 + [VMEM] * 8,
-            out_specs=[VMEM] * (SIDE - 1),
-            compiler_params=small,
-            name="select",
-        )(me, wishes, *gathered[part])
-        arrived.append([shift(chosen[d - 1], across, d) for d in range(1, SIDE)])
+    chosen = pl.pallas_call(
+        select_kernel,
+        out_shape=[slots] * 9,
+        in_specs=[SMEM] * 2 + [VMEM] * 24,
+        out_specs=[VMEM] * 9,
+        compiler_params=pltpu.CompilerParams(vmem_limit_bytes=2 * SELECT_VMEM),
+        name="select",
+    )(me, wishes, *[a for part in gathered for a in part])
+    for part, (across, _, _) in enumerate(ROUTES):
+        arrived.append([shift(chosen[3 * part + d - 1], across, d) for d in range(1, SIDE)])
     own_slots = pl.pallas_call(
         own_kernel,
         out_shape=[slots] * PARTS,

time: 219 us -> 238 us (1.087)
  waiting for transfers between devices: 86 us -> 101 us
  starting transfers between devices: 54.6 us -> 57.5 us
    ppermute x36, waiting for transfers between devices: 86 us -> 101 us  [shift(): return lax.ppermute(value, 'pb', pairs)]
    ppermute x36, starting transfers between devices: 43.7 us -> 49 us  [shift(): return lax.ppermute(value, 'pb', pairs)]
    pallas_call x3 -> x1, Pallas kernels: 6.79 us -> 4.71 us  [on_device(): pl.pallas_call(select_kernel, out_shape=[slots] * 9, in_specs=[SMEM] * 2...]
    unnamed x71 -> x61, local copies, waits for them, and re-layouts: 18.2 us -> 20 us
  transfers between devices with their start and end apart: 40 -> 40, of which waited for: 13 -> 16; matrix products, arithmetic and copies ran while one was open for 0% -> 0% of each run, Pallas kernels for 10% -> 7%
where the time goes in v3:
time: 238 us; the launch traced here: 235 us
  waiting for transfers between devices  101 us (42%)
  starting transfers between devices  57.5 us (24%)
  Pallas kernels  53.8 us (23%)
  local copies, waits for them, and re-layouts  21.7 us (9%)
    ppermute x36, waiting for transfers between devices, shift(): return lax.ppermute(value, 'pb', pairs)  101 us
    ppermute x36, starting transfers between devices, shift(): return lax.ppermute(value, 'pb', pairs)  49 us
    pallas_call x1, Pallas kernels, on_device(): pl.pallas_call(lambda *refs: attend_kernel(True, True, *refs), out_shape=...  30.5 us
    unnamed x61, local copies, waits for them, and re-layouts  20 us
    pallas_call x3, Pallas kernels, on_device(): pl.pallas_call(lambda *refs: hand_kernel(part, *refs), out_shape=jax.Shap...  12.9 us
    ppermute x4, starting transfers between devices, swap(): return lax.ppermute(value, 'ka', [(0, 1), (1, 0)])  8.51 us
  transfers between devices with their start and end apart: 40, of which 16 were waited for; matrix products, arithmetic and copies ran while one was open for 0% of the time, Pallas kernels for 7%

profile of v3, /device:TPU:1, one launch (start us, length us, event | category | flops | bytes accessed | tf_op | source)
XLA Modules:
  0.0 235.2 jit_solution(8473568104283778488)
XLA Ops:
  19.6 10.6 %collective-permute-done.1 = bf16[400,256]{1,0:T(8,128)(2,1)S(1)} collective-permute-done((bf16[400,256]{1,0:T(8,128)(2,1)S(1)}, bf16[400,256]{1,0:T(8,128)(2,1)S(1)}, u32[]{:S(2)}, u32[]{:S(2)}) %collective-permute-start.1) | collective-permute-done | bytes 204832 | tf_op jit(solution)/shard_map/ppermute | solution.py:42
  30.2 2.7 %collective-permute-start.8 = (bf16[400,256]{1,0:T(8,128)(2,1)S(1)}, bf16[400,256]{1,0:T(8,128)(2,1)S(1)}, u32[]{:S(2)}, u32[]{:S(2)}) collective-permute-start(bf16[400,256]{1,0:T(8,128)(2,1)S(1)} %get-tuple-element.37), channel_id=1, source_target_pairs={{0,24},{2,26},{4,28},{6,30},{8,0},{10,2},{12,4},{14,6},{16,8},{18,... | collective-permute-start | bytes 614408 | tf_op jit(solution)/shard_map/ppermute | solution.py:42
  32.9 2.6 %collective-permute-done.8 = bf16[400,256]{1,0:T(8,128)(2,1)S(1)} collective-permute-done((bf16[400,256]{1,0:T(8,128)(2,1)S(1)}, bf16[400,256]{1,0:T(8,128)(2,1)S(1)}, u32[]{:S(2)}, u32[]{:S(2)}) %collective-permute-start.8) | collective-permute-done | bytes 204832 | tf_op jit(solution)/shard_map/ppermute | solution.py:42
  35.6 3.1 %collective-permute-done.7 = bf16[400,256]{1,0:T(8,128)(2,1)S(1)} collective-permute-done((bf16[400,256]{1,0:T(8,128)(2,1)S(1)}, bf16[400,256]{1,0:T(8,128)(2,1)S(1)}, u32[]{:S(2)}, u32[]{:S(2)}) %collective-permute-start.7) | collective-permute-done | bytes 204832 | tf_op jit(solution)/shard_map/ppermute | solution.py:42
  38.7 3.6 %collective-permute-start.9 = (s32[16,128]{1,0:T(8,128)S(1)}, s32[16,128]{1,0:T(8,128)S(1)}, u32[]{:S(2)}, u32[]{:S(2)}) collective-permute-start(s32[16,128]{1,0:T(8,128)S(1)} %notes.1), channel_id=1, source_target_pairs={{0,1},{1,0},{2,3},{3,2},{4,5},{5,4},{6,7},{7,6},{8,9},{9,8},{10,11... | collective-permute-start | bytes 24584 | tf_op jit(solution)/shard_map/ppermute | solution.py:46
  46.1 7.2 %collective-permute-done.21.refs_14_ = bf16[2,400,256]{2,1,0:T(8,128)(2,1)S(1)} collective-permute-done((bf16[2,400,256]{2,1,0:T(8,128)(2,1)S(1)}, bf16[2,400,256]{2,1,0:T(8,128)(2,1)S(1)}, u32[]{:S(2)}, u32[]{:S(2)}) %collective-permute-start.21) | collective-permute-done | bytes 409632 | tf_op jit(solution)/shard_map/ppermute | solution.py:42
  56.9 7.5 %collective-permute-done.13.refs_7_ = bf16[2,400,256]{2,1,0:T(8,128)(2,1)} collective-permute-done((bf16[2,400,256]{2,1,0:T(8,128)(2,1)S(1)}, bf16[2,400,256]{2,1,0:T(8,128)(2,1)}, u32[]{:S(2)}, u32[]{:S(2)}) %collective-permute-start.13) | collective-permute-done | bytes 409632 | tf_op jit(solution)/shard_map/ppermute | solution.py:42
  68.1 2.7 %collective-permute-start.14 = (bf16[2,400,256]{2,1,0:T(8,128)(2,1)}, bf16[2,400,256]{2,1,0:T(8,128)(2,1)}, u32[]{:S(2)}, u32[]{:S(2)}) collective-permute-start(bf16[2,400,256]{2,1,0:T(8,128)(2,1)} %collective-permute-done.13.refs_7_), channel_id=1, source_target_pairs={{0,24},{2,26},{4,28},{6,30},{8,0},{10,2},{12,4},{14,6},{16,8},{18,... | collective-permute-start | bytes 1228808 | tf_op jit(solution)/shard_map/ppermute | solution.py:42
  70.8 4.4 %collective-permute-done.23.refs_19_ = bf16[2,400,256]{2,1,0:T(8,128)(2,1)S(1)} collective-permute-done((bf16[2,400,256]{2,1,0:T(8,128)(2,1)S(1)}, bf16[2,400,256]{2,1,0:T(8,128)(2,1)S(1)}, u32[]{:S(2)}, u32[]{:S(2)}) %collective-permute-start.23) | collective-permute-done | bytes 409632 | tf_op jit(solution)/shard_map/ppermute | solution.py:42
  78.9 5.1 %collective-permute-done.24.refs_20_ = bf16[2,400,256]{2,1,0:T(8,128)(2,1)} collective-permute-done((bf16[2,400,256]{2,1,0:T(8,128)(2,1)S(1)}, bf16[2,400,256]{2,1,0:T(8,128)(2,1)}, u32[]{:S(2)}, u32[]{:S(2)}) %collective-permute-start.24) | collective-permute-done | bytes 409632 | tf_op jit(solution)/shard_map/ppermute | solution.py:42
  92.5 4.7 %select.28 = (bf16[16,128,256]{2,1,0:T(8,128)(2,1)}, bf16[16,128,256]{2,1,0:T(8,128)(2,1)}, bf16[16,128,256]{2,1,0:T(8,128)(2,1)}, bf16[16,128,256]{2,1,0:T(8,12...) custom-call(s32[4]{0:T(128)S(1)} %pad_add_fusion.me_ref.refs_0_, ...), custom_call_target="tpu_custom_call" | custom-call | tf_op jit(solution)/shard_map/select/pallas_call | solution.py:397
  97.3 2.8 %collective-permute-start.35 = (bf16[16,128,256]{2,1,0:T(8,128)(2,1)S(1)}, bf16[16,128,256]{2,1,0:T(8,128)(2,1)S(1)}, u32[]{:S(2)}, u32[]{:S(2)}) collective-permute-start(bf16[16,128,256]{2,1,0:T(8,128)(2,1)S(1)} %get-tuple-element.31), channel_id=1, source_target_pairs={{0,64},{2,66},{4,68},{6,70},{8,72},{10,74},{12,76},{14,78},{16,80}... | collective-permute-start | bytes 3145736 | tf_op jit(solution)/shard_map/ppermute | solution.py:42
  100.2 4.9 %collective-permute-start.32 = (bf16[16,128,256]{2,1,0:T(8,128)(2,1)}, bf16[16,128,256]{2,1,0:T(8,128)(2,1)}, u32[]{:S(2)}, u32[]{:S(2)}) collective-permute-start(bf16[16,128,256]{2,1,0:T(8,128)(2,1)} %get-tuple-element.27), channel_id=1, source_target_pairs={{0,16},{2,18},{4,20},{6,22},{8,24},{10,26},{12,28},{14,30},{16,0},... | collective-permute-start | bytes 3145736 | tf_op jit(solution)/shard_map/ppermute | solution.py:42
  105.1 13.2 %collective-permute-done.34.refs_3_.refs_16_ = bf16[16,128,256]{2,1,0:T(8,128)(2,1)S(1)} collective-permute-done((bf16[16,128,256]{2,1,0:T(8,128)(2,1)S(1)}, bf16[16,128,256]{2,1,0:T(8,128)(2,1)S(1)}, u32[]{:S(2)}, u32[]{:S(2)}) %collective-permute-start.34) | collective-permute-done | bytes 1048608 | tf_op jit(solution)/shard_map/ppermute | solution.py:42
  118.3 9.1 %collective-permute-start.33 = (bf16[16,128,256]{2,1,0:T(8,128)(2,1)}, bf16[16,128,256]{2,1,0:T(8,128)(2,1)}, u32[]{:S(2)}, u32[]{:S(2)}) collective-permute-start(bf16[16,128,256]{2,1,0:T(8,128)(2,1)} %get-tuple-element.28), channel_id=1, source_target_pairs={{0,24},{2,26},{4,28},{6,30},{8,0},{10,2},{12,4},{14,6},{16,8},{18,... | collective-permute-start | bytes 3145736 | tf_op jit(solution)/shard_map/ppermute | solution.py:42
  127.4 15.2 %collective-permute-done.35.refs_4_.refs_17_ = bf16[16,128,256]{2,1,0:T(8,128)(2,1)S(1)} collective-permute-done((bf16[16,128,256]{2,1,0:T(8,128)(2,1)S(1)}, bf16[16,128,256]{2,1,0:T(8,128)(2,1)S(1)}, u32[]{:S(2)}, u32[]{:S(2)}) %collective-permute-start.35) | collective-permute-done | bytes 1048608 | tf_op jit(solution)/shard_map/ppermute | solution.py:42
  145.5 4.2 %collective-permute-start.29 = (bf16[16,128,256]{2,1,0:T(8,128)(2,1)}, bf16[16,128,256]{2,1,0:T(8,128)(2,1)}, u32[]{:S(2)}, u32[]{:S(2)}) collective-permute-start(bf16[16,128,256]{2,1,0:T(8,128)(2,1)} %get-tuple-element.23), channel_id=1, source_target_pairs={{0,4},{2,6},{4,0},{6,2},{8,12},{10,14},{12,8},{14,10},{16,20},{18,... | collective-permute-start | bytes 3145736 | tf_op jit(solution)/shard_map/ppermute | solution.py:42
  157.6 4.5 %hand.5 = bf16[24,128,256]{2,1,0:T(8,128)(2,1)} custom-call(s32[4]{0:T(128)} %copy-done.24, s32[2,128]{1,0:T(2,128)} %slice.21.refs_1_, bf16[16,128,256]{2,1,0:T(8,128)(2,1)} %copy-done.3, bf16[16,128,256]{2,1,0:T(8,128)(2,1)} %copy-done.26, bf16[16,128,256]{2,1,0:T(8,128)(2,1)} %copy-done.27, bf16[16,128,256]{2,1,0:T(8,128)(2,1)} %copy-done.28), custom_call_target="tpu_custom_call" | custom-call | tf_op jit(solution)/shard_map/hand/pallas_call | solution.py:435
  162.0 3.4 %collective-permute-start.39 = (bf16[24,128,256]{2,1,0:T(8,128)(2,1)}, bf16[24,128,256]{2,1,0:T(8,128)(2,1)}, u32[]{:S(2)}, u32[]{:S(2)}) collective-permute-start(bf16[24,128,256]{2,1,0:T(8,128)(2,1)} %hand.5), channel_id=1, source_target_pairs={{0,1},{1,0},{2,3},{3,2},{4,5},{5,4},{6,7},{7,6},{8,9},{9,8},{10,11... | collective-permute-start | bytes 4718600 | tf_op jit(solution)/shard_map/ppermute | solution.py:46
  165.5 4.4 %hand.4 = bf16[24,128,256]{2,1,0:T(8,128)(2,1)} custom-call(s32[4]{0:T(128)} %copy-done.24, s32[2,128]{1,0:T(2,128)} %slice.21.refs_1_, bf16[16,128,256]{2,1,0:T(8,128)(2,1)} %copy-done.2, bf16[16,128,256]{2,1,0:T(8,128)(2,1)} %copy-done.29, bf16[16,128,256]{2,1,0:T(8,128)(2,1)} %collective-permute-done.32.refs_4_.refs_13_, ...), custom_call_target="tpu_custom_call" | custom-call | tf_op jit(solution)/shard_map/hand/pallas_call | solution.py:435
  170.0 19.8 %collective-permute-done.29.refs_4_.refs_9_ = bf16[16,128,256]{2,1,0:T(8,128)(2,1)} collective-permute-done((bf16[16,128,256]{2,1,0:T(8,128)(2,1)}, bf16[16,128,256]{2,1,0:T(8,128)(2,1)}, u32[]{:S(2)}, u32[]{:S(2)}) %collective-permute-start.29) | collective-permute-done | bytes 1048608 | tf_op jit(solution)/shard_map/ppermute | solution.py:42
  189.8 4.8 %collective-permute-done.30.refs_5_.refs_10_ = bf16[16,128,256]{2,1,0:T(8,128)(2,1)} collective-permute-done((bf16[16,128,256]{2,1,0:T(8,128)(2,1)}, bf16[16,128,256]{2,1,0:T(8,128)(2,1)}, u32[]{:S(2)}, u32[]{:S(2)}) %collective-permute-start.30) | collective-permute-done | bytes 1048608 | tf_op jit(solution)/shard_map/ppermute | solution.py:42
  194.7 4.0 %hand.3 = bf16[24,128,256]{2,1,0:T(8,128)(2,1)} custom-call(s32[4]{0:T(128)} %copy-done.24, s32[2,128]{1,0:T(2,128)} %slice.21.refs_1_, bf16[16,128,256]{2,1,0:T(8,128)(2,1)} %copy-done.1, bf16[16,128,256]{2,1,0:T(8,128)(2,1)} %collective-permute-done.28.refs_3_.refs_8_, bf16[16,128,256]{2,1,0:T(8,128)(2,1)} %collective-permute-done.29.refs_4_.refs_9_, ...), custom_call_target="tpu_custom_call" | custom-call | tf_op jit(solution)/shard_map/hand/pallas_call | solution.py:435
  204.6 30.5 %attend.1 = bf16[512,768]{1,0:T(8,128)(2,1)} custom-call(s32[4]{0:T(128)} %copy-done.24, s32[2,128]{1,0:T(2,128)} %tables.1.table_ref.refs_1_, s32[4,2]{1,0:T(4,128)} %copy.9.refs_1_.refs_2_, bf16[4,6,256,128]{3,2,1,0:T(8,128)(2,1)} %copy-done, bf16[768,768]{1,0:T(8,128)(2,1)} %copy-done.21, bf16[768,768]{1,0:T(8,128)(2,1)} %copy-done.22, ...), custom_call_target="tpu_custom_call" | custom-call | tf_op jit(solution)/shard_map/attend/pallas_call | solution.py:444
  (139 shorter events, 59.8 us)
Async XLA Ops:
  14.2 30.9 %collective-permute-start.16 = (bf16[2,400,256]{2,1,0:T(8,128)(2,1)S(1)}, bf16[2,400,256]{2,1,0:T(8,128)(2,1)S(1)}, u32[]{:S(2)}, u32[]{:S(2)}) collective-permute-start(bf16[2,400,256]{2,1,0:T(8,128)(2,1)S(1)} %pad_maximum_fusion.2.refs_2_.refs_8_), channel_id=1, source_target_pairs={{0,32},{2,34},{4,36},{6,38},{8,40},{10,42},{12,44},{14,46},{16,48}... | collective-permute-start | bytes 1228808 | tf_op jit(solution)/shard_map/ppermute | solution.py:42
  15.8 17.0 %collective-permute-start.4 = (bf16[400,256]{1,0:T(8,128)(2,1)S(1)}, bf16[400,256]{1,0:T(8,128)(2,1)S(1)}, u32[]{:S(2)}, u32[]{:S(2)}) collective-permute-start(bf16[400,256]{1,0:T(8,128)(2,1)S(1)} %collective-permute-done.3), channel_id=1, source_target_pairs={{0,2},{2,4},{4,6},{6,0},{8,10},{10,12},{12,14},{14,8},{16,18},{18,... | collective-permute-start | bytes 614408 | tf_op jit(solution)/shard_map/ppermute | solution.py:42
  17.1 13.1 %collective-permute-start.1 = (bf16[400,256]{1,0:T(8,128)(2,1)S(1)}, bf16[400,256]{1,0:T(8,128)(2,1)S(1)}, u32[]{:S(2)}, u32[]{:S(2)}) collective-permute-start(bf16[400,256]{1,0:T(8,128)(2,1)S(1)} %collective-permute-done), channel_id=1, source_target_pairs={{0,32},{2,34},{4,36},{6,38},{8,40},{10,42},{12,44},{14,46},{16,48}... | collective-permute-start | bytes 614408 | tf_op jit(solution)/shard_map/ppermute | solution.py:42
  17.7 27.4 %collective-permute-start.22 = (bf16[2,400,256]{2,1,0:T(8,128)(2,1)S(1)}, bf16[2,400,256]{2,1,0:T(8,128)(2,1)S(1)}, u32[]{:S(2)}, u32[]{:S(2)}) collective-permute-start(bf16[2,400,256]{2,1,0:T(8,128)(2,1)S(1)} %pad_maximum_fusion.4.refs_4_.refs_16_), channel_id=1, source_target_pairs={{0,2},{2,4},{4,6},{6,0},{8,10},{10,12},{12,14},{14,8},{16,18},{18,... | collective-permute-start | bytes 1228808 | tf_op jit(solution)/shard_map/ppermute | solution.py:42
  19.0 26.2 %collective-permute-start.10 = (bf16[2,400,256]{2,1,0:T(8,128)(2,1)S(1)}, bf16[2,400,256]{2,1,0:T(8,128)(2,1)}, u32[]{:S(2)}, u32[]{:S(2)}) collective-permute-start(bf16[2,400,256]{2,1,0:T(8,128)(2,1)S(1)} %pad_maximum_fusion.refs_0_), channel_id=1, source_target_pairs={{0,8},{2,10},{4,12},{6,14},{8,16},{10,18},{12,20},{14,22},{16,24},... | collective-permute-start | bytes 1228808 | tf_op jit(solution)/shard_map/ppermute | solution.py:42
  43.8 11.5 %collective-permute-start.27 = (bf16[2,400,256]{2,1,0:T(8,128)(2,1)S(1)}, bf16[2,400,256]{2,1,0:T(8,128)(2,1)S(1)}, u32[]{:S(2)}, u32[]{:S(2)}) collective-permute-start(bf16[2,400,256]{2,1,0:T(8,128)(2,1)S(1)} %pad_maximum_fusion.4.refs_4_.refs_16_), channel_id=1, source_target_pairs={{0,6},{2,0},{4,2},{6,4},{8,14},{10,8},{12,10},{14,12},{16,22},{18,... | collective-permute-start | bytes 1228808 | tf_op jit(solution)/shard_map/ppermute | solution.py:42
  45.1 11.0 %collective-permute-start.15 = (bf16[2,400,256]{2,1,0:T(8,128)(2,1)S(1)}, bf16[2,400,256]{2,1,0:T(8,128)(2,1)S(1)}, u32[]{:S(2)}, u32[]{:S(2)}) collective-permute-start(bf16[2,400,256]{2,1,0:T(8,128)(2,1)S(1)} %pad_maximum_fusion.refs_0_), channel_id=1, source_target_pairs={{0,24},{2,26},{4,28},{6,30},{8,0},{10,2},{12,4},{14,6},{16,8},{18,... | collective-permute-start | bytes 1228808 | tf_op jit(solution)/shard_map/ppermute | solution.py:42
  45.1 19.3 %collective-permute-start.13 = (bf16[2,400,256]{2,1,0:T(8,128)(2,1)S(1)}, bf16[2,400,256]{2,1,0:T(8,128)(2,1)}, u32[]{:S(2)}, u32[]{:S(2)}) collective-permute-start(bf16[2,400,256]{2,1,0:T(8,128)(2,1)S(1)} %pad_maximum_fusion.1.refs_1_), channel_id=1, source_target_pairs={{0,24},{2,26},{4,28},{6,30},{8,0},{10,2},{12,4},{14,6},{16,8},{18,... | collective-permute-start | bytes 1228808 | tf_op jit(solution)/shard_map/ppermute | solution.py:42
  45.2 19.4 %collective-permute-start.19 = (bf16[2,400,256]{2,1,0:T(8,128)(2,1)S(1)}, bf16[2,400,256]{2,1,0:T(8,128)(2,1)}, u32[]{:S(2)}, u32[]{:S(2)}) collective-permute-start(bf16[2,400,256]{2,1,0:T(8,128)(2,1)S(1)} %pad_maximum_fusion.3.refs_3_.refs_9_), channel_id=1, source_target_pairs={{0,96},{2,98},{4,100},{6,102},{8,104},{10,106},{12,108},{14,110},{... | collective-permute-start | bytes 1228808 | tf_op jit(solution)/shard_map/ppermute | solution.py:42
  64.6 12.8 %collective-permute-start.18 = (bf16[2,400,256]{2,1,0:T(8,128)(2,1)S(1)}, bf16[2,400,256]{2,1,0:T(8,128)(2,1)S(1)}, u32[]{:S(2)}, u32[]{:S(2)}) collective-permute-start(bf16[2,400,256]{2,1,0:T(8,128)(2,1)S(1)} %collective-permute-done.16.refs_10_), channel_id=1, source_target_pairs={{0,32},{2,34},{4,36},{6,38},{8,40},{10,42},{12,44},{14,46},{16,48}... | collective-permute-start | bytes 1228808 | tf_op jit(solution)/shard_map/ppermute | solution.py:42
  64.6 19.4 %collective-permute-start.24 = (bf16[2,400,256]{2,1,0:T(8,128)(2,1)S(1)}, bf16[2,400,256]{2,1,0:T(8,128)(2,1)}, u32[]{:S(2)}, u32[]{:S(2)}) collective-permute-start(bf16[2,400,256]{2,1,0:T(8,128)(2,1)S(1)} %collective-permute-done.22.refs_18_), channel_id=1, source_target_pairs={{0,2},{2,4},{4,6},{6,0},{8,10},{10,12},{12,14},{14,8},{16,18},{18,... | collective-permute-start | bytes 1228808 | tf_op jit(solution)/shard_map/ppermute | solution.py:42
  67.4 16.6 %collective-permute-start.12 = (bf16[2,400,256]{2,1,0:T(8,128)(2,1)}, bf16[2,400,256]{2,1,0:T(8,128)(2,1)}, u32[]{:S(2)}, u32[]{:S(2)}) collective-permute-start(bf16[2,400,256]{2,1,0:T(8,128)(2,1)} %collective-permute-done.10.refs_2_), channel_id=1, source_target_pairs={{0,8},{2,10},{4,12},{6,14},{8,16},{10,18},{12,20},{14,22},{16,24},... | collective-permute-start | bytes 1228808 | tf_op jit(solution)/shard_map/ppermute | solution.py:42
  68.1 15.9 %collective-permute-start.14 = (bf16[2,400,256]{2,1,0:T(8,128)(2,1)}, bf16[2,400,256]{2,1,0:T(8,128)(2,1)}, u32[]{:S(2)}, u32[]{:S(2)}) collective-permute-start(bf16[2,400,256]{2,1,0:T(8,128)(2,1)} %collective-permute-done.13.refs_7_), channel_id=1, source_target_pairs={{0,24},{2,26},{4,28},{6,30},{8,0},{10,2},{12,4},{14,6},{16,8},{18,... | collective-permute-start | bytes 1228808 | tf_op jit(solution)/shard_map/ppermute | solution.py:42
  97.2 21.1 %collective-permute-start.34 = (bf16[16,128,256]{2,1,0:T(8,128)(2,1)S(1)}, bf16[16,128,256]{2,1,0:T(8,128)(2,1)S(1)}, u32[]{:S(2)}, u32[]{:S(2)}) collective-permute-start(bf16[16,128,256]{2,1,0:T(8,128)(2,1)S(1)} %get-tuple-element.30), channel_id=1, source_target_pairs={{0,32},{2,34},{4,36},{6,38},{8,40},{10,42},{12,44},{14,46},{16,48}... | collective-permute-start | bytes 3145736 | tf_op jit(solution)/shard_map/ppermute | solution.py:42
  97.3 45.3 %collective-permute-start.35 = (bf16[16,128,256]{2,1,0:T(8,128)(2,1)S(1)}, bf16[16,128,256]{2,1,0:T(8,128)(2,1)S(1)}, u32[]{:S(2)}, u32[]{:S(2)}) collective-permute-start(bf16[16,128,256]{2,1,0:T(8,128)(2,1)S(1)} %get-tuple-element.31), channel_id=1, source_target_pairs={{0,64},{2,66},{4,68},{6,70},{8,72},{10,74},{12,76},{14,78},{16,80}... | collective-permute-start | bytes 3145736 | tf_op jit(solution)/shard_map/ppermute | solution.py:42
  100.2 45.3 %collective-permute-start.36 = (bf16[16,128,256]{2,1,0:T(8,128)(2,1)S(1)}, bf16[16,128,256]{2,1,0:T(8,128)(2,1)S(1)}, u32[]{:S(2)}, u32[]{:S(2)}) collective-permute-start(bf16[16,128,256]{2,1,0:T(8,128)(2,1)S(1)} %get-tuple-element.32), channel_id=1, source_target_pairs={{0,96},{2,98},{4,100},{6,102},{8,104},{10,106},{12,108},{14,110},{... | collective-permute-start | bytes 3145736 | tf_op jit(solution)/shard_map/ppermute | solution.py:42
  100.2 49.5 %collective-permute-start.31 = (bf16[16,128,256]{2,1,0:T(8,128)(2,1)S(1)}, bf16[16,128,256]{2,1,0:T(8,128)(2,1)S(1)}, u32[]{:S(2)}, u32[]{:S(2)}) collective-permute-start(bf16[16,128,256]{2,1,0:T(8,128)(2,1)S(1)} %get-tuple-element.26), channel_id=1, source_target_pairs={{0,8},{2,10},{4,12},{6,14},{8,16},{10,18},{12,20},{14,22},{16,24},... | collective-permute-start | bytes 3145736 | tf_op jit(solution)/shard_map/ppermute | solution.py:42
  100.2 61.8 %collective-permute-start.32 = (bf16[16,128,256]{2,1,0:T(8,128)(2,1)}, bf16[16,128,256]{2,1,0:T(8,128)(2,1)}, u32[]{:S(2)}, u32[]{:S(2)}) collective-permute-start(bf16[16,128,256]{2,1,0:T(8,128)(2,1)} %get-tuple-element.27), channel_id=1, source_target_pairs={{0,16},{2,18},{4,20},{6,22},{8,24},{10,26},{12,28},{14,30},{16,0},... | collective-permute-start | bytes 3145736 | tf_op jit(solution)/shard_map/ppermute | solution.py:42
  118.3 47.1 %collective-permute-start.33 = (bf16[16,128,256]{2,1,0:T(8,128)(2,1)}, bf16[16,128,256]{2,1,0:T(8,128)(2,1)}, u32[]{:S(2)}, u32[]{:S(2)}) collective-permute-start(bf16[16,128,256]{2,1,0:T(8,128)(2,1)} %get-tuple-element.28), channel_id=1, source_target_pairs={{0,24},{2,26},{4,28},{6,30},{8,0},{10,2},{12,4},{14,6},{16,8},{18,... | collective-permute-start | bytes 3145736 | tf_op jit(solution)/shard_map/ppermute | solution.py:42
  142.6 27.4 %collective-permute-start.28 = (bf16[16,128,256]{2,1,0:T(8,128)(2,1)}, bf16[16,128,256]{2,1,0:T(8,128)(2,1)}, u32[]{:S(2)}, u32[]{:S(2)}) collective-permute-start(bf16[16,128,256]{2,1,0:T(8,128)(2,1)} %get-tuple-element.22), channel_id=1, source_target_pairs={{0,2},{2,4},{4,6},{6,0},{8,10},{10,12},{12,14},{14,8},{16,18},{18,... | collective-permute-start | bytes 3145736 | tf_op jit(solution)/shard_map/ppermute | solution.py:42
  145.5 44.3 %collective-permute-start.29 = (bf16[16,128,256]{2,1,0:T(8,128)(2,1)}, bf16[16,128,256]{2,1,0:T(8,128)(2,1)}, u32[]{:S(2)}, u32[]{:S(2)}) collective-permute-start(bf16[16,128,256]{2,1,0:T(8,128)(2,1)} %get-tuple-element.23), channel_id=1, source_target_pairs={{0,4},{2,6},{4,0},{6,2},{8,12},{10,14},{12,8},{14,10},{16,20},{18,... | collective-permute-start | bytes 3145736 | tf_op jit(solution)/shard_map/ppermute | solution.py:42
  149.7 45.0 %collective-permute-start.30 = (bf16[16,128,256]{2,1,0:T(8,128)(2,1)}, bf16[16,128,256]{2,1,0:T(8,128)(2,1)}, u32[]{:S(2)}, u32[]{:S(2)}) collective-permute-start(bf16[16,128,256]{2,1,0:T(8,128)(2,1)} %get-tuple-element.24), channel_id=1, source_target_pairs={{0,6},{2,0},{4,2},{6,4},{8,14},{10,8},{12,10},{14,12},{16,22},{18,... | collective-permute-start | bytes 3145736 | tf_op jit(solution)/shard_map/ppermute | solution.py:42
  162.0 42.5 %collective-permute-start.39 = (bf16[24,128,256]{2,1,0:T(8,128)(2,1)}, bf16[24,128,256]{2,1,0:T(8,128)(2,1)}, u32[]{:S(2)}, u32[]{:S(2)}) collective-permute-start(bf16[24,128,256]{2,1,0:T(8,128)(2,1)} %hand.5), channel_id=1, source_target_pairs={{0,1},{1,0},{2,3},{3,2},{4,5},{5,4},{6,7},{7,6},{8,9},{9,8},{10,11... | collective-permute-start | bytes 4718600 | tf_op jit(solution)/shard_map/ppermute | solution.py:46
  169.9 34.7 %collective-permute-start.38 = (bf16[24,128,256]{2,1,0:T(8,128)(2,1)}, bf16[24,128,256]{2,1,0:T(8,128)(2,1)}, u32[]{:S(2)}, u32[]{:S(2)}) collective-permute-start(bf16[24,128,256]{2,1,0:T(8,128)(2,1)} %hand.4), channel_id=1, source_target_pairs={{0,1},{1,0},{2,3},{3,2},{4,5},{5,4},{6,7},{7,6},{8,9},{9,8},{10,11... | collective-permute-start | bytes 4718600 | tf_op jit(solution)/shard_map/ppermute | solution.py:46
  (46 other events, 377.0 us)

commit v4 on v3

--- a/solution.py
+++ b/solution.py
@@ -113,9 +113,18 @@
 
 
 def select_kernel(me_ref, table_ref, *refs):
+    outs = refs[24:33]
+    stage, sems = refs[33:]
+    sends = [
+        pltpu.make_async_copy(stage.at[n], out, sems.at[n]) for n, out in enumerate(outs)
+    ]
     for part in range(PARTS):
-        outs = list(enumerate(refs[24 + 3 * part : 27 + 3 * part], 1))
-        walk_slots(part, me_ref, table_ref, refs[8 * part : 8 * part + 8], outs)
+        for d in range(1, SIDE):
+            n = 3 * part + d - 1
+            walk_slots(part, me_ref, table_ref, refs[8 * part : 8 * part + 8], [(d, stage.at[n])])
+            sends[n].start()
+    for send in sends:
+        send.wait()
 
 
 def own_kernel(me_ref, table_ref, *refs):
@@ -150,7 +159,7 @@
                 ).start()
 
 
-def hand_kernel(part, me_ref, code_ref, *refs):
+def hand_kernel(part, code_ref, *refs):
     arrived = refs[:SIDE]
     out, sem = refs[SIDE:]
     count = out.shape[0]
@@ -158,7 +167,7 @@
     shifts = (4, 2, 0)
 
     def start(i, _):
-        code = jnp.maximum(code_ref[1, me_ref[3] * count + i], 0)
+        code = jnp.maximum(code_ref[i], 0)
         away = [lax.shift_right_logical(code, shifts[axis]) & 3 for axis in range(3)]
         place = away[second] * 4 + away[first]
 
@@ -178,7 +187,8 @@
 
 def attend_kernel(first, last, *refs):
     refs = list(refs)
-    me_ref, code_ref, count_ref, spread, wk_ref, wvt_ref, wo_ref = refs[:7]
+    me_ref, code_ref, count_ref = refs[:3]
+    held = refs[3:7]
     arrived = [refs[7 + 4 * part : 11 + 4 * part] for part in range(PARTS)]
     handed = refs[19:22]
     refs = refs[22:]
@@ -192,7 +202,14 @@
         peak, total, sums = refs[:3]
         refs = refs[3:]
     item_q, item_n, item_code, tokens, keys, values, sems = refs[:7]
+    spread, wk_ref, wvt_ref, wo_ref, load_sems = refs[7:12]
     blocks = spread.shape[0]
+    loads = [
+        pltpu.make_async_copy(source, target, load_sems.at[i])
+        for i, (source, target) in enumerate(zip(held, (spread, wk_ref, wvt_ref, wo_ref)))
+    ]
+    for i in (1, 2, 0, 3):
+        loads[i].start()
     mine = me_ref[3]
     span = blocks * CAP
 
@@ -266,9 +283,14 @@
     else:
         for mine_ref, old_ref in zip((peak, total, sums), before):
             mine_ref[...] = old_ref[...]
+    loads[1].wait()
     landed(0)
-    for chunk in range(6):
+    for chunk in range(3):
         project(0, chunk)
+    loads[2].wait()
+    for chunk in range(3, 6):
+        project(0, chunk)
+    loads[0].wait()
 
     def step(t, _):
         slot = t & 1
@@ -335,6 +357,7 @@
         return 0
 
     lax.fori_loop(0, steps, step, 0)
+    loads[3].wait()
     if last:
         for q in range(blocks):
             done = []
@@ -384,7 +407,9 @@
     )(table, *[half for line in lines for half in line])
     partner = swap(wishes)
     wishes = wishes + partner
-    partner = partner[9:11]
+    codes = lax.dynamic_slice(
+        partner[10], (lax.axis_index("ka") * blocks * CAP,), (blocks * CAP,)
+    )
 
     slots = jax.ShapeDtypeStruct((SIDE * SIDE, BLK, CUT), BF)
     gathered = []
@@ -398,7 +423,11 @@
         select_kernel,
         out_shape=[slots] * 9,
         in_specs=[SMEM] * 2 + [VMEM] * 24,
-        out_specs=[VMEM] * 9,
+        out_specs=[HBM] * 9,
+        scratch_shapes=[
+            pltpu.VMEM((9, SIDE * SIDE, BLK, CUT), BF),
+            pltpu.SemaphoreType.DMA((9,)),
+        ],
         compiler_params=pltpu.CompilerParams(vmem_limit_bytes=2 * SELECT_VMEM),
         name="select",
     )(me, wishes, *[a for part in gathered for a in part])
@@ -435,16 +464,16 @@
         given = pl.pallas_call(
             lambda *refs: hand_kernel(part, *refs),
             out_shape=jax.ShapeDtypeStruct((blocks * CAP, BLK, CUT), BF),
-            in_specs=[SMEM] * 2 + [HBM] * SIDE,
+            in_specs=[SMEM] + [HBM] * SIDE,
             out_specs=VMEM,
             scratch_shapes=[pltpu.SemaphoreType.DMA],
             name="hand",
-        )(me, partner, *arrived[part])
+        )(codes, *arrived[part])
         handed.append(swap(given))
     return pl.pallas_call(
         lambda *refs: attend_kernel(True, True, *refs),
         out_shape=jax.ShapeDtypeStruct(query_tokens.shape, BF),
-        in_specs=[SMEM] * 3 + [VMEM] * 4 + [HBM] * 15,
+        in_specs=[SMEM] * 3 + [HBM] * 19,
         out_specs=VMEM,
         scratch_shapes=[
             pltpu.SMEM((items,), I32),
@@ -454,6 +483,11 @@
             pltpu.VMEM((2, ITEM, WIDTH), BF),
             pltpu.VMEM((2, WIDTH, ITEM), BF),
             pltpu.SemaphoreType.DMA((2,)),
+            pltpu.VMEM((blocks, PAIRS, 2 * BLK, BLK), BF),
+            pltpu.VMEM((WIDTH, WIDTH), BF),
+            pltpu.VMEM((WIDTH, WIDTH), BF),
+            pltpu.VMEM((WIDTH, WIDTH), BF),
+            pltpu.SemaphoreType.DMA((4,)),
             pltpu.VMEM((blocks, 8, 2 * BLK), F32),
             pltpu.VMEM((blocks, 8, 2 * BLK), F32),
             pltpu.VMEM((blocks, WIDTH, BLK), F32),

time: 238 us -> 240 us (level)
  waiting for transfers between devices: 101 us -> 92.5 us
  local copies, waits for them, and re-layouts: 21.7 us -> 29.7 us
    ppermute x36, waiting for transfers between devices: 101 us -> 92.5 us  [shift(): return lax.ppermute(value, 'pb', pairs)]
    unnamed x61 -> x73, local copies, waits for them, and re-layouts: 20 us -> 28 us
where the time goes in v4:
time: 240 us; the launch traced here: 235 us
  waiting for transfers between devices  92.5 us (39%)
  starting transfers between devices  58.3 us (24%)
  Pallas kernels  52.7 us (22%)
  local copies, waits for them, and re-layouts  29.7 us (12%)
    ppermute x36, waiting for transfers between devices, shift(): return lax.ppermute(value, 'pb', pairs)  92.5 us
    ppermute x36, starting transfers between devices, shift(): return lax.ppermute(value, 'pb', pairs)  49.5 us
    pallas_call x1, Pallas kernels, on_device(): pl.pallas_call(lambda *refs: attend_kernel(True, True, *refs), out_shape=...  30.3 us
    unnamed x73, local copies, waits for them, and re-layouts  28 us
    pallas_call x3, Pallas kernels, on_device(): pl.pallas_call(lambda *refs: hand_kernel(part, *refs), out_shape=jax.Shap...  12.3 us
    ppermute x4, starting transfers between devices, swap(): return lax.ppermute(value, 'ka', [(0, 1), (1, 0)])  8.8 us
  transfers between devices with their start and end apart: 40, of which 16 were waited for; matrix products, arithmetic and copies ran while one was open for 0% of the time, Pallas kernels for 7%

profile of v4, /device:TPU:1, one launch (start us, length us, event | category | flops | bytes accessed | tf_op | source)
XLA Modules:
  0.0 234.9 jit_solution(16727574319758414736)
XLA Ops:
  19.7 10.6 %collective-permute-done.1 = bf16[400,256]{1,0:T(8,128)(2,1)S(1)} collective-permute-done((bf16[400,256]{1,0:T(8,128)(2,1)S(1)}, bf16[400,256]{1,0:T(8,128)(2,1)S(1)}, u32[]{:S(2)}, u32[]{:S(2)}) %collective-permute-start.1) | collective-permute-done | bytes 204832 | tf_op jit(solution)/shard_map/ppermute | solution.py:42
  30.3 2.7 %collective-permute-start.8 = (bf16[400,256]{1,0:T(8,128)(2,1)S(1)}, bf16[400,256]{1,0:T(8,128)(2,1)S(1)}, u32[]{:S(2)}, u32[]{:S(2)}) collective-permute-start(bf16[400,256]{1,0:T(8,128)(2,1)S(1)} %get-tuple-element.37), channel_id=1, source_target_pairs={{0,24},{2,26},{4,28},{6,30},{8,0},{10,2},{12,4},{14,6},{16,8},{18,... | collective-permute-start | bytes 614408 | tf_op jit(solution)/shard_map/ppermute | solution.py:42
  33.0 2.6 %collective-permute-done.8 = bf16[400,256]{1,0:T(8,128)(2,1)S(1)} collective-permute-done((bf16[400,256]{1,0:T(8,128)(2,1)S(1)}, bf16[400,256]{1,0:T(8,128)(2,1)S(1)}, u32[]{:S(2)}, u32[]{:S(2)}) %collective-permute-start.8) | collective-permute-done | bytes 204832 | tf_op jit(solution)/shard_map/ppermute | solution.py:42
  35.6 3.1 %collective-permute-done.7 = bf16[400,256]{1,0:T(8,128)(2,1)S(1)} collective-permute-done((bf16[400,256]{1,0:T(8,128)(2,1)S(1)}, bf16[400,256]{1,0:T(8,128)(2,1)S(1)}, u32[]{:S(2)}, u32[]{:S(2)}) %collective-permute-start.7) | collective-permute-done | bytes 204832 | tf_op jit(solution)/shard_map/ppermute | solution.py:42
  38.8 3.6 %collective-permute-start.9 = (s32[16,128]{1,0:T(8,128)S(1)}, s32[16,128]{1,0:T(8,128)S(1)}, u32[]{:S(2)}, u32[]{:S(2)}) collective-permute-start(s32[16,128]{1,0:T(8,128)S(1)} %notes.1), channel_id=1, source_target_pairs={{0,1},{1,0},{2,3},{3,2},{4,5},{5,4},{6,7},{7,6},{8,9},{9,8},{10,11... | collective-permute-start | bytes 24584 | tf_op jit(solution)/shard_map/ppermute | solution.py:46
  46.1 7.2 %collective-permute-done.21.refs_14_ = bf16[2,400,256]{2,1,0:T(8,128)(2,1)S(1)} collective-permute-done((bf16[2,400,256]{2,1,0:T(8,128)(2,1)S(1)}, bf16[2,400,256]{2,1,0:T(8,128)(2,1)S(1)}, u32[]{:S(2)}, u32[]{:S(2)}) %collective-permute-start.21) | collective-permute-done | bytes 409632 | tf_op jit(solution)/shard_map/ppermute | solution.py:42
  56.9 7.5 %collective-permute-done.13.refs_7_ = bf16[2,400,256]{2,1,0:T(8,128)(2,1)} collective-permute-done((bf16[2,400,256]{2,1,0:T(8,128)(2,1)S(1)}, bf16[2,400,256]{2,1,0:T(8,128)(2,1)}, u32[]{:S(2)}, u32[]{:S(2)}) %collective-permute-start.13) | collective-permute-done | bytes 409632 | tf_op jit(solution)/shard_map/ppermute | solution.py:42
  68.1 2.7 %collective-permute-start.14 = (bf16[2,400,256]{2,1,0:T(8,128)(2,1)}, bf16[2,400,256]{2,1,0:T(8,128)(2,1)}, u32[]{:S(2)}, u32[]{:S(2)}) collective-permute-start(bf16[2,400,256]{2,1,0:T(8,128)(2,1)} %collective-permute-done.13.refs_7_), channel_id=1, source_target_pairs={{0,24},{2,26},{4,28},{6,30},{8,0},{10,2},{12,4},{14,6},{16,8},{18,... | collective-permute-start | bytes 1228808 | tf_op jit(solution)/shard_map/ppermute | solution.py:42
  70.8 4.5 %collective-permute-done.23.refs_19_ = bf16[2,400,256]{2,1,0:T(8,128)(2,1)S(1)} collective-permute-done((bf16[2,400,256]{2,1,0:T(8,128)(2,1)S(1)}, bf16[2,400,256]{2,1,0:T(8,128)(2,1)S(1)}, u32[]{:S(2)}, u32[]{:S(2)}) %collective-permute-start.23) | collective-permute-done | bytes 409632 | tf_op jit(solution)/shard_map/ppermute | solution.py:42
  79.0 5.1 %collective-permute-done.24.refs_20_ = bf16[2,400,256]{2,1,0:T(8,128)(2,1)} collective-permute-done((bf16[2,400,256]{2,1,0:T(8,128)(2,1)S(1)}, bf16[2,400,256]{2,1,0:T(8,128)(2,1)}, u32[]{:S(2)}, u32[]{:S(2)}) %collective-permute-start.24) | collective-permute-done | bytes 409632 | tf_op jit(solution)/shard_map/ppermute | solution.py:42
  92.5 4.5 %select.28 = (bf16[16,128,256]{2,1,0:T(8,128)(2,1)}, bf16[16,128,256]{2,1,0:T(8,128)(2,1)}, bf16[16,128,256]{2,1,0:T(8,128)(2,1)}, bf16[16,128,256]{2,1,0:T(8,12...) custom-call(s32[4]{0:T(128)S(1)} %pad_add_fusion.me_ref.refs_0_, ...), custom_call_target="tpu_custom_call" | custom-call | tf_op jit(solution)/shard_map/select/pallas_call | solution.py:422
  97.2 2.8 %collective-permute-start.35 = (bf16[16,128,256]{2,1,0:T(8,128)(2,1)S(1)}, bf16[16,128,256]{2,1,0:T(8,128)(2,1)S(1)}, u32[]{:S(2)}, u32[]{:S(2)}) collective-permute-start(bf16[16,128,256]{2,1,0:T(8,128)(2,1)S(1)} %get-tuple-element.31), channel_id=1, source_target_pairs={{0,64},{2,66},{4,68},{6,70},{8,72},{10,74},{12,76},{14,78},{16,80}... | collective-permute-start | bytes 3145736 | tf_op jit(solution)/shard_map/ppermute | solution.py:42
  100.0 5.0 %collective-permute-start.32 = (bf16[16,128,256]{2,1,0:T(8,128)(2,1)}, bf16[16,128,256]{2,1,0:T(8,128)(2,1)}, u32[]{:S(2)}, u32[]{:S(2)}) collective-permute-start(bf16[16,128,256]{2,1,0:T(8,128)(2,1)} %get-tuple-element.27), channel_id=1, source_target_pairs={{0,16},{2,18},{4,20},{6,22},{8,24},{10,26},{12,28},{14,30},{16,0},... | collective-permute-start | bytes 3145736 | tf_op jit(solution)/shard_map/ppermute | solution.py:42
  105.0 13.1 %collective-permute-done.34.refs_2_.refs_16_ = bf16[16,128,256]{2,1,0:T(8,128)(2,1)S(1)} collective-permute-done((bf16[16,128,256]{2,1,0:T(8,128)(2,1)S(1)}, bf16[16,128,256]{2,1,0:T(8,128)(2,1)S(1)}, u32[]{:S(2)}, u32[]{:S(2)}) %collective-permute-start.34) | collective-permute-done | bytes 1048608 | tf_op jit(solution)/shard_map/ppermute | solution.py:42
  118.2 9.2 %collective-permute-start.33 = (bf16[16,128,256]{2,1,0:T(8,128)(2,1)}, bf16[16,128,256]{2,1,0:T(8,128)(2,1)}, u32[]{:S(2)}, u32[]{:S(2)}) collective-permute-start(bf16[16,128,256]{2,1,0:T(8,128)(2,1)} %get-tuple-element.28), channel_id=1, source_target_pairs={{0,24},{2,26},{4,28},{6,30},{8,0},{10,2},{12,4},{14,6},{16,8},{18,... | collective-permute-start | bytes 3145736 | tf_op jit(solution)/shard_map/ppermute | solution.py:42
  127.4 15.0 %collective-permute-done.35.refs_3_.refs_17_ = bf16[16,128,256]{2,1,0:T(8,128)(2,1)S(1)} collective-permute-done((bf16[16,128,256]{2,1,0:T(8,128)(2,1)S(1)}, bf16[16,128,256]{2,1,0:T(8,128)(2,1)S(1)}, u32[]{:S(2)}, u32[]{:S(2)}) %collective-permute-start.35) | collective-permute-done | bytes 1048608 | tf_op jit(solution)/shard_map/ppermute | solution.py:42
  145.3 4.3 %collective-permute-start.29 = (bf16[16,128,256]{2,1,0:T(8,128)(2,1)}, bf16[16,128,256]{2,1,0:T(8,128)(2,1)}, u32[]{:S(2)}, u32[]{:S(2)}) collective-permute-start(bf16[16,128,256]{2,1,0:T(8,128)(2,1)} %get-tuple-element.23), channel_id=1, source_target_pairs={{0,4},{2,6},{4,0},{6,2},{8,12},{10,14},{12,8},{14,10},{16,20},{18,... | collective-permute-start | bytes 3145736 | tf_op jit(solution)/shard_map/ppermute | solution.py:42
  165.5 3.9 %hand.5 = bf16[24,128,256]{2,1,0:T(8,128)(2,1)} custom-call(s32[24]{0:T(128)} %dynamic-slice_bitcast_fusion.refs_0_, bf16[16,128,256]{2,1,0:T(8,128)(2,1)} %copy-done.3, bf16[16,128,256]{2,1,0:T(8,128)(2,1)} %copy-done.32, bf16[16,128,256]{2,1,0:T(8,128)(2,1)} %copy-done.33, bf16[16,128,256]{2,1,0:T(8,128)(2,1)} %copy-done.34), custom_call_target="tpu_custom_call" | custom-call | tf_op jit(solution)/shard_map/hand/pallas_call | solution.py:464
  169.5 3.8 %collective-permute-start.39 = (bf16[24,128,256]{2,1,0:T(8,128)(2,1)}, bf16[24,128,256]{2,1,0:T(8,128)(2,1)}, u32[]{:S(2)}, u32[]{:S(2)}) collective-permute-start(bf16[24,128,256]{2,1,0:T(8,128)(2,1)} %hand.5), channel_id=1, source_target_pairs={{0,1},{1,0},{2,3},{3,2},{4,5},{5,4},{6,7},{7,6},{8,9},{9,8},{10,11... | collective-permute-start | bytes 4718600 | tf_op jit(solution)/shard_map/ppermute | solution.py:46
  173.3 4.3 %hand.4 = bf16[24,128,256]{2,1,0:T(8,128)(2,1)} custom-call(s32[24]{0:T(128)} %dynamic-slice_bitcast_fusion.refs_0_, bf16[16,128,256]{2,1,0:T(8,128)(2,1)} %copy-done.2, bf16[16,128,256]{2,1,0:T(8,128)(2,1)} %copy-done.35, bf16[16,128,256]{2,1,0:T(8,128)(2,1)} %collective-permute-done.32.refs_3_.refs_13_, ...), custom_call_target="tpu_custom_call" | custom-call | tf_op jit(solution)/shard_map/hand/pallas_call | solution.py:464
  177.7 12.1 %collective-permute-done.29.refs_3_.refs_9_ = bf16[16,128,256]{2,1,0:T(8,128)(2,1)} collective-permute-done((bf16[16,128,256]{2,1,0:T(8,128)(2,1)}, bf16[16,128,256]{2,1,0:T(8,128)(2,1)}, u32[]{:S(2)}, u32[]{:S(2)}) %collective-permute-start.29) | collective-permute-done | bytes 1048608 | tf_op jit(solution)/shard_map/ppermute | solution.py:42
  189.8 4.8 %collective-permute-done.30.refs_4_.refs_10_ = bf16[16,128,256]{2,1,0:T(8,128)(2,1)} collective-permute-done((bf16[16,128,256]{2,1,0:T(8,128)(2,1)}, bf16[16,128,256]{2,1,0:T(8,128)(2,1)}, u32[]{:S(2)}, u32[]{:S(2)}) %collective-permute-start.30) | collective-permute-done | bytes 1048608 | tf_op jit(solution)/shard_map/ppermute | solution.py:42
  194.6 4.0 %hand.3 = bf16[24,128,256]{2,1,0:T(8,128)(2,1)} custom-call(s32[24]{0:T(128)} %dynamic-slice_bitcast_fusion.refs_0_, bf16[16,128,256]{2,1,0:T(8,128)(2,1)} %copy-done.1, bf16[16,128,256]{2,1,0:T(8,128)(2,1)} %collective-permute-done.28.refs_2_.refs_8_, bf16[16,128,256]{2,1,0:T(8,128)(2,1)} %collective-permute-done.29.refs_3_.refs_9_, ...), custom_call_target="tpu_custom_call" | custom-call | tf_op jit(solution)/shard_map/hand/pallas_call | solution.py:464
  204.5 30.3 %attend.1 = bf16[512,768]{1,0:T(8,128)(2,1)} custom-call(s32[4]{0:T(128)} %copy-done.31, s32[2,128]{1,0:T(2,128)} %tables.1.table_ref.refs_1_, s32[4,2]{1,0:T(4,128)} %copy.9.refs_1_.refs_2_, bf16[4,6,256,128]{3,2,1,0:T(8,128)(2,1)} %copy-done, bf16[768,768]{1,0:T(8,128)(2,1)} %copy-done.27, bf16[768,768]{1,0:T(8,128)(2,1)} %copy-done.28, ...), custom_call_target="tpu_custom_call" | custom-call | tf_op jit(solution)/shard_map/attend/pallas_call | solution.py:473
  (152 shorter events, 67.8 us)
Async XLA Ops:
  14.2 30.9 %collective-permute-start.16 = (bf16[2,400,256]{2,1,0:T(8,128)(2,1)S(1)}, bf16[2,400,256]{2,1,0:T(8,128)(2,1)S(1)}, u32[]{:S(2)}, u32[]{:S(2)}) collective-permute-start(bf16[2,400,256]{2,1,0:T(8,128)(2,1)S(1)} %pad_maximum_fusion.2.refs_2_.refs_8_), channel_id=1, source_target_pairs={{0,32},{2,34},{4,36},{6,38},{8,40},{10,42},{12,44},{14,46},{16,48}... | collective-permute-start | bytes 1228808 | tf_op jit(solution)/shard_map/ppermute | solution.py:42
  15.9 17.0 %collective-permute-start.4 = (bf16[400,256]{1,0:T(8,128)(2,1)S(1)}, bf16[400,256]{1,0:T(8,128)(2,1)S(1)}, u32[]{:S(2)}, u32[]{:S(2)}) collective-permute-start(bf16[400,256]{1,0:T(8,128)(2,1)S(1)} %collective-permute-done.3), channel_id=1, source_target_pairs={{0,2},{2,4},{4,6},{6,0},{8,10},{10,12},{12,14},{14,8},{16,18},{18,... | collective-permute-start | bytes 614408 | tf_op jit(solution)/shard_map/ppermute | solution.py:42
  17.1 13.1 %collective-permute-start.1 = (bf16[400,256]{1,0:T(8,128)(2,1)S(1)}, bf16[400,256]{1,0:T(8,128)(2,1)S(1)}, u32[]{:S(2)}, u32[]{:S(2)}) collective-permute-start(bf16[400,256]{1,0:T(8,128)(2,1)S(1)} %collective-permute-done), channel_id=1, source_target_pairs={{0,32},{2,34},{4,36},{6,38},{8,40},{10,42},{12,44},{14,46},{16,48}... | collective-permute-start | bytes 614408 | tf_op jit(solution)/shard_map/ppermute | solution.py:42
  17.8 27.4 %collective-permute-start.22 = (bf16[2,400,256]{2,1,0:T(8,128)(2,1)S(1)}, bf16[2,400,256]{2,1,0:T(8,128)(2,1)S(1)}, u32[]{:S(2)}, u32[]{:S(2)}) collective-permute-start(bf16[2,400,256]{2,1,0:T(8,128)(2,1)S(1)} %pad_maximum_fusion.4.refs_4_.refs_16_), channel_id=1, source_target_pairs={{0,2},{2,4},{4,6},{6,0},{8,10},{10,12},{12,14},{14,8},{16,18},{18,... | collective-permute-start | bytes 1228808 | tf_op jit(solution)/shard_map/ppermute | solution.py:42
  19.0 26.2 %collective-permute-start.10 = (bf16[2,400,256]{2,1,0:T(8,128)(2,1)S(1)}, bf16[2,400,256]{2,1,0:T(8,128)(2,1)}, u32[]{:S(2)}, u32[]{:S(2)}) collective-permute-start(bf16[2,400,256]{2,1,0:T(8,128)(2,1)S(1)} %pad_maximum_fusion.refs_0_), channel_id=1, source_target_pairs={{0,8},{2,10},{4,12},{6,14},{8,16},{10,18},{12,20},{14,22},{16,24},... | collective-permute-start | bytes 1228808 | tf_op jit(solution)/shard_map/ppermute | solution.py:42
  43.9 11.5 %collective-permute-start.27 = (bf16[2,400,256]{2,1,0:T(8,128)(2,1)S(1)}, bf16[2,400,256]{2,1,0:T(8,128)(2,1)S(1)}, u32[]{:S(2)}, u32[]{:S(2)}) collective-permute-start(bf16[2,400,256]{2,1,0:T(8,128)(2,1)S(1)} %pad_maximum_fusion.4.refs_4_.refs_16_), channel_id=1, source_target_pairs={{0,6},{2,0},{4,2},{6,4},{8,14},{10,8},{12,10},{14,12},{16,22},{18,... | collective-permute-start | bytes 1228808 | tf_op jit(solution)/shard_map/ppermute | solution.py:42
  45.2 11.0 %collective-permute-start.15 = (bf16[2,400,256]{2,1,0:T(8,128)(2,1)S(1)}, bf16[2,400,256]{2,1,0:T(8,128)(2,1)S(1)}, u32[]{:S(2)}, u32[]{:S(2)}) collective-permute-start(bf16[2,400,256]{2,1,0:T(8,128)(2,1)S(1)} %pad_maximum_fusion.refs_0_), channel_id=1, source_target_pairs={{0,24},{2,26},{4,28},{6,30},{8,0},{10,2},{12,4},{14,6},{16,8},{18,... | collective-permute-start | bytes 1228808 | tf_op jit(solution)/shard_map/ppermute | solution.py:42
  45.2 19.3 %collective-permute-start.13 = (bf16[2,400,256]{2,1,0:T(8,128)(2,1)S(1)}, bf16[2,400,256]{2,1,0:T(8,128)(2,1)}, u32[]{:S(2)}, u32[]{:S(2)}) collective-permute-start(bf16[2,400,256]{2,1,0:T(8,128)(2,1)S(1)} %pad_maximum_fusion.1.refs_1_), channel_id=1, source_target_pairs={{0,24},{2,26},{4,28},{6,30},{8,0},{10,2},{12,4},{14,6},{16,8},{18,... | collective-permute-start | bytes 1228808 | tf_op jit(solution)/shard_map/ppermute | solution.py:42
  45.3 19.4 %collective-permute-start.19 = (bf16[2,400,256]{2,1,0:T(8,128)(2,1)S(1)}, bf16[2,400,256]{2,1,0:T(8,128)(2,1)}, u32[]{:S(2)}, u32[]{:S(2)}) collective-permute-start(bf16[2,400,256]{2,1,0:T(8,128)(2,1)S(1)} %pad_maximum_fusion.3.refs_3_.refs_9_), channel_id=1, source_target_pairs={{0,96},{2,98},{4,100},{6,102},{8,104},{10,106},{12,108},{14,110},{... | collective-permute-start | bytes 1228808 | tf_op jit(solution)/shard_map/ppermute | solution.py:42
  64.6 12.7 %collective-permute-start.18 = (bf16[2,400,256]{2,1,0:T(8,128)(2,1)S(1)}, bf16[2,400,256]{2,1,0:T(8,128)(2,1)S(1)}, u32[]{:S(2)}, u32[]{:S(2)}) collective-permute-start(bf16[2,400,256]{2,1,0:T(8,128)(2,1)S(1)} %collective-permute-done.16.refs_10_), channel_id=1, source_target_pairs={{0,32},{2,34},{4,36},{6,38},{8,40},{10,42},{12,44},{14,46},{16,48}... | collective-permute-start | bytes 1228808 | tf_op jit(solution)/shard_map/ppermute | solution.py:42
  64.6 19.4 %collective-permute-start.24 = (bf16[2,400,256]{2,1,0:T(8,128)(2,1)S(1)}, bf16[2,400,256]{2,1,0:T(8,128)(2,1)}, u32[]{:S(2)}, u32[]{:S(2)}) collective-permute-start(bf16[2,400,256]{2,1,0:T(8,128)(2,1)S(1)} %collective-permute-done.22.refs_18_), channel_id=1, source_target_pairs={{0,2},{2,4},{4,6},{6,0},{8,10},{10,12},{12,14},{14,8},{16,18},{18,... | collective-permute-start | bytes 1228808 | tf_op jit(solution)/shard_map/ppermute | solution.py:42
  67.4 16.7 %collective-permute-start.12 = (bf16[2,400,256]{2,1,0:T(8,128)(2,1)}, bf16[2,400,256]{2,1,0:T(8,128)(2,1)}, u32[]{:S(2)}, u32[]{:S(2)}) collective-permute-start(bf16[2,400,256]{2,1,0:T(8,128)(2,1)} %collective-permute-done.10.refs_2_), channel_id=1, source_target_pairs={{0,8},{2,10},{4,12},{6,14},{8,16},{10,18},{12,20},{14,22},{16,24},... | collective-permute-start | bytes 1228808 | tf_op jit(solution)/shard_map/ppermute | solution.py:42
  68.1 15.9 %collective-permute-start.14 = (bf16[2,400,256]{2,1,0:T(8,128)(2,1)}, bf16[2,400,256]{2,1,0:T(8,128)(2,1)}, u32[]{:S(2)}, u32[]{:S(2)}) collective-permute-start(bf16[2,400,256]{2,1,0:T(8,128)(2,1)} %collective-permute-done.13.refs_7_), channel_id=1, source_target_pairs={{0,24},{2,26},{4,28},{6,30},{8,0},{10,2},{12,4},{14,6},{16,8},{18,... | collective-permute-start | bytes 1228808 | tf_op jit(solution)/shard_map/ppermute | solution.py:42
  97.0 21.1 %collective-permute-start.34 = (bf16[16,128,256]{2,1,0:T(8,128)(2,1)S(1)}, bf16[16,128,256]{2,1,0:T(8,128)(2,1)S(1)}, u32[]{:S(2)}, u32[]{:S(2)}) collective-permute-start(bf16[16,128,256]{2,1,0:T(8,128)(2,1)S(1)} %get-tuple-element.30), channel_id=1, source_target_pairs={{0,32},{2,34},{4,36},{6,38},{8,40},{10,42},{12,44},{14,46},{16,48}... | collective-permute-start | bytes 3145736 | tf_op jit(solution)/shard_map/ppermute | solution.py:42
  97.2 45.1 %collective-permute-start.35 = (bf16[16,128,256]{2,1,0:T(8,128)(2,1)S(1)}, bf16[16,128,256]{2,1,0:T(8,128)(2,1)S(1)}, u32[]{:S(2)}, u32[]{:S(2)}) collective-permute-start(bf16[16,128,256]{2,1,0:T(8,128)(2,1)S(1)} %get-tuple-element.31), channel_id=1, source_target_pairs={{0,64},{2,66},{4,68},{6,70},{8,72},{10,74},{12,76},{14,78},{16,80}... | collective-permute-start | bytes 3145736 | tf_op jit(solution)/shard_map/ppermute | solution.py:42
  100.0 45.3 %collective-permute-start.36 = (bf16[16,128,256]{2,1,0:T(8,128)(2,1)S(1)}, bf16[16,128,256]{2,1,0:T(8,128)(2,1)S(1)}, u32[]{:S(2)}, u32[]{:S(2)}) collective-permute-start(bf16[16,128,256]{2,1,0:T(8,128)(2,1)S(1)} %get-tuple-element.32), channel_id=1, source_target_pairs={{0,96},{2,98},{4,100},{6,102},{8,104},{10,106},{12,108},{14,110},{... | collective-permute-start | bytes 3145736 | tf_op jit(solution)/shard_map/ppermute | solution.py:42
  100.0 49.6 %collective-permute-start.31 = (bf16[16,128,256]{2,1,0:T(8,128)(2,1)S(1)}, bf16[16,128,256]{2,1,0:T(8,128)(2,1)S(1)}, u32[]{:S(2)}, u32[]{:S(2)}) collective-permute-start(bf16[16,128,256]{2,1,0:T(8,128)(2,1)S(1)} %get-tuple-element.26), channel_id=1, source_target_pairs={{0,8},{2,10},{4,12},{6,14},{8,16},{10,18},{12,20},{14,22},{16,24},... | collective-permute-start | bytes 3145736 | tf_op jit(solution)/shard_map/ppermute | solution.py:42
  100.0 69.5 %collective-permute-start.32 = (bf16[16,128,256]{2,1,0:T(8,128)(2,1)}, bf16[16,128,256]{2,1,0:T(8,128)(2,1)}, u32[]{:S(2)}, u32[]{:S(2)}) collective-permute-start(bf16[16,128,256]{2,1,0:T(8,128)(2,1)} %get-tuple-element.27), channel_id=1, source_target_pairs={{0,16},{2,18},{4,20},{6,22},{8,24},{10,26},{12,28},{14,30},{16,0},... | collective-permute-start | bytes 3145736 | tf_op jit(solution)/shard_map/ppermute | solution.py:42
  118.2 55.1 %collective-permute-start.33 = (bf16[16,128,256]{2,1,0:T(8,128)(2,1)}, bf16[16,128,256]{2,1,0:T(8,128)(2,1)}, u32[]{:S(2)}, u32[]{:S(2)}) collective-permute-start(bf16[16,128,256]{2,1,0:T(8,128)(2,1)} %get-tuple-element.28), channel_id=1, source_target_pairs={{0,24},{2,26},{4,28},{6,30},{8,0},{10,2},{12,4},{14,6},{16,8},{18,... | collective-permute-start | bytes 3145736 | tf_op jit(solution)/shard_map/ppermute | solution.py:42
  142.4 35.3 %collective-permute-start.28 = (bf16[16,128,256]{2,1,0:T(8,128)(2,1)}, bf16[16,128,256]{2,1,0:T(8,128)(2,1)}, u32[]{:S(2)}, u32[]{:S(2)}) collective-permute-start(bf16[16,128,256]{2,1,0:T(8,128)(2,1)} %get-tuple-element.22), channel_id=1, source_target_pairs={{0,2},{2,4},{4,6},{6,0},{8,10},{10,12},{12,14},{14,8},{16,18},{18,... | collective-permute-start | bytes 3145736 | tf_op jit(solution)/shard_map/ppermute | solution.py:42
  145.3 44.5 %collective-permute-start.29 = (bf16[16,128,256]{2,1,0:T(8,128)(2,1)}, bf16[16,128,256]{2,1,0:T(8,128)(2,1)}, u32[]{:S(2)}, u32[]{:S(2)}) collective-permute-start(bf16[16,128,256]{2,1,0:T(8,128)(2,1)} %get-tuple-element.23), channel_id=1, source_target_pairs={{0,4},{2,6},{4,0},{6,2},{8,12},{10,14},{12,8},{14,10},{16,20},{18,... | collective-permute-start | bytes 3145736 | tf_op jit(solution)/shard_map/ppermute | solution.py:42
  150.7 43.9 %collective-permute-start.30 = (bf16[16,128,256]{2,1,0:T(8,128)(2,1)}, bf16[16,128,256]{2,1,0:T(8,128)(2,1)}, u32[]{:S(2)}, u32[]{:S(2)}) collective-permute-start(bf16[16,128,256]{2,1,0:T(8,128)(2,1)} %get-tuple-element.24), channel_id=1, source_target_pairs={{0,6},{2,0},{4,2},{6,4},{8,14},{10,8},{12,10},{14,12},{16,22},{18,... | collective-permute-start | bytes 3145736 | tf_op jit(solution)/shard_map/ppermute | solution.py:42
  169.5 35.0 %collective-permute-start.39 = (bf16[24,128,256]{2,1,0:T(8,128)(2,1)}, bf16[24,128,256]{2,1,0:T(8,128)(2,1)}, u32[]{:S(2)}, u32[]{:S(2)}) collective-permute-start(bf16[24,128,256]{2,1,0:T(8,128)(2,1)} %hand.5), channel_id=1, source_target_pairs={{0,1},{1,0},{2,3},{3,2},{4,5},{5,4},{6,7},{7,6},{8,9},{9,8},{10,11... | collective-permute-start | bytes 4718600 | tf_op jit(solution)/shard_map/ppermute | solution.py:46
  177.6 26.9 %collective-permute-start.38 = (bf16[24,128,256]{2,1,0:T(8,128)(2,1)}, bf16[24,128,256]{2,1,0:T(8,128)(2,1)}, u32[]{:S(2)}, u32[]{:S(2)}) collective-permute-start(bf16[24,128,256]{2,1,0:T(8,128)(2,1)} %hand.4), channel_id=1, source_target_pairs={{0,1},{1,0},{2,3},{3,2},{4,5},{5,4},{6,7},{7,6},{8,9},{9,8},{10,11... | collective-permute-start | bytes 4718600 | tf_op jit(solution)/shard_map/ppermute | solution.py:46
  (52 other events, 307.1 us)

commit v5 on v4

--- a/solution.py
+++ b/solution.py
@@ -148,15 +148,16 @@
 def fetch_parts(code, arrived, target, sem_of):
     away = (lax.shift_right_logical(code, 4), lax.shift_right_logical(code, 2) & 3, code & 3)
     for part, (across, first, second) in enumerate(ROUTES):
-        for d in range(SIDE):
-
-            @pl.when(away[across] == d)
-            def _():
-                pltpu.make_async_copy(
-                    arrived[part][d].at[away[second] * 4 + away[first]],
-                    target(part),
-                    sem_of(part),
-                ).start()
+        place = away[second] * 4 + away[first]
+
+        def bring(d):
+            pltpu.make_async_copy(arrived[part][d].at[place], target(part), sem_of(part)).start()
+            return 0
+
+        def either(d):
+            return lambda: lax.cond(away[across] == d, lambda: bring(d), lambda: bring(d + 1))
+
+        lax.cond(away[across] < 2, either(0), either(2))
 
 
 def hand_kernel(part, code_ref, *refs):

time: 240 us -> 239 us (level)
  no operation moved by 1% of the time
where the time goes in v5:
time: 239 us; the launch traced here: 235 us
  waiting for transfers between devices  92.5 us (39%)
  starting transfers between devices  58.3 us (24%)
  Pallas kernels  52.7 us (22%)
  local copies, waits for them, and re-layouts  29.7 us (12%)
    ppermute x36, waiting for transfers between devices, shift(): return lax.ppermute(value, 'pb', pairs)  92.5 us
    ppermute x36, starting transfers between devices, shift(): return lax.ppermute(value, 'pb', pairs)  49.5 us
    pallas_call x1, Pallas kernels, on_device(): pl.pallas_call(lambda *refs: attend_kernel(True, True, *refs), out_shape=...  30.3 us
    unnamed x73, local copies, waits for them, and re-layouts  28 us
    pallas_call x3, Pallas kernels, on_device(): pl.pallas_call(lambda *refs: hand_kernel(part, *refs), out_shape=jax.Shap...  12.3 us
    ppermute x4, starting transfers between devices, swap(): return lax.ppermute(value, 'ka', [(0, 1), (1, 0)])  8.8 us
  transfers between devices with their start and end apart: 40, of which 16 were waited for; matrix products, arithmetic and copies ran while one was open for 0% of the time, Pallas kernels for 7%

profile of v5, /device:TPU:1, one launch (start us, length us, event | category | flops | bytes accessed | tf_op | source)
XLA Modules:
  0.0 234.9 jit_solution(17797632320965923121)
XLA Ops:
  19.7 10.6 %collective-permute-done.1 = bf16[400,256]{1,0:T(8,128)(2,1)S(1)} collective-permute-done((bf16[400,256]{1,0:T(8,128)(2,1)S(1)}, bf16[400,256]{1,0:T(8,128)(2,1)S(1)}, u32[]{:S(2)}, u32[]{:S(2)}) %collective-permute-start.1) | collective-permute-done | bytes 204832 | tf_op jit(solution)/shard_map/ppermute | solution.py:42
  30.3 2.7 %collective-permute-start.8 = (bf16[400,256]{1,0:T(8,128)(2,1)S(1)}, bf16[400,256]{1,0:T(8,128)(2,1)S(1)}, u32[]{:S(2)}, u32[]{:S(2)}) collective-permute-start(bf16[400,256]{1,0:T(8,128)(2,1)S(1)} %get-tuple-element.37), channel_id=1, source_target_pairs={{0,24},{2,26},{4,28},{6,30},{8,0},{10,2},{12,4},{14,6},{16,8},{18,... | collective-permute-start | bytes 614408 | tf_op jit(solution)/shard_map/ppermute | solution.py:42
  33.0 2.6 %collective-permute-done.8 = bf16[400,256]{1,0:T(8,128)(2,1)S(1)} collective-permute-done((bf16[400,256]{1,0:T(8,128)(2,1)S(1)}, bf16[400,256]{1,0:T(8,128)(2,1)S(1)}, u32[]{:S(2)}, u32[]{:S(2)}) %collective-permute-start.8) | collective-permute-done | bytes 204832 | tf_op jit(solution)/shard_map/ppermute | solution.py:42
  35.6 3.1 %collective-permute-done.7 = bf16[400,256]{1,0:T(8,128)(2,1)S(1)} collective-permute-done((bf16[400,256]{1,0:T(8,128)(2,1)S(1)}, bf16[400,256]{1,0:T(8,128)(2,1)S(1)}, u32[]{:S(2)}, u32[]{:S(2)}) %collective-permute-start.7) | collective-permute-done | bytes 204832 | tf_op jit(solution)/shard_map/ppermute | solution.py:42
  38.8 3.6 %collective-permute-start.9 = (s32[16,128]{1,0:T(8,128)S(1)}, s32[16,128]{1,0:T(8,128)S(1)}, u32[]{:S(2)}, u32[]{:S(2)}) collective-permute-start(s32[16,128]{1,0:T(8,128)S(1)} %notes.1), channel_id=1, source_target_pairs={{0,1},{1,0},{2,3},{3,2},{4,5},{5,4},{6,7},{7,6},{8,9},{9,8},{10,11... | collective-permute-start | bytes 24584 | tf_op jit(solution)/shard_map/ppermute | solution.py:46
  46.1 7.2 %collective-permute-done.21.refs_14_ = bf16[2,400,256]{2,1,0:T(8,128)(2,1)S(1)} collective-permute-done((bf16[2,400,256]{2,1,0:T(8,128)(2,1)S(1)}, bf16[2,400,256]{2,1,0:T(8,128)(2,1)S(1)}, u32[]{:S(2)}, u32[]{:S(2)}) %collective-permute-start.21) | collective-permute-done | bytes 409632 | tf_op jit(solution)/shard_map/ppermute | solution.py:42
  56.9 7.5 %collective-permute-done.13.refs_7_ = bf16[2,400,256]{2,1,0:T(8,128)(2,1)} collective-permute-done((bf16[2,400,256]{2,1,0:T(8,128)(2,1)S(1)}, bf16[2,400,256]{2,1,0:T(8,128)(2,1)}, u32[]{:S(2)}, u32[]{:S(2)}) %collective-permute-start.13) | collective-permute-done | bytes 409632 | tf_op jit(solution)/shard_map/ppermute | solution.py:42
  68.1 2.7 %collective-permute-start.14 = (bf16[2,400,256]{2,1,0:T(8,128)(2,1)}, bf16[2,400,256]{2,1,0:T(8,128)(2,1)}, u32[]{:S(2)}, u32[]{:S(2)}) collective-permute-start(bf16[2,400,256]{2,1,0:T(8,128)(2,1)} %collective-permute-done.13.refs_7_), channel_id=1, source_target_pairs={{0,24},{2,26},{4,28},{6,30},{8,0},{10,2},{12,4},{14,6},{16,8},{18,... | collective-permute-start | bytes 1228808 | tf_op jit(solution)/shard_map/ppermute | solution.py:42
  70.8 4.5 %collective-permute-done.23.refs_19_ = bf16[2,400,256]{2,1,0:T(8,128)(2,1)S(1)} collective-permute-done((bf16[2,400,256]{2,1,0:T(8,128)(2,1)S(1)}, bf16[2,400,256]{2,1,0:T(8,128)(2,1)S(1)}, u32[]{:S(2)}, u32[]{:S(2)}) %collective-permute-start.23) | collective-permute-done | bytes 409632 | tf_op jit(solution)/shard_map/ppermute | solution.py:42
  79.0 5.1 %collective-permute-done.24.refs_20_ = bf16[2,400,256]{2,1,0:T(8,128)(2,1)} collective-permute-done((bf16[2,400,256]{2,1,0:T(8,128)(2,1)S(1)}, bf16[2,400,256]{2,1,0:T(8,128)(2,1)}, u32[]{:S(2)}, u32[]{:S(2)}) %collective-permute-start.24) | collective-permute-done | bytes 409632 | tf_op jit(solution)/shard_map/ppermute | solution.py:42
  92.5 4.5 %select.28 = (bf16[16,128,256]{2,1,0:T(8,128)(2,1)}, bf16[16,128,256]{2,1,0:T(8,128)(2,1)}, bf16[16,128,256]{2,1,0:T(8,128)(2,1)}, bf16[16,128,256]{2,1,0:T(8,12...) custom-call(s32[4]{0:T(128)S(1)} %pad_add_fusion.me_ref.refs_0_, ...), custom_call_target="tpu_custom_call" | custom-call | tf_op jit(solution)/shard_map/select/pallas_call | solution.py:423
  97.2 2.8 %collective-permute-start.35 = (bf16[16,128,256]{2,1,0:T(8,128)(2,1)S(1)}, bf16[16,128,256]{2,1,0:T(8,128)(2,1)S(1)}, u32[]{:S(2)}, u32[]{:S(2)}) collective-permute-start(bf16[16,128,256]{2,1,0:T(8,128)(2,1)S(1)} %get-tuple-element.31), channel_id=1, source_target_pairs={{0,64},{2,66},{4,68},{6,70},{8,72},{10,74},{12,76},{14,78},{16,80}... | collective-permute-start | bytes 3145736 | tf_op jit(solution)/shard_map/ppermute | solution.py:42
  100.0 5.0 %collective-permute-start.32 = (bf16[16,128,256]{2,1,0:T(8,128)(2,1)}, bf16[16,128,256]{2,1,0:T(8,128)(2,1)}, u32[]{:S(2)}, u32[]{:S(2)}) collective-permute-start(bf16[16,128,256]{2,1,0:T(8,128)(2,1)} %get-tuple-element.27), channel_id=1, source_target_pairs={{0,16},{2,18},{4,20},{6,22},{8,24},{10,26},{12,28},{14,30},{16,0},... | collective-permute-start | bytes 3145736 | tf_op jit(solution)/shard_map/ppermute | solution.py:42
  105.0 13.1 %collective-permute-done.34.refs_2_.refs_16_ = bf16[16,128,256]{2,1,0:T(8,128)(2,1)S(1)} collective-permute-done((bf16[16,128,256]{2,1,0:T(8,128)(2,1)S(1)}, bf16[16,128,256]{2,1,0:T(8,128)(2,1)S(1)}, u32[]{:S(2)}, u32[]{:S(2)}) %collective-permute-start.34) | collective-permute-done | bytes 1048608 | tf_op jit(solution)/shard_map/ppermute | solution.py:42
  118.2 9.2 %collective-permute-start.33 = (bf16[16,128,256]{2,1,0:T(8,128)(2,1)}, bf16[16,128,256]{2,1,0:T(8,128)(2,1)}, u32[]{:S(2)}, u32[]{:S(2)}) collective-permute-start(bf16[16,128,256]{2,1,0:T(8,128)(2,1)} %get-tuple-element.28), channel_id=1, source_target_pairs={{0,24},{2,26},{4,28},{6,30},{8,0},{10,2},{12,4},{14,6},{16,8},{18,... | collective-permute-start | bytes 3145736 | tf_op jit(solution)/shard_map/ppermute | solution.py:42
  127.4 15.0 %collective-permute-done.35.refs_3_.refs_17_ = bf16[16,128,256]{2,1,0:T(8,128)(2,1)S(1)} collective-permute-done((bf16[16,128,256]{2,1,0:T(8,128)(2,1)S(1)}, bf16[16,128,256]{2,1,0:T(8,128)(2,1)S(1)}, u32[]{:S(2)}, u32[]{:S(2)}) %collective-permute-start.35) | collective-permute-done | bytes 1048608 | tf_op jit(solution)/shard_map/ppermute | solution.py:42
  145.3 4.3 %collective-permute-start.29 = (bf16[16,128,256]{2,1,0:T(8,128)(2,1)}, bf16[16,128,256]{2,1,0:T(8,128)(2,1)}, u32[]{:S(2)}, u32[]{:S(2)}) collective-permute-start(bf16[16,128,256]{2,1,0:T(8,128)(2,1)} %get-tuple-element.23), channel_id=1, source_target_pairs={{0,4},{2,6},{4,0},{6,2},{8,12},{10,14},{12,8},{14,10},{16,20},{18,... | collective-permute-start | bytes 3145736 | tf_op jit(solution)/shard_map/ppermute | solution.py:42
  165.5 3.9 %hand.5 = bf16[24,128,256]{2,1,0:T(8,128)(2,1)} custom-call(s32[24]{0:T(128)} %dynamic-slice_bitcast_fusion.refs_0_, bf16[16,128,256]{2,1,0:T(8,128)(2,1)} %copy-done.3, bf16[16,128,256]{2,1,0:T(8,128)(2,1)} %copy-done.32, bf16[16,128,256]{2,1,0:T(8,128)(2,1)} %copy-done.33, bf16[16,128,256]{2,1,0:T(8,128)(2,1)} %copy-done.34), custom_call_target="tpu_custom_call" | custom-call | tf_op jit(solution)/shard_map/hand/pallas_call | solution.py:465
  169.5 3.8 %collective-permute-start.39 = (bf16[24,128,256]{2,1,0:T(8,128)(2,1)}, bf16[24,128,256]{2,1,0:T(8,128)(2,1)}, u32[]{:S(2)}, u32[]{:S(2)}) collective-permute-start(bf16[24,128,256]{2,1,0:T(8,128)(2,1)} %hand.5), channel_id=1, source_target_pairs={{0,1},{1,0},{2,3},{3,2},{4,5},{5,4},{6,7},{7,6},{8,9},{9,8},{10,11... | collective-permute-start | bytes 4718600 | tf_op jit(solution)/shard_map/ppermute | solution.py:46
  173.3 4.3 %hand.4 = bf16[24,128,256]{2,1,0:T(8,128)(2,1)} custom-call(s32[24]{0:T(128)} %dynamic-slice_bitcast_fusion.refs_0_, bf16[16,128,256]{2,1,0:T(8,128)(2,1)} %copy-done.2, bf16[16,128,256]{2,1,0:T(8,128)(2,1)} %copy-done.35, bf16[16,128,256]{2,1,0:T(8,128)(2,1)} %collective-permute-done.32.refs_3_.refs_13_, ...), custom_call_target="tpu_custom_call" | custom-call | tf_op jit(solution)/shard_map/hand/pallas_call | solution.py:465
  177.7 12.1 %collective-permute-done.29.refs_3_.refs_9_ = bf16[16,128,256]{2,1,0:T(8,128)(2,1)} collective-permute-done((bf16[16,128,256]{2,1,0:T(8,128)(2,1)}, bf16[16,128,256]{2,1,0:T(8,128)(2,1)}, u32[]{:S(2)}, u32[]{:S(2)}) %collective-permute-start.29) | collective-permute-done | bytes 1048608 | tf_op jit(solution)/shard_map/ppermute | solution.py:42
  189.8 4.8 %collective-permute-done.30.refs_4_.refs_10_ = bf16[16,128,256]{2,1,0:T(8,128)(2,1)} collective-permute-done((bf16[16,128,256]{2,1,0:T(8,128)(2,1)}, bf16[16,128,256]{2,1,0:T(8,128)(2,1)}, u32[]{:S(2)}, u32[]{:S(2)}) %collective-permute-start.30) | collective-permute-done | bytes 1048608 | tf_op jit(solution)/shard_map/ppermute | solution.py:42
  194.6 4.0 %hand.3 = bf16[24,128,256]{2,1,0:T(8,128)(2,1)} custom-call(s32[24]{0:T(128)} %dynamic-slice_bitcast_fusion.refs_0_, bf16[16,128,256]{2,1,0:T(8,128)(2,1)} %copy-done.1, bf16[16,128,256]{2,1,0:T(8,128)(2,1)} %collective-permute-done.28.refs_2_.refs_8_, bf16[16,128,256]{2,1,0:T(8,128)(2,1)} %collective-permute-done.29.refs_3_.refs_9_, ...), custom_call_target="tpu_custom_call" | custom-call | tf_op jit(solution)/shard_map/hand/pallas_call | solution.py:465
  204.5 30.3 %attend.1 = bf16[512,768]{1,0:T(8,128)(2,1)} custom-call(s32[4]{0:T(128)} %copy-done.31, s32[2,128]{1,0:T(2,128)} %tables.1.table_ref.refs_1_, s32[4,2]{1,0:T(4,128)} %copy.9.refs_1_.refs_2_, bf16[4,6,256,128]{3,2,1,0:T(8,128)(2,1)} %copy-done, bf16[768,768]{1,0:T(8,128)(2,1)} %copy-done.27, bf16[768,768]{1,0:T(8,128)(2,1)} %copy-done.28, ...), custom_call_target="tpu_custom_call" | custom-call | tf_op jit(solution)/shard_map/attend/pallas_call | solution.py:474
  (152 shorter events, 67.8 us)
Async XLA Ops:
  14.2 30.9 %collective-permute-start.16 = (bf16[2,400,256]{2,1,0:T(8,128)(2,1)S(1)}, bf16[2,400,256]{2,1,0:T(8,128)(2,1)S(1)}, u32[]{:S(2)}, u32[]{:S(2)}) collective-permute-start(bf16[2,400,256]{2,1,0:T(8,128)(2,1)S(1)} %pad_maximum_fusion.2.refs_2_.refs_8_), channel_id=1, source_target_pairs={{0,32},{2,34},{4,36},{6,38},{8,40},{10,42},{12,44},{14,46},{16,48}... | collective-permute-start | bytes 1228808 | tf_op jit(solution)/shard_map/ppermute | solution.py:42
  15.9 17.0 %collective-permute-start.4 = (bf16[400,256]{1,0:T(8,128)(2,1)S(1)}, bf16[400,256]{1,0:T(8,128)(2,1)S(1)}, u32[]{:S(2)}, u32[]{:S(2)}) collective-permute-start(bf16[400,256]{1,0:T(8,128)(2,1)S(1)} %collective-permute-done.3), channel_id=1, source_target_pairs={{0,2},{2,4},{4,6},{6,0},{8,10},{10,12},{12,14},{14,8},{16,18},{18,... | collective-permute-start | bytes 614408 | tf_op jit(solution)/shard_map/ppermute | solution.py:42
  17.1 13.1 %collective-permute-start.1 = (bf16[400,256]{1,0:T(8,128)(2,1)S(1)}, bf16[400,256]{1,0:T(8,128)(2,1)S(1)}, u32[]{:S(2)}, u32[]{:S(2)}) collective-permute-start(bf16[400,256]{1,0:T(8,128)(2,1)S(1)} %collective-permute-done), channel_id=1, source_target_pairs={{0,32},{2,34},{4,36},{6,38},{8,40},{10,42},{12,44},{14,46},{16,48}... | collective-permute-start | bytes 614408 | tf_op jit(solution)/shard_map/ppermute | solution.py:42
  17.8 27.4 %collective-permute-start.22 = (bf16[2,400,256]{2,1,0:T(8,128)(2,1)S(1)}, bf16[2,400,256]{2,1,0:T(8,128)(2,1)S(1)}, u32[]{:S(2)}, u32[]{:S(2)}) collective-permute-start(bf16[2,400,256]{2,1,0:T(8,128)(2,1)S(1)} %pad_maximum_fusion.4.refs_4_.refs_16_), channel_id=1, source_target_pairs={{0,2},{2,4},{4,6},{6,0},{8,10},{10,12},{12,14},{14,8},{16,18},{18,... | collective-permute-start | bytes 1228808 | tf_op jit(solution)/shard_map/ppermute | solution.py:42
  19.0 26.2 %collective-permute-start.10 = (bf16[2,400,256]{2,1,0:T(8,128)(2,1)S(1)}, bf16[2,400,256]{2,1,0:T(8,128)(2,1)}, u32[]{:S(2)}, u32[]{:S(2)}) collective-permute-start(bf16[2,400,256]{2,1,0:T(8,128)(2,1)S(1)} %pad_maximum_fusion.refs_0_), channel_id=1, source_target_pairs={{0,8},{2,10},{4,12},{6,14},{8,16},{10,18},{12,20},{14,22},{16,24},... | collective-permute-start | bytes 1228808 | tf_op jit(solution)/shard_map/ppermute | solution.py:42
  43.9 11.5 %collective-permute-start.27 = (bf16[2,400,256]{2,1,0:T(8,128)(2,1)S(1)}, bf16[2,400,256]{2,1,0:T(8,128)(2,1)S(1)}, u32[]{:S(2)}, u32[]{:S(2)}) collective-permute-start(bf16[2,400,256]{2,1,0:T(8,128)(2,1)S(1)} %pad_maximum_fusion.4.refs_4_.refs_16_), channel_id=1, source_target_pairs={{0,6},{2,0},{4,2},{6,4},{8,14},{10,8},{12,10},{14,12},{16,22},{18,... | collective-permute-start | bytes 1228808 | tf_op jit(solution)/shard_map/ppermute | solution.py:42
  45.2 11.0 %collective-permute-start.15 = (bf16[2,400,256]{2,1,0:T(8,128)(2,1)S(1)}, bf16[2,400,256]{2,1,0:T(8,128)(2,1)S(1)}, u32[]{:S(2)}, u32[]{:S(2)}) collective-permute-start(bf16[2,400,256]{2,1,0:T(8,128)(2,1)S(1)} %pad_maximum_fusion.refs_0_), channel_id=1, source_target_pairs={{0,24},{2,26},{4,28},{6,30},{8,0},{10,2},{12,4},{14,6},{16,8},{18,... | collective-permute-start | bytes 1228808 | tf_op jit(solution)/shard_map/ppermute | solution.py:42
  45.2 19.3 %collective-permute-start.13 = (bf16[2,400,256]{2,1,0:T(8,128)(2,1)S(1)}, bf16[2,400,256]{2,1,0:T(8,128)(2,1)}, u32[]{:S(2)}, u32[]{:S(2)}) collective-permute-start(bf16[2,400,256]{2,1,0:T(8,128)(2,1)S(1)} %pad_maximum_fusion.1.refs_1_), channel_id=1, source_target_pairs={{0,24},{2,26},{4,28},{6,30},{8,0},{10,2},{12,4},{14,6},{16,8},{18,... | collective-permute-start | bytes 1228808 | tf_op jit(solution)/shard_map/ppermute | solution.py:42
  45.3 19.4 %collective-permute-start.19 = (bf16[2,400,256]{2,1,0:T(8,128)(2,1)S(1)}, bf16[2,400,256]{2,1,0:T(8,128)(2,1)}, u32[]{:S(2)}, u32[]{:S(2)}) collective-permute-start(bf16[2,400,256]{2,1,0:T(8,128)(2,1)S(1)} %pad_maximum_fusion.3.refs_3_.refs_9_), channel_id=1, source_target_pairs={{0,96},{2,98},{4,100},{6,102},{8,104},{10,106},{12,108},{14,110},{... | collective-permute-start | bytes 1228808 | tf_op jit(solution)/shard_map/ppermute | solution.py:42
  64.6 12.7 %collective-permute-start.18 = (bf16[2,400,256]{2,1,0:T(8,128)(2,1)S(1)}, bf16[2,400,256]{2,1,0:T(8,128)(2,1)S(1)}, u32[]{:S(2)}, u32[]{:S(2)}) collective-permute-start(bf16[2,400,256]{2,1,0:T(8,128)(2,1)S(1)} %collective-permute-done.16.refs_10_), channel_id=1, source_target_pairs={{0,32},{2,34},{4,36},{6,38},{8,40},{10,42},{12,44},{14,46},{16,48}... | collective-permute-start | bytes 1228808 | tf_op jit(solution)/shard_map/ppermute | solution.py:42
  64.6 19.4 %collective-permute-start.24 = (bf16[2,400,256]{2,1,0:T(8,128)(2,1)S(1)}, bf16[2,400,256]{2,1,0:T(8,128)(2,1)}, u32[]{:S(2)}, u32[]{:S(2)}) collective-permute-start(bf16[2,400,256]{2,1,0:T(8,128)(2,1)S(1)} %collective-permute-done.22.refs_18_), channel_id=1, source_target_pairs={{0,2},{2,4},{4,6},{6,0},{8,10},{10,12},{12,14},{14,8},{16,18},{18,... | collective-permute-start | bytes 1228808 | tf_op jit(solution)/shard_map/ppermute | solution.py:42
  67.4 16.7 %collective-permute-start.12 = (bf16[2,400,256]{2,1,0:T(8,128)(2,1)}, bf16[2,400,256]{2,1,0:T(8,128)(2,1)}, u32[]{:S(2)}, u32[]{:S(2)}) collective-permute-start(bf16[2,400,256]{2,1,0:T(8,128)(2,1)} %collective-permute-done.10.refs_2_), channel_id=1, source_target_pairs={{0,8},{2,10},{4,12},{6,14},{8,16},{10,18},{12,20},{14,22},{16,24},... | collective-permute-start | bytes 1228808 | tf_op jit(solution)/shard_map/ppermute | solution.py:42
  68.1 15.9 %collective-permute-start.14 = (bf16[2,400,256]{2,1,0:T(8,128)(2,1)}, bf16[2,400,256]{2,1,0:T(8,128)(2,1)}, u32[]{:S(2)}, u32[]{:S(2)}) collective-permute-start(bf16[2,400,256]{2,1,0:T(8,128)(2,1)} %collective-permute-done.13.refs_7_), channel_id=1, source_target_pairs={{0,24},{2,26},{4,28},{6,30},{8,0},{10,2},{12,4},{14,6},{16,8},{18,... | collective-permute-start | bytes 1228808 | tf_op jit(solution)/shard_map/ppermute | solution.py:42
  97.0 21.1 %collective-permute-start.34 = (bf16[16,128,256]{2,1,0:T(8,128)(2,1)S(1)}, bf16[16,128,256]{2,1,0:T(8,128)(2,1)S(1)}, u32[]{:S(2)}, u32[]{:S(2)}) collective-permute-start(bf16[16,128,256]{2,1,0:T(8,128)(2,1)S(1)} %get-tuple-element.30), channel_id=1, source_target_pairs={{0,32},{2,34},{4,36},{6,38},{8,40},{10,42},{12,44},{14,46},{16,48}... | collective-permute-start | bytes 3145736 | tf_op jit(solution)/shard_map/ppermute | solution.py:42
  97.2 45.1 %collective-permute-start.35 = (bf16[16,128,256]{2,1,0:T(8,128)(2,1)S(1)}, bf16[16,128,256]{2,1,0:T(8,128)(2,1)S(1)}, u32[]{:S(2)}, u32[]{:S(2)}) collective-permute-start(bf16[16,128,256]{2,1,0:T(8,128)(2,1)S(1)} %get-tuple-element.31), channel_id=1, source_target_pairs={{0,64},{2,66},{4,68},{6,70},{8,72},{10,74},{12,76},{14,78},{16,80}... | collective-permute-start | bytes 3145736 | tf_op jit(solution)/shard_map/ppermute | solution.py:42
  100.0 45.3 %collective-permute-start.36 = (bf16[16,128,256]{2,1,0:T(8,128)(2,1)S(1)}, bf16[16,128,256]{2,1,0:T(8,128)(2,1)S(1)}, u32[]{:S(2)}, u32[]{:S(2)}) collective-permute-start(bf16[16,128,256]{2,1,0:T(8,128)(2,1)S(1)} %get-tuple-element.32), channel_id=1, source_target_pairs={{0,96},{2,98},{4,100},{6,102},{8,104},{10,106},{12,108},{14,110},{... | collective-permute-start | bytes 3145736 | tf_op jit(solution)/shard_map/ppermute | solution.py:42
  100.0 49.6 %collective-permute-start.31 = (bf16[16,128,256]{2,1,0:T(8,128)(2,1)S(1)}, bf16[16,128,256]{2,1,0:T(8,128)(2,1)S(1)}, u32[]{:S(2)}, u32[]{:S(2)}) collective-permute-start(bf16[16,128,256]{2,1,0:T(8,128)(2,1)S(1)} %get-tuple-element.26), channel_id=1, source_target_pairs={{0,8},{2,10},{4,12},{6,14},{8,16},{10,18},{12,20},{14,22},{16,24},... | collective-permute-start | bytes 3145736 | tf_op jit(solution)/shard_map/ppermute | solution.py:42
  100.0 69.5 %collective-permute-start.32 = (bf16[16,128,256]{2,1,0:T(8,128)(2,1)}, bf16[16,128,256]{2,1,0:T(8,128)(2,1)}, u32[]{:S(2)}, u32[]{:S(2)}) collective-permute-start(bf16[16,128,256]{2,1,0:T(8,128)(2,1)} %get-tuple-element.27), channel_id=1, source_target_pairs={{0,16},{2,18},{4,20},{6,22},{8,24},{10,26},{12,28},{14,30},{16,0},... | collective-permute-start | bytes 3145736 | tf_op jit(solution)/shard_map/ppermute | solution.py:42
  118.2 55.1 %collective-permute-start.33 = (bf16[16,128,256]{2,1,0:T(8,128)(2,1)}, bf16[16,128,256]{2,1,0:T(8,128)(2,1)}, u32[]{:S(2)}, u32[]{:S(2)}) collective-permute-start(bf16[16,128,256]{2,1,0:T(8,128)(2,1)} %get-tuple-element.28), channel_id=1, source_target_pairs={{0,24},{2,26},{4,28},{6,30},{8,0},{10,2},{12,4},{14,6},{16,8},{18,... | collective-permute-start | bytes 3145736 | tf_op jit(solution)/shard_map/ppermute | solution.py:42
  142.4 35.3 %collective-permute-start.28 = (bf16[16,128,256]{2,1,0:T(8,128)(2,1)}, bf16[16,128,256]{2,1,0:T(8,128)(2,1)}, u32[]{:S(2)}, u32[]{:S(2)}) collective-permute-start(bf16[16,128,256]{2,1,0:T(8,128)(2,1)} %get-tuple-element.22), channel_id=1, source_target_pairs={{0,2},{2,4},{4,6},{6,0},{8,10},{10,12},{12,14},{14,8},{16,18},{18,... | collective-permute-start | bytes 3145736 | tf_op jit(solution)/shard_map/ppermute | solution.py:42
  145.3 44.5 %collective-permute-start.29 = (bf16[16,128,256]{2,1,0:T(8,128)(2,1)}, bf16[16,128,256]{2,1,0:T(8,128)(2,1)}, u32[]{:S(2)}, u32[]{:S(2)}) collective-permute-start(bf16[16,128,256]{2,1,0:T(8,128)(2,1)} %get-tuple-element.23), channel_id=1, source_target_pairs={{0,4},{2,6},{4,0},{6,2},{8,12},{10,14},{12,8},{14,10},{16,20},{18,... | collective-permute-start | bytes 3145736 | tf_op jit(solution)/shard_map/ppermute | solution.py:42
  150.7 43.9 %collective-permute-start.30 = (bf16[16,128,256]{2,1,0:T(8,128)(2,1)}, bf16[16,128,256]{2,1,0:T(8,128)(2,1)}, u32[]{:S(2)}, u32[]{:S(2)}) collective-permute-start(bf16[16,128,256]{2,1,0:T(8,128)(2,1)} %get-tuple-element.24), channel_id=1, source_target_pairs={{0,6},{2,0},{4,2},{6,4},{8,14},{10,8},{12,10},{14,12},{16,22},{18,... | collective-permute-start | bytes 3145736 | tf_op jit(solution)/shard_map/ppermute | solution.py:42
  169.5 35.0 %collective-permute-start.39 = (bf16[24,128,256]{2,1,0:T(8,128)(2,1)}, bf16[24,128,256]{2,1,0:T(8,128)(2,1)}, u32[]{:S(2)}, u32[]{:S(2)}) collective-permute-start(bf16[24,128,256]{2,1,0:T(8,128)(2,1)} %hand.5), channel_id=1, source_target_pairs={{0,1},{1,0},{2,3},{3,2},{4,5},{5,4},{6,7},{7,6},{8,9},{9,8},{10,11... | collective-permute-start | bytes 4718600 | tf_op jit(solution)/shard_map/ppermute | solution.py:46
  177.6 26.9 %collective-permute-start.38 = (bf16[24,128,256]{2,1,0:T(8,128)(2,1)}, bf16[24,128,256]{2,1,0:T(8,128)(2,1)}, u32[]{:S(2)}, u32[]{:S(2)}) collective-permute-start(bf16[24,128,256]{2,1,0:T(8,128)(2,1)} %hand.4), channel_id=1, source_target_pairs={{0,1},{1,0},{2,3},{3,2},{4,5},{5,4},{6,7},{7,6},{8,9},{9,8},{10,11... | collective-permute-start | bytes 4718600 | tf_op jit(solution)/shard_map/ppermute | solution.py:46
  (52 other events, 307.1 us)
